TPU v7x, 32 devices: a whole 2x2x4 slice. The times are simulated.
32 devices in a mesh: gx: 4 (over y, x), gy: 4 (over z), gz: 2 (over core).
Axes of the slice: x: 2, y: 2, z: 4, core: 2. Of those that a mesh axis runs over, the one named last changes fastest.
Arguments:
- src_fields: float32 [1024, 1080], P(('gx', 'gy', 'gz')), may hold values from -6 to 6
- owner_peer: int32 [1024, 8, 1], P(('gx', 'gy', 'gz')), may hold values from 0 to 15; in each aligned block of 256 rows (0 to 255, 256 to 511, ..., all dimensions but the last counted through in order) at most 18 rows name the same one
- src_local: int32 [1024, 8], P(('gx', 'gy', 'gz')), may hold values from 0 to 31
- jac: float32 [1024, 4096], P(('gx', 'gy', 'gz')), may hold values from 0.25 to 4
Outputs:
- remapped: float32 [1024, 1080], P(('gx', 'gy', 'gz'))
- nodal_accel: float32 [1024, 648], P(('gx', 'gy', 'gz'))
Inputs may be any that keep to these rules, and one draw needn't show every extreme that they name: owner_peer[r, k, 0] is the index, within the 16 devices that share target r's gz index (gx-major), of the device owning intersection k's source element; among the 256 intersections of one device's targets at most 18 name the same device, and some device reaches 18 in every draw.
All inputs are finite; a program needn't handle non-finite values.
Results may differ from a plain program's by a relative error of at most 0.0002.
Values sent between devices are 32-bit elements; how exact they have to be, the bound alone decides.
No kernel may reach another device: no remote copies, remote signals or barrier semaphores. Data moves between devices by JAX's collectives and lax.ppermute only.
A program may use at most 64 MiB of HBM per device.

v0:
```python
import math

import jax
import jax.numpy as jnp
import numpy as np
from jax import lax
from jax.experimental import pallas as pl
from jax.experimental.pallas import tpu as pltpu
from jax.sharding import PartitionSpec as P

EX = 4
EY = 4
EZ = 2
FIELDS = 5
NB = 216
QP = 512
OVL = 8
PAD = 256
CUT = 512
BF = jnp.bfloat16
F32 = jnp.float32


def three_way(table):
    parts = []
    rest = np.asarray(table, np.float32)
    for _ in range(3):
        part = rest.astype(jnp.bfloat16)
        parts.append(part)
        rest = rest - part.astype(np.float32)
    return parts


def lower_integral(first, second):
    if first < 0 or first > 4:
        return 0.0
    return math.comb(4, first) * math.comb(5, second) / (10.0 * math.comb(9, first + second))


def force_table():
    mass_one = np.zeros((6, 6))
    grad_one = np.zeros((6, 6))
    for left in range(6):
        for right in range(6):
            mass_one[left, right] = (
                math.comb(5, left) * math.comb(5, right) / (11.0 * math.comb(10, left + right))
            )
            grad_one[left, right] = 5.0 * (
                lower_integral(left - 1, right) - lower_integral(left, right)
            )
    grad_x = np.kron(grad_one, np.kron(mass_one, mass_one))
    grad_y = np.kron(mass_one, np.kron(grad_one, mass_one))
    grad_z = np.kron(mass_one, np.kron(mass_one, grad_one))
    joined = np.zeros((NB, 3 * PAD), np.float32)
    for c, grad in enumerate((grad_x, grad_y, grad_z)):
        joined[:, c * PAD : c * PAD + NB] = grad.T * 8.0
    high, low, _ = three_way(joined)
    return jnp.asarray(high, BF), jnp.asarray(low, BF)


def split(value):
    high = value.astype(BF)
    return high, (value - high.astype(F32)).astype(BF)


def dot(a, b, dims=((1,), (0,))):
    return lax.dot_general(a, b, (dims, ((), ())), preferred_element_type=F32)


def dot3(a, b, dims=((1,), (0,))):
    return dot(a[0], b[0], dims) + (dot(a[0], b[1], dims) + dot(a[1], b[0], dims))


NT = ((1,), (1,))


def bern_rows(stride, bit):
    row = lax.broadcasted_iota(jnp.int32, (8, QP), 0)
    point = lax.broadcasted_iota(jnp.int32, (8, QP), 1) // stride % 8
    u = point.astype(F32) * (1.0 / 16.0) + (1.0 / 32.0 + 0.5 - 0.5 * bit)
    value = jnp.zeros((8, QP), F32)
    for i in range(6):
        value = jnp.where(row == i, float(math.comb(5, i)), value)
    for n in range(5):
        value = value * jnp.where(row > n, u, 1.0 - u)
    return value


def prep_kernel(high_ref, low_ref):
    coef = lax.broadcasted_iota(jnp.int32, (NB, 24), 0)
    col = lax.broadcasted_iota(jnp.int32, (NB, 24), 1)
    factors = []
    for stride, spacing in ((36, 64), (6, 8), (1, 1)):
        pick = jnp.where(coef // stride % 6 == col % 8, 1.0, 0.0).astype(BF)
        pair = []
        for bit in range(2):
            rows = bern_rows(spacing, bit)
            high = rows.astype(BF)
            middle, low = split(rows - high.astype(F32))
            parts = [part.astype(F32) for part in (high, middle, low)]
            pair.append(dot(pick, jnp.concatenate(parts, 0).astype(BF)))
        factors.append(pair)
    for k in range(OVL):
        table = factors[0][k >> 2 & 1] * factors[1][k >> 1 & 1] * factors[2][k & 1]
        high, low = split(table)
        high_ref[k] = high
        low_ref[k] = low


def hits(index_ref, wanted, spans):
    elems = index_ref.shape[0]
    out = []
    for k in spans:
        column = jnp.broadcast_to(index_ref[:, k : k + 1], (elems, wanted.shape[1]))
        out.append(jnp.where(column == wanted, 1.0, 0.0))
    return out


def packing(mask, capacity, elems, owners):
    width = owners * elems
    row = lax.broadcasted_iota(jnp.int32, (width, width), 0)
    col = lax.broadcasted_iota(jnp.int32, (width, width), 1)
    earlier = jnp.where((row // elems == col // elems) & (row < col), 1.0, 0.0).astype(BF)
    rank = dot(jnp.broadcast_to(mask, (8, width)).astype(BF), earlier)[:1]
    slots = owners * capacity
    spot = lax.broadcasted_iota(jnp.int32, (slots, width), 0)
    lane = lax.broadcasted_iota(jnp.int32, (slots, width), 1)
    wanted = (lane // elems * capacity).astype(F32) + rank
    hit = (spot.astype(F32) == wanted) & (jnp.broadcast_to(mask, (slots, width)) > 0.5)
    return jnp.where(hit, 1.0, 0.0).astype(BF)


def front_kernel(owners, capacity, rows, owner, local, near_ref, far_ref, ids_ref, index_ref, *refs):
    *mask_refs, owner_ref, local_ref, sems = refs
    pairs = (
        (owner, owner_ref),
        (local, local_ref),
        (rows.at[:, :CUT], near_ref),
        (rows.at[:, CUT:], far_ref),
    )
    copies = [
        pltpu.make_async_copy(source, target, sems.at[n]) for n, (source, target) in enumerate(pairs)
    ]
    for copy in copies:
        copy.start()
    elems = owner.shape[1]
    copies[0].wait()
    copies[1].wait()
    owner = owner_ref[...]
    outer = slot_of(owner // owners, lax.axis_index("gx"), lax.axis_size("gx"))
    inner = slot_of(owner % owners, lax.axis_index("gy"), owners)
    index_ref[...] = ((outer * owners + inner) * elems + local_ref[...]).T
    width = owners * elems
    lane = lax.broadcasted_iota(jnp.int32, (elems, (1 + len(mask_refs)) * width), 1)
    named = sum(hits(index_ref, lane, range(OVL)))
    named = jnp.sum(named, 0, keepdims=True)
    mask = jnp.where(named > 0.5, 1.0, 0.0)
    ids_ref[:, :width] = lane[:1, :width]
    local = lax.broadcasted_iota(jnp.int32, (8, width), 1) + 1
    slots = owners * capacity
    for s, mask_ref in enumerate(mask_refs):
        part = mask[:, (s + 1) * width : (s + 2) * width]
        mask_ref[...] = jnp.broadcast_to(part, mask_ref.shape)
        order = packing(part, capacity, elems, owners)
        ids = dot(local.astype(F32).astype(BF), order, NT)[:1].astype(jnp.int32)
        ids = jnp.where(ids > 0, ids + ((s + 1) * width - 1), -1)
        ids_ref[:, width + s * slots : width + (s + 1) * slots] = ids
    copies[2].wait()
    copies[3].wait()


def lanes_of(pieces, width, part):
    span = slice(0, CUT) if part == 0 else slice(CUT, width)
    return [ref[:, span] if ref.shape[1] == width else ref[...] for ref in pieces]


def pack_kernel(owners, capacity, count, width, part, *refs):
    masks = refs[:count]
    column = refs[count : count + owners]
    outs = refs[count + owners :]
    elems = column[0].shape[0]
    order = jnp.concatenate(
        [packing(mask[:1], capacity, elems, owners) for mask in masks], 0
    )
    rows = jnp.concatenate(lanes_of(column, width, part), 0)
    high = rows.astype(BF)
    rest = rows - high.astype(F32)
    middle, low = split(rest)
    packed = (dot(order, high) + dot(order, middle)) + dot(order, low)
    slots = owners * capacity
    for s in range(count):
        outs[s][...] = packed[s * slots : (s + 1) * slots]


def pick(hot, rows, outs):
    high, low = split(rows)
    outs[0][...] = dot(hot, high)
    outs[1][...] = dot(hot, low)


def mirror():
    row = lax.broadcasted_iota(jnp.int32, (NB, NB), 0)
    col = lax.broadcasted_iota(jnp.int32, (NB, NB), 1)
    return jnp.where(row + col // 36 * 72 == col + 180, 1.0, 0.0).astype(BF)


def project(offset, picked, jac_ref, high_ref, low_ref, extra):
    elems = jac_ref.shape[0]
    count = (picked[0].shape[1] - offset) // NB
    half = OVL // 2
    flip = mirror()

    def apply(pair, table, dims=((1,), (0,))):
        size = pair[0].shape[0]
        both = dot(jnp.concatenate(pair, 0), high_ref[table], dims)
        return both[:size] + (both[size:] + dot(pair[0], low_ref[table], dims))

    def fields_of(ref, first, last):
        at = slice(first * elems, last * elems)
        return [
            ref[at, offset + f * NB : offset + (f + 1) * NB].astype(BF) for f in range(count)
        ]

    turned = jnp.concatenate([x for ref in picked for x in fields_of(ref, 0, half)], 0)
    turned = dot(turned, flip).astype(BF)
    total = None
    for n in range(half):
        source = []
        for m, ref in enumerate(picked):
            rows = fields_of(ref, half + n, half + n + 1)
            for f in range(count):
                base = ((m * count + f) * half + n) * elems
                rows.append(turned[base : base + elems])
            source.append(jnp.concatenate(rows, 0))
        values = apply(source, half + n)
        weights = jac_ref[:, (half + n) * QP : (half + n + 1) * QP]
        other = [
            pltpu.roll(jac_ref[:, base : base + 128], 64, 1)
            for base in range((n + 1) * QP - 128, n * QP - 128, -128)
        ]
        other = jnp.concatenate(other, 1)
        scaled = values * jnp.concatenate([weights] * count + [other] * count, 0)
        if extra:
            scaled = jnp.concatenate([scaled, weights, other], 0)
        part = apply(split(scaled), half - 1 - n, NT)
        total = part if total is None else total + part
    own = [total[: count * elems]]
    turned = [total[count * elems : 2 * count * elems]]
    if extra:
        own.append(total[2 * count * elems : (2 * count + 1) * elems])
        turned.append(total[(2 * count + 1) * elems :])
    own, turned = jnp.concatenate(own, 0), jnp.concatenate(turned, 0)
    high = turned.astype(BF)
    middle, low = split(turned - high.astype(F32))
    size = turned.shape[0]
    back = dot(jnp.concatenate([high, middle, low], 0), flip)
    return own + ((back[:size] + back[size : 2 * size]) + back[2 * size :])


def send_faces(even, first, last, send_ref, back_ref):
    send_ref[...] = jnp.where(even, last, first)
    back_ref[...] = jnp.where(even, first, last)


def take_faces(axis, got, back):
    me, count = lax.axis_index(axis), lax.axis_size(axis)
    even = me % 2 == 0
    before = jnp.where(even, back, got)
    after = jnp.where(even, got, back)
    return jnp.where(me > 0, before, 0.0), jnp.where(me < count - 1, after, 0.0)


def lead_kernel(owners, count, ids_ref, index_ref, jac_ref, high_ref, low_ref, fhigh_ref, flow_ref, *refs):
    column = refs[:owners]
    packed = refs[owners : owners + count]
    refs = refs[owners + count :]
    fields_ref, lumped_ref, parts_ref, send_ref, back_ref, *picked = refs
    elems = jac_ref.shape[0]
    hot = jnp.concatenate(hits(index_ref, ids_ref[...], range(OVL)), 0).astype(BF)
    rows = lanes_of((*column, *packed), NB * FIELDS, 0)
    pick(hot, jnp.concatenate(rows, 0), picked)
    total = project(0, picked, jac_ref, high_ref, low_ref, True)
    lumped = total[2 * elems :]
    lumped_ref[...] = lumped
    fields = [total[f * elems : (f + 1) * elems] / lumped for f in range(2)]
    for f in range(2):
        fields_ref[:, f * NB : (f + 1) * NB] = fields[f]
    pressure = fields[0] * fields[1]
    force = dot3(split(pressure), (fhigh_ref[...], flow_ref[...]))
    mass = jnp.concatenate([lumped * (1.0 / 4096.0), jnp.zeros((elems, PAD - NB), F32)], 1)
    parts = jnp.concatenate([force, mass], 1)
    parts_ref[...] = parts
    width = EY * EZ
    even = lax.axis_index("gx") % 2 == 0
    send_faces(even, parts[:width], parts[-width:], send_ref, back_ref)


def tail_kernel(count, ids_ref, index_ref, jac_ref, high_ref, low_ref, lumped_ref, lead_ref, *refs):
    near, far = refs[:count], refs[count : 2 * count]
    out_ref, *picked = refs[2 * count :]
    elems = jac_ref.shape[0]
    start = CUT - 128
    hot = jnp.concatenate(hits(index_ref, ids_ref[...], range(OVL)), 0).astype(BF)
    rows = []
    for a, b in zip(near, far):
        if a.shape[1] == NB * FIELDS:
            rows.append(a[:, start:])
        else:
            rows.append(jnp.concatenate([a[:, start:], b[...]], 1))
    pick(hot, jnp.concatenate(rows, 0), picked)
    total = project(2 * NB - start, picked, jac_ref, high_ref, low_ref, False)
    lumped = lumped_ref[...]
    out_ref[:, : 2 * NB] = lead_ref[...]
    for f in range(3):
        out_ref[:, (f + 2) * NB : (f + 3) * NB] = total[f * elems : (f + 1) * elems] / lumped


def face_add(parts, before, after, shift, stride):
    comps = []
    elems = parts.shape[0]
    lane = lax.broadcasted_iota(jnp.int32, (elems, PAD), 1)
    spot = lane // stride % 6
    inside = lane < NB
    for c in range(4):
        at = slice(c * PAD, (c + 1) * PAD)
        low = pltpu.roll(before[:, at], PAD - shift, 1)
        high = pltpu.roll(after[:, at], shift, 1)
        low = jnp.where((spot == 0) & inside, low, 0.0)
        high = jnp.where((spot == 5) & inside, high, 0.0)
        comps.append(parts[:, at] + (low + high))
    return jnp.concatenate(comps, 1)


def x_kernel(parts_ref, got_ref, turn_ref, out_ref, send_ref, back_ref):
    parts = parts_ref[...]
    width = EY * EZ
    before, after = take_faces("gx", got_ref[...], turn_ref[...])
    before = jnp.concatenate([before, parts[:-width]], 0)
    after = jnp.concatenate([parts[width:], after], 0)
    parts = face_add(parts, before, after, 180, 36)
    out_ref[...] = parts
    first = [parts[x * width : x * width + EZ] for x in range(EX)]
    last = [parts[(x + 1) * width - EZ : (x + 1) * width] for x in range(EX)]
    first, last = jnp.concatenate(first, 0), jnp.concatenate(last, 0)
    send_faces(lax.axis_index("gy") % 2 == 0, first, last, send_ref, back_ref)


def y_kernel(parts_ref, got_ref, turn_ref, out_ref):
    parts = parts_ref[...]
    width = EY * EZ
    far_before, far_after = take_faces("gy", got_ref[...], turn_ref[...])
    before = []
    after = []
    for x in range(EX):
        base = x * width
        near = slice(x * EZ, (x + 1) * EZ)
        before += [far_before[near], parts[base : base + width - EZ]]
        after += [parts[base + EZ : base + width], far_after[near]]
    before = jnp.concatenate(before, 0)
    after = jnp.concatenate(after, 0)
    out_ref[...] = face_add(parts, before, after, 30, 6)


def z_kernel(parts_ref, before_ref, after_ref, out_ref):
    parts = parts_ref[...]
    elems = parts.shape[0]
    odd = lax.broadcasted_iota(jnp.int32, parts.shape, 0) % EZ == EZ - 1
    has_before = lax.axis_index("gz") > 0
    has_after = lax.axis_index("gz") < lax.axis_size("gz") - 1
    far_before = jnp.where(has_before, pltpu.roll(before_ref[...], elems - 1, 0), 0.0)
    far_after = jnp.where(has_after, pltpu.roll(after_ref[...], 1, 0), 0.0)
    before = jnp.where(odd, pltpu.roll(parts, 1, 0), far_before)
    after = jnp.where(odd, far_after, pltpu.roll(parts, elems - 1, 0))
    parts = face_add(parts, before, after, 5, 1)
    mass = parts[:, 3 * PAD :]
    for c in range(3):
        accel = parts[:, c * PAD : c * PAD + NB] / mass[:, :NB]
        out_ref[:, c * NB : (c + 1) * NB] = accel


VM = pl.BlockSpec(memory_space=pltpu.VMEM)
HB = pl.BlockSpec(memory_space=pltpu.HBM)


def call(kernel, shapes, specs, scratch=(), cost=None):
    return pl.pallas_call(
        kernel,
        out_shape=shapes,
        in_specs=specs,
        out_specs=jax.tree.map(lambda _: VM, shapes),
        scratch_shapes=scratch,
        cost_estimate=cost,
        compiler_params=pltpu.CompilerParams(vmem_limit_bytes=16 << 20),
    )


def partner(count, step):
    if count & (count - 1) == 0:
        return [(i, i ^ step) for i in range(count)]
    return [(i, (i + step) % count) for i in range(count)]


def slot_of(owner, me, count):
    if count & (count - 1) == 0:
        return owner ^ me
    return (me - owner) % count


def shape(dims, dtype=F32):
    return jax.ShapeDtypeStruct(dims, dtype)


def swap_faces(piece, back, axis, count):
    near = [(i, i ^ 1) for i in range(count)]
    across = [(i, (i + 1) % count if i % 2 else (i - 1) % count) for i in range(count)]
    return lax.ppermute(piece, axis, near), lax.ppermute(back, axis, across)


def per_device(src_fields, owner_peer, src_local, jac):
    n_x = lax.axis_size("gx")
    n_y = lax.axis_size("gy")
    n_z = lax.axis_size("gz")
    elems = src_fields.shape[0]
    width = src_fields.shape[1]
    capacity = max(2, 9 * elems // (n_x * n_y))
    slots = n_y * capacity
    nearest = lax.ppermute(src_fields, "gy", partner(n_y, 1))
    total = n_y * elems + (n_x - 1) * slots
    turned = (OVL, elems)
    own_a, own_b, ids, index, *masks = call(
        lambda *refs: front_kernel(n_y, capacity, *refs),
        (
            shape((elems, CUT)),
            shape((elems, width - CUT)),
            shape((1, total), jnp.int32),
            shape(src_local.shape, jnp.int32),
        )
        + (shape((8, n_y * elems)),) * (n_x - 1),
        [HB] * 3,
        [pltpu.VMEM(turned, jnp.int32)] * 2 + [pltpu.SemaphoreType.DMA((4,))],
    )(*[
        pltpu.with_memory_space_constraint(operand, pltpu.HBM)
        for operand in (src_fields, owner_peer[:, :, 0].T, src_local.T)
    ])
    columns = [
        [piece, nearest] + [lax.ppermute(piece, "gy", partner(n_y, step)) for step in range(2, n_y)]
        for piece in (own_a, own_b)
    ]
    fhigh, flow = force_table()
    table = shape((OVL, NB, QP), BF)
    heavy = pl.CostEstimate(flops=2_000_000_000, bytes_accessed=8_000_000, transcendentals=0)
    high, low = call(prep_kernel, (table, table), [], cost=heavy)()
    asked = [lax.ppermute(mask, "gx", partner(n_x, step + 1)) for step, mask in enumerate(masks)]
    gathered = []
    for part in range(2):
        span = (CUT, width - CUT)[part]
        packed = call(
            lambda *refs: pack_kernel(n_y, capacity, n_x - 1, width, part, *refs),
            (shape((slots, span)),) * (n_x - 1),
            [VM] * (n_x - 1 + n_y),
        )(*asked, *columns[part])
        arrived = [
            lax.ppermute(piece, "gx", partner(n_x, step + 1))
            for step, piece in enumerate(packed)
        ]
        gathered.append(columns[part] + arrived)
    near, far = gathered
    face = shape((EY * EZ, 4 * PAD))
    whole = shape((elems, 4 * PAD))
    lead, lumped, parts, piece, back = call(
        lambda *refs: lead_kernel(n_y, n_x - 1, *refs),
        (shape((elems, 2 * NB)), shape((elems, NB)), whole, face, face),
        [VM] * (7 + len(near)),
        [pltpu.VMEM((OVL * elems, CUT), F32)] * 2,
    )(ids, index, jac, high, low, fhigh, flow, *near)
    got, turn = swap_faces(piece, back, "gx", n_x)
    face = shape((EX * EZ, 4 * PAD))
    parts, piece, back = call(x_kernel, (whole, face, face), [VM] * 3)(parts, got, turn)
    got, turn = swap_faces(piece, back, "gy", n_y)
    scratch = pltpu.VMEM((OVL * elems, width - CUT + 128), F32)
    fields = call(
        lambda *refs: tail_kernel(len(near), *refs),
        shape((elems, width)),
        [VM] * (7 + 2 * len(near)),
        [scratch] * 2,
        heavy,
    )(ids, index, jac, high, low, lumped, lead, *near, *far)
    got, turn, fields = lax.optimization_barrier((got, turn, fields))
    parts = call(y_kernel, whole, [VM] * 3)(parts, got, turn)
    if n_z == 2:
        before = after = lax.ppermute(parts, "gz", [(0, 1), (1, 0)])
    else:
        before = lax.ppermute(parts, "gz", [(i, i + 1) for i in range(n_z - 1)])
        after = lax.ppermute(parts, "gz", [(i + 1, i) for i in range(n_z - 1)])
    accel = call(z_kernel, shape((elems, 3 * NB)), [VM] * 3)(parts, before, after)
    return fields, accel


def solution(mesh):
    rows = ("gx", "gy", "gz")
    placed = (P(rows, None), P(rows, None, None), P(rows, None), P(rows, None))

    return jax.shard_map(
        per_device,
        mesh=mesh,
        in_specs=placed,
        out_specs=(P(rows, None), P(rows, None)),
        check_vma=False,
    )
```

profile of v0, /device:TPU:0, one launch (start us, length us, event | category | flops | bytes accessed | tf_op | source)
XLA Modules:
  0.0 50.1 jit_solution(14266137024834414860)
XLA Ops:
  0.6 3.1 %collective-permute-start = (f32[32,1080]{1,0:T(8,128)}, f32[32,1080]{1,0:T(8,128)S(1)}, u32[]{:S(2)}, u32[]{:S(2)}) collective-permute-start(f32[32,1080]{1,0:T(8,128)} %refs_0_.1), channel_id=1, source_target_pairs={{0,2},{2,0},{4,6},{6,4},{1,3},{3,1},{5,7},{7,5},{8,10},{10,8},{12,... | collective-permute-start | bytes 414728 | tf_op jit(solution)/shard_map/ppermute | solution.py:427
  3.7 1.3 %shard_map.77 = (f32[32,512]{1,0:T(8,128)S(1)}, f32[32,568]{1,0:T(8,128)S(1)}, s32[1,344]{1,0:T(1,128)S(1)}, s32[32,8]{1,0:T(8,128)S(1)}, f32[8,128]{1,0:T(8,128...) custom-call(f32[32,1080]{1,0:T(8,128)} %refs_0_.1, s32[8,32]{1,0:T(8,128)} %bitcast.4, s32[8,32]{1,0:T(8,128)} %bitcast.5), custom_call_target="tpu_custom_call" | custom-call | tf_op jit(solution)/shard_map/pallas_call | solution.py:430
  5.1 2.5 %collective-permute-start.2 = (f32[32,512]{1,0:T(8,128)S(1)}, f32[32,512]{1,0:T(8,128)S(1)}, u32[]{:S(2)}, u32[]{:S(2)}) collective-permute-start(f32[32,512]{1,0:T(8,128)S(1)} %get-tuple-element.32.refs_3_.refs_7_), channel_id=1, source_target_pairs={{0,6},{2,4},{4,2},{6,0},{1,7},{3,5},{5,3},{7,1},{8,14},{10,12},{12... | collective-permute-start | bytes 196616 | tf_op jit(solution)/shard_map/ppermute | solution.py:446
  7.6 0.2 collective-permute-start.1
  7.8 1.5 %collective-permute-start.3 = (f32[8,128]{1,0:T(8,128)S(1)}, f32[8,128]{1,0:T(8,128)S(1)}, u32[]{:S(2)}, u32[]{:S(2)}) collective-permute-start(f32[8,128]{1,0:T(8,128)S(1)} %get-tuple-element.33), channel_id=1, source_target_pairs={{0,8},{8,0},{16,24},{24,16},{1,9},{9,1},{17,25},{25,17},{2,10},{10... | collective-permute-start | bytes 12296 | tf_op jit(solution)/shard_map/ppermute | solution.py:453
  9.3 1.5 %collective-permute-start.4 = (f32[8,128]{1,0:T(8,128)S(1)}, f32[8,128]{1,0:T(8,128)S(1)}, u32[]{:S(2)}, u32[]{:S(2)}) collective-permute-start(f32[8,128]{1,0:T(8,128)S(1)} %get-tuple-element.34), channel_id=1, source_target_pairs={{0,16},{8,24},{16,0},{24,8},{1,17},{9,25},{17,1},{25,9},{2,18},{10... | collective-permute-start | bytes 12296 | tf_op jit(solution)/shard_map/ppermute | solution.py:453
  10.8 0.6 %collective-permute-done.3.refs_0_ = f32[8,128]{1,0:T(8,128)S(1)} collective-permute-done((f32[8,128]{1,0:T(8,128)S(1)}, f32[8,128]{1,0:T(8,128)S(1)}, u32[]{:S(2)}, u32[]{:S(2)}) %collective-permute-start.3) | collective-permute-done | bytes 4128 | tf_op jit(solution)/shard_map/ppermute | solution.py:453
  11.4 2.4 %collective-permute-start.5 = (f32[8,128]{1,0:T(8,128)S(1)}, f32[8,128]{1,0:T(8,128)S(1)}, u32[]{:S(2)}, u32[]{:S(2)}) collective-permute-start(f32[8,128]{1,0:T(8,128)S(1)} %get-tuple-element.35), channel_id=1, source_target_pairs={{0,24},{8,16},{16,8},{24,0},{1,25},{9,17},{17,9},{25,1},{2,26},{10... | collective-permute-start | bytes 12296 | tf_op jit(solution)/shard_map/ppermute | solution.py:453
  13.9 2.1 %collective-permute-done.5.refs_2_ = f32[8,128]{1,0:T(8,128)S(1)} collective-permute-done((f32[8,128]{1,0:T(8,128)S(1)}, f32[8,128]{1,0:T(8,128)S(1)}, u32[]{:S(2)}, u32[]{:S(2)}) %collective-permute-start.5) | collective-permute-done | bytes 4128 | tf_op jit(solution)/shard_map/ppermute | solution.py:453
  16.0 0.4 shard_map.79
  16.4 1.6 %collective-permute-start.6 = (f32[72,512]{1,0:T(8,128)S(1)}, f32[72,512]{1,0:T(8,128)S(1)}, u32[]{:S(2)}, u32[]{:S(2)}) collective-permute-start(f32[72,512]{1,0:T(8,128)S(1)} %get-tuple-element.36), channel_id=1, source_target_pairs={{0,8},{8,0},{16,24},{24,16},{1,9},{9,1},{17,25},{25,17},{2,10},{10... | collective-permute-start | bytes 442376 | tf_op jit(solution)/shard_map/ppermute | solution.py:463
  18.0 2.8 %collective-permute-start.14 = (f32[32,568]{1,0:T(8,128)S(1)}, f32[32,568]{1,0:T(8,128)S(1)}, u32[]{:S(2)}, u32[]{:S(2)}) collective-permute-start(f32[32,568]{1,0:T(8,128)S(1)} %get-tuple-element.46.refs_3_.refs_14_), channel_id=1, source_target_pairs={{0,6},{2,4},{4,2},{6,0},{1,7},{3,5},{5,3},{7,1},{8,14},{10,12},{12... | collective-permute-start | bytes 218120 | tf_op jit(solution)/shard_map/ppermute | solution.py:446
  20.8 0.3 collective-permute-start.13
  21.1 1.5 %collective-permute-start.7 = (f32[72,512]{1,0:T(8,128)S(1)}, f32[72,512]{1,0:T(8,128)S(1)}, u32[]{:S(2)}, u32[]{:S(2)}) collective-permute-start(f32[72,512]{1,0:T(8,128)S(1)} %get-tuple-element.37), channel_id=1, source_target_pairs={{0,16},{8,24},{16,0},{24,8},{1,17},{9,25},{17,1},{25,9},{2,18},{10... | collective-permute-start | bytes 442376 | tf_op jit(solution)/shard_map/ppermute | solution.py:463
  22.7 0.5 collective-permute-start.8
  23.1 1.2 %collective-permute-done.14.refs_6_.refs_17_ = f32[32,568]{1,0:T(8,128)S(1)} collective-permute-done((f32[32,568]{1,0:T(8,128)S(1)}, f32[32,568]{1,0:T(8,128)S(1)}, u32[]{:S(2)}, u32[]{:S(2)}) %collective-permute-start.14) | collective-permute-done | bytes 72736 | tf_op jit(solution)/shard_map/ppermute | solution.py:446
  24.3 2.6 %collective-permute-done.13.refs_5_.refs_16_ = f32[32,568]{1,0:T(8,128)S(1)} collective-permute-done((f32[32,568]{1,0:T(8,128)S(1)}, f32[32,568]{1,0:T(8,128)S(1)}, u32[]{:S(2)}, u32[]{:S(2)}) %collective-permute-start.13) | collective-permute-done | bytes 72736 | tf_op jit(solution)/shard_map/ppermute | solution.py:446
  26.9 0.5 %shard_map.82 = (f32[72,568]{1,0:T(8,128)S(1)}, f32[72,568]{1,0:T(8,128)S(1)}, f32[72,568]{1,0:T(8,128)S(1)}) custom-call(f32[8,128]{1,0:T(8,128)S(1)} %collective-permute-done.3.refs_0_, f32[8,128]{1,0:T(8,128)S(1)} %collective-permute-done.4.refs_1_, f32[8,128]{1,0:T(8,128)S(1)} %collective-permute-done.5.refs_2_, ...), custom_call_target="tpu_custom_call" | custom-call | tf_op jit(solution)/shard_map/pallas_call | solution.py:457
  27.4 0.6 %collective-permute-start.15 = (f32[72,568]{1,0:T(8,128)S(1)}, f32[72,568]{1,0:T(8,128)S(1)}, u32[]{:S(2)}, u32[]{:S(2)}) collective-permute-start(f32[72,568]{1,0:T(8,128)S(1)} %get-tuple-element.47), channel_id=1, source_target_pairs={{0,8},{8,0},{16,24},{24,16},{1,9},{9,1},{17,25},{25,17},{2,10},{10... | collective-permute-start | bytes 490760 | tf_op jit(solution)/shard_map/ppermute | solution.py:463
  28.0 1.5 %collective-permute-start.16 = (f32[72,568]{1,0:T(8,128)S(1)}, f32[72,568]{1,0:T(8,128)S(1)}, u32[]{:S(2)}, u32[]{:S(2)}) collective-permute-start(f32[72,568]{1,0:T(8,128)S(1)} %get-tuple-element.48), channel_id=1, source_target_pairs={{0,16},{8,24},{16,0},{24,8},{1,17},{9,25},{17,1},{25,9},{2,18},{10... | collective-permute-start | bytes 490760 | tf_op jit(solution)/shard_map/ppermute | solution.py:463
  29.6 1.5 %collective-permute-start.17 = (f32[72,568]{1,0:T(8,128)S(1)}, f32[72,568]{1,0:T(8,128)S(1)}, u32[]{:S(2)}, u32[]{:S(2)}) collective-permute-start(f32[72,568]{1,0:T(8,128)S(1)} %get-tuple-element.49), channel_id=1, source_target_pairs={{0,24},{8,16},{16,8},{24,0},{1,25},{9,17},{17,9},{25,1},{2,26},{10... | collective-permute-start | bytes 490760 | tf_op jit(solution)/shard_map/ppermute | solution.py:463
  31.1 1.0 %shard_map.78 = (bf16[8,216,512]{2,1,0:T(8,128)(2,1)S(1)}, bf16[8,216,512]{2,1,0:T(8,128)(2,1)S(1)}) custom-call(), custom_call_target="tpu_custom_call" | custom-call | flops 2000000000 | bytes 8000000 | tf_op jit(solution)/shard_map/pallas_call | solution.py:452
  32.1 2.8 %shard_map.80 = (f32[32,432]{1,0:T(8,128)S(1)}, f32[32,216]{1,0:T(8,128)S(1)}, f32[32,1024]{1,0:T(8,128)S(1)}, f32[8,1024]{1,0:T(8,128)S(1)}, f32[8,1024]{1,0:T(8,128)S(1)}) custom-call(s32[1,344]{1,0:T(1,128)S(1)} %get-tuple-element.28.refs_0_, s32[32,8]{1,0:T(8,128)S(1)} %get-tuple-element.29.refs_1_, f32[32,4096]{1,0:T(8,128)S(1)} %copy-done, ...), custom_call_target="tpu_custom_call" | custom-call | tf_op jit(solution)/shard_map/pallas_call | solution.py:470
  34.9 0.6 %collective-permute-start.9 = (f32[8,1024]{1,0:T(8,128)S(1)}, f32[8,1024]{1,0:T(8,128)S(1)}, u32[]{:S(2)}, u32[]{:S(2)}) collective-permute-start(f32[8,1024]{1,0:T(8,128)S(1)} %get-tuple-element.40), channel_id=1, source_target_pairs={{0,8},{8,0},{16,24},{24,16},{1,9},{9,1},{17,25},{25,17},{2,10},{10... | collective-permute-start | bytes 98312 | tf_op jit(solution)/shard_map/ppermute | solution.py:416
  35.5 2.4 %collective-permute-start.10 = (f32[8,1024]{1,0:T(8,128)S(1)}, f32[8,1024]{1,0:T(8,128)S(1)}, u32[]{:S(2)}, u32[]{:S(2)}) collective-permute-start(f32[8,1024]{1,0:T(8,128)S(1)} %get-tuple-element.41), channel_id=1, source_target_pairs={{0,24},{8,16},{16,8},{24,0},{1,25},{9,17},{17,9},{25,1},{2,26},{10... | collective-permute-start | bytes 98312 | tf_op jit(solution)/shard_map/ppermute | solution.py:416
  38.0 0.9 %collective-permute-done.9.got_ref = f32[8,1024]{1,0:T(8,128)S(1)} collective-permute-done((f32[8,1024]{1,0:T(8,128)S(1)}, f32[8,1024]{1,0:T(8,128)S(1)}, u32[]{:S(2)}, u32[]{:S(2)}) %collective-permute-start.9) | collective-permute-done | bytes 32800 | tf_op jit(solution)/shard_map/ppermute | solution.py:416
  38.9 1.4 %collective-permute-done.10.turn_ref = f32[8,1024]{1,0:T(8,128)S(1)} collective-permute-done((f32[8,1024]{1,0:T(8,128)S(1)}, f32[8,1024]{1,0:T(8,128)S(1)}, u32[]{:S(2)}, u32[]{:S(2)}) %collective-permute-start.10) | collective-permute-done | bytes 32800 | tf_op jit(solution)/shard_map/ppermute | solution.py:416
  40.5 1.2 %collective-permute-start.11 = (f32[8,1024]{1,0:T(8,128)S(1)}, f32[8,1024]{1,0:T(8,128)S(1)}, u32[]{:S(2)}, u32[]{:S(2)}) collective-permute-start(f32[8,1024]{1,0:T(8,128)S(1)} %get-tuple-element.42), channel_id=1, source_target_pairs={{0,2},{2,0},{4,6},{6,4},{1,3},{3,1},{5,7},{7,5},{8,10},{10,8},{12,... | collective-permute-start | bytes 98312 | tf_op jit(solution)/shard_map/ppermute | solution.py:416
  41.7 2.3 %collective-permute-start.12 = (f32[8,1024]{1,0:T(8,128)S(1)}, f32[8,1024]{1,0:T(8,128)S(1)}, u32[]{:S(2)}, u32[]{:S(2)}) collective-permute-start(f32[8,1024]{1,0:T(8,128)S(1)} %get-tuple-element.43), channel_id=1, source_target_pairs={{0,6},{2,4},{4,2},{6,0},{1,7},{3,5},{5,3},{7,1},{8,14},{10,12},{12... | collective-permute-start | bytes 98312 | tf_op jit(solution)/shard_map/ppermute | solution.py:416
  44.0 3.7 %shard_map.83 = f32[32,1080]{1,0:T(8,128)} custom-call(s32[1,344]{1,0:T(1,128)S(1)} %get-tuple-element.28.refs_0_, s32[32,8]{1,0:T(8,128)S(1)} %get-tuple-element.29.refs_1_, f32[32,4096]{1,0:T(8,128)S(1)} %copy-done, bf16[8,216,512]{2,1,0:T(8,128)(2,1)S(1)} %get-tuple-element.30.refs_3_, bf16[8,216,512]{2,1,0:T(8,128)(2,1)S(1)} %get-tuple-element.31.refs_4_, ...), custom_call_target="tpu_custom_call" | custom-call | flops 2000000000 | bytes 8000000 | tf_op jit(solution)/shard_map/pallas_call | solution.py:481
  47.9 1.3 %collective-permute-done.18.before_ref.after_ref = f32[32,1024]{1,0:T(8,128)S(1)} collective-permute-done((f32[32,1024]{1,0:T(8,128)S(1)}, f32[32,1024]{1,0:T(8,128)S(1)}, u32[]{:S(2)}, u32[]{:S(2)}) %collective-permute-start.18) | collective-permute-done | bytes 131104 | tf_op jit(solution)/shard_map/ppermute | solution.py:491
  49.3 0.8 %shard_map.85 = f32[32,648]{1,0:T(8,128)} custom-call(f32[32,1024]{1,0:T(8,128)S(1)} %shard_map.84.parts_ref, f32[32,1024]{1,0:T(8,128)S(1)} %collective-permute-done.18.before_ref.after_ref, f32[32,1024]{1,0:T(8,128)S(1)} %collective-permute-done.18.before_ref.after_ref), custom_call_target="tpu_custom_call" | custom-call | tf_op jit(solution)/shard_map/pallas_call | solution.py:495
  (21 shorter events, 0.4 us)
Async XLA Ops:
  0.6 15.3 %collective-permute-start = (f32[32,1080]{1,0:T(8,128)}, f32[32,1080]{1,0:T(8,128)S(1)}, u32[]{:S(2)}, u32[]{:S(2)}) collective-permute-start(f32[32,1080]{1,0:T(8,128)} %refs_0_.1), channel_id=1, source_target_pairs={{0,2},{2,0},{4,6},{6,4},{1,3},{3,1},{5,7},{7,5},{8,10},{10,8},{12,... | collective-permute-start | bytes 414728 | tf_op jit(solution)/shard_map/ppermute | solution.py:427
  5.1 10.9 %collective-permute-start.2 = (f32[32,512]{1,0:T(8,128)S(1)}, f32[32,512]{1,0:T(8,128)S(1)}, u32[]{:S(2)}, u32[]{:S(2)}) collective-permute-start(f32[32,512]{1,0:T(8,128)S(1)} %get-tuple-element.32.refs_3_.refs_7_), channel_id=1, source_target_pairs={{0,6},{2,4},{4,2},{6,0},{1,7},{3,5},{5,3},{7,1},{8,14},{10,12},{12... | collective-permute-start | bytes 196616 | tf_op jit(solution)/shard_map/ppermute | solution.py:446
  7.6 8.3 %collective-permute-start.1 = (f32[32,512]{1,0:T(8,128)S(1)}, f32[32,512]{1,0:T(8,128)S(1)}, u32[]{:S(2)}, u32[]{:S(2)}) collective-permute-start(f32[32,512]{1,0:T(8,128)S(1)} %get-tuple-element.32.refs_3_.refs_7_), channel_id=1, source_target_pairs={{0,4},{2,6},{4,0},{6,2},{1,5},{3,7},{5,1},{7,3},{8,12},{10,14},{12... | collective-permute-start | bytes 196616 | tf_op jit(solution)/shard_map/ppermute | solution.py:446
  7.8 3.6 %collective-permute-start.3 = (f32[8,128]{1,0:T(8,128)S(1)}, f32[8,128]{1,0:T(8,128)S(1)}, u32[]{:S(2)}, u32[]{:S(2)}) collective-permute-start(f32[8,128]{1,0:T(8,128)S(1)} %get-tuple-element.33), channel_id=1, source_target_pairs={{0,8},{8,0},{16,24},{24,16},{1,9},{9,1},{17,25},{25,17},{2,10},{10... | collective-permute-start | bytes 12296 | tf_op jit(solution)/shard_map/ppermute | solution.py:453
  9.3 4.6 %collective-permute-start.4 = (f32[8,128]{1,0:T(8,128)S(1)}, f32[8,128]{1,0:T(8,128)S(1)}, u32[]{:S(2)}, u32[]{:S(2)}) collective-permute-start(f32[8,128]{1,0:T(8,128)S(1)} %get-tuple-element.34), channel_id=1, source_target_pairs={{0,16},{8,24},{16,0},{24,8},{1,17},{9,25},{17,1},{25,9},{2,18},{10... | collective-permute-start | bytes 12296 | tf_op jit(solution)/shard_map/ppermute | solution.py:453
  11.4 4.5 %collective-permute-start.5 = (f32[8,128]{1,0:T(8,128)S(1)}, f32[8,128]{1,0:T(8,128)S(1)}, u32[]{:S(2)}, u32[]{:S(2)}) collective-permute-start(f32[8,128]{1,0:T(8,128)S(1)} %get-tuple-element.35), channel_id=1, source_target_pairs={{0,24},{8,16},{16,8},{24,0},{1,25},{9,17},{17,9},{25,1},{2,26},{10... | collective-permute-start | bytes 12296 | tf_op jit(solution)/shard_map/ppermute | solution.py:453
  16.4 13.1 %collective-permute-start.6 = (f32[72,512]{1,0:T(8,128)S(1)}, f32[72,512]{1,0:T(8,128)S(1)}, u32[]{:S(2)}, u32[]{:S(2)}) collective-permute-start(f32[72,512]{1,0:T(8,128)S(1)} %get-tuple-element.36), channel_id=1, source_target_pairs={{0,8},{8,0},{16,24},{24,16},{1,9},{9,1},{17,25},{25,17},{2,10},{10... | collective-permute-start | bytes 442376 | tf_op jit(solution)/shard_map/ppermute | solution.py:463
  18.0 6.3 %collective-permute-start.14 = (f32[32,568]{1,0:T(8,128)S(1)}, f32[32,568]{1,0:T(8,128)S(1)}, u32[]{:S(2)}, u32[]{:S(2)}) collective-permute-start(f32[32,568]{1,0:T(8,128)S(1)} %get-tuple-element.46.refs_3_.refs_14_), channel_id=1, source_target_pairs={{0,6},{2,4},{4,2},{6,0},{1,7},{3,5},{5,3},{7,1},{8,14},{10,12},{12... | collective-permute-start | bytes 218120 | tf_op jit(solution)/shard_map/ppermute | solution.py:446
  20.8 6.1 %collective-permute-start.13 = (f32[32,568]{1,0:T(8,128)S(1)}, f32[32,568]{1,0:T(8,128)S(1)}, u32[]{:S(2)}, u32[]{:S(2)}) collective-permute-start(f32[32,568]{1,0:T(8,128)S(1)} %get-tuple-element.46.refs_3_.refs_14_), channel_id=1, source_target_pairs={{0,4},{2,6},{4,0},{6,2},{1,5},{3,7},{5,1},{7,3},{8,12},{10,14},{12... | collective-permute-start | bytes 218120 | tf_op jit(solution)/shard_map/ppermute | solution.py:446
  21.1 10.9 %collective-permute-start.7 = (f32[72,512]{1,0:T(8,128)S(1)}, f32[72,512]{1,0:T(8,128)S(1)}, u32[]{:S(2)}, u32[]{:S(2)}) collective-permute-start(f32[72,512]{1,0:T(8,128)S(1)} %get-tuple-element.37), channel_id=1, source_target_pairs={{0,16},{8,24},{16,0},{24,8},{1,17},{9,25},{17,1},{25,9},{2,18},{10... | collective-permute-start | bytes 442376 | tf_op jit(solution)/shard_map/ppermute | solution.py:463
  22.7 9.4 %collective-permute-start.8 = (f32[72,512]{1,0:T(8,128)S(1)}, f32[72,512]{1,0:T(8,128)S(1)}, u32[]{:S(2)}, u32[]{:S(2)}) collective-permute-start(f32[72,512]{1,0:T(8,128)S(1)} %get-tuple-element.38), channel_id=1, source_target_pairs={{0,24},{8,16},{16,8},{24,0},{1,25},{9,17},{17,9},{25,1},{2,26},{10... | collective-permute-start | bytes 442376 | tf_op jit(solution)/shard_map/ppermute | solution.py:463
  27.4 16.5 %collective-permute-start.15 = (f32[72,568]{1,0:T(8,128)S(1)}, f32[72,568]{1,0:T(8,128)S(1)}, u32[]{:S(2)}, u32[]{:S(2)}) collective-permute-start(f32[72,568]{1,0:T(8,128)S(1)} %get-tuple-element.47), channel_id=1, source_target_pairs={{0,8},{8,0},{16,24},{24,16},{1,9},{9,1},{17,25},{25,17},{2,10},{10... | collective-permute-start | bytes 490760 | tf_op jit(solution)/shard_map/ppermute | solution.py:463
  28.0 15.9 %collective-permute-start.16 = (f32[72,568]{1,0:T(8,128)S(1)}, f32[72,568]{1,0:T(8,128)S(1)}, u32[]{:S(2)}, u32[]{:S(2)}) collective-permute-start(f32[72,568]{1,0:T(8,128)S(1)} %get-tuple-element.48), channel_id=1, source_target_pairs={{0,16},{8,24},{16,0},{24,8},{1,17},{9,25},{17,1},{25,9},{2,18},{10... | collective-permute-start | bytes 490760 | tf_op jit(solution)/shard_map/ppermute | solution.py:463
  29.5 2.5 %copy-start = (f32[32,4096]{1,0:T(8,128)S(1)}, f32[32,4096]{1,0:T(8,128)}, u32[]{:S(2)}) copy-start(f32[32,4096]{1,0:T(8,128)} %refs_2_.3) | copy-start | bytes 1572868
  29.6 2.5 %copy-start.1 = (bf16[216,768]{1,0:T(8,128)(2,1)S(1)}, bf16[216,768]{1,0:T(8,128)(2,1)}, u32[]{:S(2)}) copy-start(bf16[216,768]{1,0:T(8,128)(2,1)} %constant.5.clone.refs_6_) | copy-start | bytes 995332
  29.6 2.5 %copy-start.2 = (bf16[216,768]{1,0:T(8,128)(2,1)S(1)}, bf16[216,768]{1,0:T(8,128)(2,1)}, u32[]{:S(2)}) copy-start(bf16[216,768]{1,0:T(8,128)(2,1)} %constant.4.clone.refs_5_) | copy-start | bytes 995332
  29.6 14.4 %collective-permute-start.17 = (f32[72,568]{1,0:T(8,128)S(1)}, f32[72,568]{1,0:T(8,128)S(1)}, u32[]{:S(2)}, u32[]{:S(2)}) collective-permute-start(f32[72,568]{1,0:T(8,128)S(1)} %get-tuple-element.49), channel_id=1, source_target_pairs={{0,24},{8,16},{16,8},{24,0},{1,25},{9,17},{17,9},{25,1},{2,26},{10... | collective-permute-start | bytes 490760 | tf_op jit(solution)/shard_map/ppermute | solution.py:463
  34.9 4.0 %collective-permute-start.9 = (f32[8,1024]{1,0:T(8,128)S(1)}, f32[8,1024]{1,0:T(8,128)S(1)}, u32[]{:S(2)}, u32[]{:S(2)}) collective-permute-start(f32[8,1024]{1,0:T(8,128)S(1)} %get-tuple-element.40), channel_id=1, source_target_pairs={{0,8},{8,0},{16,24},{24,16},{1,9},{9,1},{17,25},{25,17},{2,10},{10... | collective-permute-start | bytes 98312 | tf_op jit(solution)/shard_map/ppermute | solution.py:416
  35.5 4.8 %collective-permute-start.10 = (f32[8,1024]{1,0:T(8,128)S(1)}, f32[8,1024]{1,0:T(8,128)S(1)}, u32[]{:S(2)}, u32[]{:S(2)}) collective-permute-start(f32[8,1024]{1,0:T(8,128)S(1)} %get-tuple-element.41), channel_id=1, source_target_pairs={{0,24},{8,16},{16,8},{24,0},{1,25},{9,17},{17,9},{25,1},{2,26},{10... | collective-permute-start | bytes 98312 | tf_op jit(solution)/shard_map/ppermute | solution.py:416
  40.5 7.2 %collective-permute-start.11 = (f32[8,1024]{1,0:T(8,128)S(1)}, f32[8,1024]{1,0:T(8,128)S(1)}, u32[]{:S(2)}, u32[]{:S(2)}) collective-permute-start(f32[8,1024]{1,0:T(8,128)S(1)} %get-tuple-element.42), channel_id=1, source_target_pairs={{0,2},{2,0},{4,6},{6,4},{1,3},{3,1},{5,7},{7,5},{8,10},{10,8},{12,... | collective-permute-start | bytes 98312 | tf_op jit(solution)/shard_map/ppermute | solution.py:416
  41.7 6.0 %collective-permute-start.12 = (f32[8,1024]{1,0:T(8,128)S(1)}, f32[8,1024]{1,0:T(8,128)S(1)}, u32[]{:S(2)}, u32[]{:S(2)}) collective-permute-start(f32[8,1024]{1,0:T(8,128)S(1)} %get-tuple-element.43), channel_id=1, source_target_pairs={{0,6},{2,4},{4,2},{6,0},{1,7},{3,5},{5,3},{7,1},{8,14},{10,12},{12... | collective-permute-start | bytes 98312 | tf_op jit(solution)/shard_map/ppermute | solution.py:416
  47.8 1.4 %collective-permute-start.18 = (f32[32,1024]{1,0:T(8,128)S(1)}, f32[32,1024]{1,0:T(8,128)S(1)}, u32[]{:S(2)}, u32[]{:S(2)}) collective-permute-start(f32[32,1024]{1,0:T(8,128)S(1)} %shard_map.84.parts_ref), channel_id=1, source_target_pairs={{0,1},{1,0},{2,3},{3,2},{4,5},{5,4},{6,7},{7,6},{8,9},{9,8},{10,11... | collective-permute-start | bytes 393224 | tf_op jit(solution)/shard_map/ppermute | solution.py:491
where the time goes:
time: 50.3 us; the launch traced here: 50.1 us
  starting transfers between devices  28.2 us (56%)
  Pallas kernels  10.9 us (22%)
  waiting for transfers between devices  10.2 us (20%)
  between operations  0.75 us (1%)
    ppermute x6, starting transfers between devices, per_device(): lax.ppermute(piece, 'gx', partner(n_x, step + 1))  7.18 us
    ppermute x4, starting transfers between devices, swap_faces(): return (lax.ppermute(piece, axis, near), lax.ppermute(back, axis, across))  6.51 us
    ppermute x4, starting transfers between devices, per_device(): lax.ppermute(piece, 'gy', partner(n_y, step))  5.9 us
    ppermute x3, starting transfers between devices, per_device(): lax.ppermute(mask, 'gx', partner(n_x, step + 1))  5.46 us
    ppermute x4, waiting for transfers between devices, per_device(): lax.ppermute(piece, 'gy', partner(n_y, step))  3.77 us
    pallas_call x1, Pallas kernels, per_device(): call(lambda *refs: tail_kernel(len(near), *refs), shape((elems, width)),...  3.72 us
    ppermute x1, starting transfers between devices, per_device(): nearest = lax.ppermute(src_fields, 'gy', partner(n_y, 1))  3.12 us
    pallas_call x1, Pallas kernels, per_device(): call(lambda *refs: lead_kernel(n_y, n_x - 1, *refs), (shape((elems, 2 * N...  2.83 us
  transfers between devices with their start and end apart: 19, of which 7 were waited for; matrix products, arithmetic and copies ran while one was open for 0% of the time, Pallas kernels for 19%

commit v1 on v0

--- a/solution.py
+++ b/solution.py
@@ -257,7 +257,26 @@
     return own + ((back[:size] + back[size : 2 * size]) + back[2 * size :])
 
 
-def send_faces(even, first, last, send_ref, back_ref):
+def fold(rows, stride, end):
+    lane = lax.broadcasted_iota(jnp.int32, (rows.shape[0], PAD), 1)
+    keep = (lane // stride % 6 == end) & (lane < NB)
+    out = []
+    for c in range(4):
+        face = jnp.where(keep, rows[:, c * PAD : (c + 1) * PAD], 0.0)
+        out.append(face[:, : PAD // 2] + face[:, PAD // 2 :])
+    return jnp.concatenate(out, 1)
+
+
+def unfold(face):
+    half = PAD // 2
+    out = []
+    for c in range(4):
+        out += [face[:, c * half : (c + 1) * half]] * 2
+    return jnp.concatenate(out, 1)
+
+
+def send_faces(even, first, last, stride, send_ref, back_ref):
+    first, last = fold(first, stride, 0), fold(last, stride, 5)
     send_ref[...] = jnp.where(even, last, first)
     back_ref[...] = jnp.where(even, first, last)
 
@@ -265,6 +284,7 @@
 def take_faces(axis, got, back):
     me, count = lax.axis_index(axis), lax.axis_size(axis)
     even = me % 2 == 0
+    got, back = unfold(got), unfold(back)
     before = jnp.where(even, back, got)
     after = jnp.where(even, got, back)
     return jnp.where(me > 0, before, 0.0), jnp.where(me < count - 1, after, 0.0)
@@ -292,7 +312,7 @@
     parts_ref[...] = parts
     width = EY * EZ
     even = lax.axis_index("gx") % 2 == 0
-    send_faces(even, parts[:width], parts[-width:], send_ref, back_ref)
+    send_faces(even, parts[:width], parts[-width:], 36, send_ref, back_ref)
 
 
 def tail_kernel(count, ids_ref, index_ref, jac_ref, high_ref, low_ref, lumped_ref, lead_ref, *refs):
@@ -342,10 +362,10 @@
     first = [parts[x * width : x * width + EZ] for x in range(EX)]
     last = [parts[(x + 1) * width - EZ : (x + 1) * width] for x in range(EX)]
     first, last = jnp.concatenate(first, 0), jnp.concatenate(last, 0)
-    send_faces(lax.axis_index("gy") % 2 == 0, first, last, send_ref, back_ref)
-
-
-def y_kernel(parts_ref, got_ref, turn_ref, out_ref):
+    send_faces(lax.axis_index("gy") % 2 == 0, first, last, 6, send_ref, back_ref)
+
+
+def y_kernel(parts_ref, got_ref, turn_ref, out_ref, *face_refs):
     parts = parts_ref[...]
     width = EY * EZ
     far_before, far_after = take_faces("gy", got_ref[...], turn_ref[...])
@@ -358,7 +378,14 @@
         after += [parts[base + EZ : base + width], far_after[near]]
     before = jnp.concatenate(before, 0)
     after = jnp.concatenate(after, 0)
-    out_ref[...] = face_add(parts, before, after, 30, 6)
+    parts = face_add(parts, before, after, 30, 6)
+    out_ref[...] = parts
+    last, first = fold(parts, 1, 5), fold(parts, 1, 0)
+    if len(face_refs) == 1:
+        face_refs[0][...] = jnp.where(lax.axis_index("gz") % 2 == 0, last, first)
+    else:
+        face_refs[0][...] = last
+        face_refs[1][...] = first
 
 
 def z_kernel(parts_ref, before_ref, after_ref, out_ref):
@@ -367,8 +394,8 @@
     odd = lax.broadcasted_iota(jnp.int32, parts.shape, 0) % EZ == EZ - 1
     has_before = lax.axis_index("gz") > 0
     has_after = lax.axis_index("gz") < lax.axis_size("gz") - 1
-    far_before = jnp.where(has_before, pltpu.roll(before_ref[...], elems - 1, 0), 0.0)
-    far_after = jnp.where(has_after, pltpu.roll(after_ref[...], 1, 0), 0.0)
+    far_before = jnp.where(has_before, pltpu.roll(unfold(before_ref[...]), elems - 1, 0), 0.0)
+    far_after = jnp.where(has_after, pltpu.roll(unfold(after_ref[...]), 1, 0), 0.0)
     before = jnp.where(odd, pltpu.roll(parts, 1, 0), far_before)
     after = jnp.where(odd, far_after, pltpu.roll(parts, elems - 1, 0))
     parts = face_add(parts, before, after, 5, 1)
@@ -465,7 +492,7 @@
         ]
         gathered.append(columns[part] + arrived)
     near, far = gathered
-    face = shape((EY * EZ, 4 * PAD))
+    face = shape((EY * EZ, 2 * PAD))
     whole = shape((elems, 4 * PAD))
     lead, lumped, parts, piece, back = call(
         lambda *refs: lead_kernel(n_y, n_x - 1, *refs),
@@ -474,7 +501,7 @@
         [pltpu.VMEM((OVL * elems, CUT), F32)] * 2,
     )(ids, index, jac, high, low, fhigh, flow, *near)
     got, turn = swap_faces(piece, back, "gx", n_x)
-    face = shape((EX * EZ, 4 * PAD))
+    face = shape((EX * EZ, 2 * PAD))
     parts, piece, back = call(x_kernel, (whole, face, face), [VM] * 3)(parts, got, turn)
     got, turn = swap_faces(piece, back, "gy", n_y)
     scratch = pltpu.VMEM((OVL * elems, width - CUT + 128), F32)
@@ -486,12 +513,13 @@
         heavy,
     )(ids, index, jac, high, low, lumped, lead, *near, *far)
     got, turn, fields = lax.optimization_barrier((got, turn, fields))
-    parts = call(y_kernel, whole, [VM] * 3)(parts, got, turn)
+    ends = (shape((elems, 2 * PAD)),) * (1 if n_z == 2 else 2)
+    parts, *ends = call(y_kernel, (whole, *ends), [VM] * 3)(parts, got, turn)
     if n_z == 2:
-        before = after = lax.ppermute(parts, "gz", [(0, 1), (1, 0)])
+        before = after = lax.ppermute(ends[0], "gz", [(0, 1), (1, 0)])
     else:
-        before = lax.ppermute(parts, "gz", [(i, i + 1) for i in range(n_z - 1)])
-        after = lax.ppermute(parts, "gz", [(i + 1, i) for i in range(n_z - 1)])
+        before = lax.ppermute(ends[0], "gz", [(i, i + 1) for i in range(n_z - 1)])
+        after = lax.ppermute(ends[1], "gz", [(i + 1, i) for i in range(n_z - 1)])
     accel = call(z_kernel, shape((elems, 3 * NB)), [VM] * 3)(parts, before, after)
     return fields, accel
 

time: 50.3 us -> 50 us (level)
  no operation moved by 1% of the time
where the time goes in v1:
time: 50 us; the launch traced here: 49.8 us
  starting transfers between devices  28.2 us (56%)
  Pallas kernels  10.9 us (22%)
  waiting for transfers between devices  9.89 us (20%)
  between operations  0.75 us (2%)
    ppermute x6, starting transfers between devices, per_device(): lax.ppermute(piece, 'gx', partner(n_x, step + 1))  7.18 us
    ppermute x4, starting transfers between devices, swap_faces(): return (lax.ppermute(piece, axis, near), lax.ppermute(back, axis, across))  6.51 us
    ppermute x4, starting transfers between devices, per_device(): lax.ppermute(piece, 'gy', partner(n_y, step))  5.9 us
    ppermute x3, starting transfers between devices, per_device(): lax.ppermute(mask, 'gx', partner(n_x, step + 1))  5.46 us
    ppermute x4, waiting for transfers between devices, per_device(): lax.ppermute(piece, 'gy', partner(n_y, step))  3.77 us
    pallas_call x1, Pallas kernels, per_device(): call(lambda *refs: tail_kernel(len(near), *refs), shape((elems, width)),...  3.72 us
    ppermute x1, starting transfers between devices, per_device(): nearest = lax.ppermute(src_fields, 'gy', partner(n_y, 1))  3.12 us
    pallas_call x1, Pallas kernels, per_device(): call(lambda *refs: lead_kernel(n_y, n_x - 1, *refs), (shape((elems, 2 * N...  2.83 us
  transfers between devices with their start and end apart: 19, of which 7 were waited for; matrix products, arithmetic and copies ran while one was open for 0% of the time, Pallas kernels for 19%

profile of v1, /device:TPU:0, one launch (start us, length us, event | category | flops | bytes accessed | tf_op | source)
XLA Modules:
  0.0 49.8 jit_solution(15796702287926376456)
XLA Ops:
  0.6 3.1 %collective-permute-start = (f32[32,1080]{1,0:T(8,128)}, f32[32,1080]{1,0:T(8,128)S(1)}, u32[]{:S(2)}, u32[]{:S(2)}) collective-permute-start(f32[32,1080]{1,0:T(8,128)} %refs_0_.1), channel_id=1, source_target_pairs={{0,2},{2,0},{4,6},{6,4},{1,3},{3,1},{5,7},{7,5},{8,10},{10,8},{12,... | collective-permute-start | bytes 414728 | tf_op jit(solution)/shard_map/ppermute | solution.py:454
  3.7 1.3 %shard_map.77 = (f32[32,512]{1,0:T(8,128)S(1)}, f32[32,568]{1,0:T(8,128)S(1)}, s32[1,344]{1,0:T(1,128)S(1)}, s32[32,8]{1,0:T(8,128)S(1)}, f32[8,128]{1,0:T(8,128...) custom-call(f32[32,1080]{1,0:T(8,128)} %refs_0_.1, s32[8,32]{1,0:T(8,128)} %bitcast.4, s32[8,32]{1,0:T(8,128)} %bitcast.5), custom_call_target="tpu_custom_call" | custom-call | tf_op jit(solution)/shard_map/pallas_call | solution.py:457
  5.1 2.5 %collective-permute-start.2 = (f32[32,512]{1,0:T(8,128)S(1)}, f32[32,512]{1,0:T(8,128)S(1)}, u32[]{:S(2)}, u32[]{:S(2)}) collective-permute-start(f32[32,512]{1,0:T(8,128)S(1)} %get-tuple-element.34.refs_3_.refs_7_), channel_id=1, source_target_pairs={{0,6},{2,4},{4,2},{6,0},{1,7},{3,5},{5,3},{7,1},{8,14},{10,12},{12... | collective-permute-start | bytes 196616 | tf_op jit(solution)/shard_map/ppermute | solution.py:473
  7.6 0.2 collective-permute-start.1
  7.8 1.5 %collective-permute-start.3 = (f32[8,128]{1,0:T(8,128)S(1)}, f32[8,128]{1,0:T(8,128)S(1)}, u32[]{:S(2)}, u32[]{:S(2)}) collective-permute-start(f32[8,128]{1,0:T(8,128)S(1)} %get-tuple-element.35), channel_id=1, source_target_pairs={{0,8},{8,0},{16,24},{24,16},{1,9},{9,1},{17,25},{25,17},{2,10},{10... | collective-permute-start | bytes 12296 | tf_op jit(solution)/shard_map/ppermute | solution.py:480
  9.3 1.5 %collective-permute-start.4 = (f32[8,128]{1,0:T(8,128)S(1)}, f32[8,128]{1,0:T(8,128)S(1)}, u32[]{:S(2)}, u32[]{:S(2)}) collective-permute-start(f32[8,128]{1,0:T(8,128)S(1)} %get-tuple-element.36), channel_id=1, source_target_pairs={{0,16},{8,24},{16,0},{24,8},{1,17},{9,25},{17,1},{25,9},{2,18},{10... | collective-permute-start | bytes 12296 | tf_op jit(solution)/shard_map/ppermute | solution.py:480
  10.8 0.6 %collective-permute-done.3.refs_0_ = f32[8,128]{1,0:T(8,128)S(1)} collective-permute-done((f32[8,128]{1,0:T(8,128)S(1)}, f32[8,128]{1,0:T(8,128)S(1)}, u32[]{:S(2)}, u32[]{:S(2)}) %collective-permute-start.3) | collective-permute-done | bytes 4128 | tf_op jit(solution)/shard_map/ppermute | solution.py:480
  11.4 2.4 %collective-permute-start.5 = (f32[8,128]{1,0:T(8,128)S(1)}, f32[8,128]{1,0:T(8,128)S(1)}, u32[]{:S(2)}, u32[]{:S(2)}) collective-permute-start(f32[8,128]{1,0:T(8,128)S(1)} %get-tuple-element.37), channel_id=1, source_target_pairs={{0,24},{8,16},{16,8},{24,0},{1,25},{9,17},{17,9},{25,1},{2,26},{10... | collective-permute-start | bytes 12296 | tf_op jit(solution)/shard_map/ppermute | solution.py:480
  13.9 2.1 %collective-permute-done.5.refs_2_ = f32[8,128]{1,0:T(8,128)S(1)} collective-permute-done((f32[8,128]{1,0:T(8,128)S(1)}, f32[8,128]{1,0:T(8,128)S(1)}, u32[]{:S(2)}, u32[]{:S(2)}) %collective-permute-start.5) | collective-permute-done | bytes 4128 | tf_op jit(solution)/shard_map/ppermute | solution.py:480
  16.0 0.4 shard_map.79
  16.4 1.6 %collective-permute-start.6 = (f32[72,512]{1,0:T(8,128)S(1)}, f32[72,512]{1,0:T(8,128)S(1)}, u32[]{:S(2)}, u32[]{:S(2)}) collective-permute-start(f32[72,512]{1,0:T(8,128)S(1)} %get-tuple-element.38), channel_id=1, source_target_pairs={{0,8},{8,0},{16,24},{24,16},{1,9},{9,1},{17,25},{25,17},{2,10},{10... | collective-permute-start | bytes 442376 | tf_op jit(solution)/shard_map/ppermute | solution.py:490
  18.0 2.8 %collective-permute-start.14 = (f32[32,568]{1,0:T(8,128)S(1)}, f32[32,568]{1,0:T(8,128)S(1)}, u32[]{:S(2)}, u32[]{:S(2)}) collective-permute-start(f32[32,568]{1,0:T(8,128)S(1)} %get-tuple-element.48.refs_3_.refs_14_), channel_id=1, source_target_pairs={{0,6},{2,4},{4,2},{6,0},{1,7},{3,5},{5,3},{7,1},{8,14},{10,12},{12... | collective-permute-start | bytes 218120 | tf_op jit(solution)/shard_map/ppermute | solution.py:473
  20.8 0.3 collective-permute-start.13
  21.1 1.5 %collective-permute-start.7 = (f32[72,512]{1,0:T(8,128)S(1)}, f32[72,512]{1,0:T(8,128)S(1)}, u32[]{:S(2)}, u32[]{:S(2)}) collective-permute-start(f32[72,512]{1,0:T(8,128)S(1)} %get-tuple-element.39), channel_id=1, source_target_pairs={{0,16},{8,24},{16,0},{24,8},{1,17},{9,25},{17,1},{25,9},{2,18},{10... | collective-permute-start | bytes 442376 | tf_op jit(solution)/shard_map/ppermute | solution.py:490
  22.7 0.5 collective-permute-start.8
  23.1 1.2 %collective-permute-done.14.refs_6_.refs_17_ = f32[32,568]{1,0:T(8,128)S(1)} collective-permute-done((f32[32,568]{1,0:T(8,128)S(1)}, f32[32,568]{1,0:T(8,128)S(1)}, u32[]{:S(2)}, u32[]{:S(2)}) %collective-permute-start.14) | collective-permute-done | bytes 72736 | tf_op jit(solution)/shard_map/ppermute | solution.py:473
  24.3 2.6 %collective-permute-done.13.refs_5_.refs_16_ = f32[32,568]{1,0:T(8,128)S(1)} collective-permute-done((f32[32,568]{1,0:T(8,128)S(1)}, f32[32,568]{1,0:T(8,128)S(1)}, u32[]{:S(2)}, u32[]{:S(2)}) %collective-permute-start.13) | collective-permute-done | bytes 72736 | tf_op jit(solution)/shard_map/ppermute | solution.py:473
  26.9 0.5 %shard_map.82 = (f32[72,568]{1,0:T(8,128)S(1)}, f32[72,568]{1,0:T(8,128)S(1)}, f32[72,568]{1,0:T(8,128)S(1)}) custom-call(f32[8,128]{1,0:T(8,128)S(1)} %collective-permute-done.3.refs_0_, f32[8,128]{1,0:T(8,128)S(1)} %collective-permute-done.4.refs_1_, f32[8,128]{1,0:T(8,128)S(1)} %collective-permute-done.5.refs_2_, ...), custom_call_target="tpu_custom_call" | custom-call | tf_op jit(solution)/shard_map/pallas_call | solution.py:484
  27.4 0.6 %collective-permute-start.15 = (f32[72,568]{1,0:T(8,128)S(1)}, f32[72,568]{1,0:T(8,128)S(1)}, u32[]{:S(2)}, u32[]{:S(2)}) collective-permute-start(f32[72,568]{1,0:T(8,128)S(1)} %get-tuple-element.49), channel_id=1, source_target_pairs={{0,8},{8,0},{16,24},{24,16},{1,9},{9,1},{17,25},{25,17},{2,10},{10... | collective-permute-start | bytes 490760 | tf_op jit(solution)/shard_map/ppermute | solution.py:490
  28.0 1.5 %collective-permute-start.16 = (f32[72,568]{1,0:T(8,128)S(1)}, f32[72,568]{1,0:T(8,128)S(1)}, u32[]{:S(2)}, u32[]{:S(2)}) collective-permute-start(f32[72,568]{1,0:T(8,128)S(1)} %get-tuple-element.50), channel_id=1, source_target_pairs={{0,16},{8,24},{16,0},{24,8},{1,17},{9,25},{17,1},{25,9},{2,18},{10... | collective-permute-start | bytes 490760 | tf_op jit(solution)/shard_map/ppermute | solution.py:490
  29.6 1.5 %collective-permute-start.17 = (f32[72,568]{1,0:T(8,128)S(1)}, f32[72,568]{1,0:T(8,128)S(1)}, u32[]{:S(2)}, u32[]{:S(2)}) collective-permute-start(f32[72,568]{1,0:T(8,128)S(1)} %get-tuple-element.51), channel_id=1, source_target_pairs={{0,24},{8,16},{16,8},{24,0},{1,25},{9,17},{17,9},{25,1},{2,26},{10... | collective-permute-start | bytes 490760 | tf_op jit(solution)/shard_map/ppermute | solution.py:490
  31.1 1.0 %shard_map.78 = (bf16[8,216,512]{2,1,0:T(8,128)(2,1)S(1)}, bf16[8,216,512]{2,1,0:T(8,128)(2,1)S(1)}) custom-call(), custom_call_target="tpu_custom_call" | custom-call | flops 2000000000 | bytes 8000000 | tf_op jit(solution)/shard_map/pallas_call | solution.py:479
  32.1 2.8 %shard_map.80 = (f32[32,432]{1,0:T(8,128)S(1)}, f32[32,216]{1,0:T(8,128)S(1)}, f32[32,1024]{1,0:T(8,128)S(1)}, f32[8,512]{1,0:T(8,128)S(1)}, f32[8,512]{1,0:T(8,128)S(1)}) custom-call(s32[1,344]{1,0:T(1,128)S(1)} %get-tuple-element.30.refs_0_, s32[32,8]{1,0:T(8,128)S(1)} %get-tuple-element.31.refs_1_, f32[32,4096]{1,0:T(8,128)S(1)} %copy-done, ...), custom_call_target="tpu_custom_call" | custom-call | tf_op jit(solution)/shard_map/pallas_call | solution.py:497
  34.9 0.6 %collective-permute-start.9 = (f32[8,512]{1,0:T(8,128)S(1)}, f32[8,512]{1,0:T(8,128)S(1)}, u32[]{:S(2)}, u32[]{:S(2)}) collective-permute-start(f32[8,512]{1,0:T(8,128)S(1)} %get-tuple-element.42), channel_id=1, source_target_pairs={{0,8},{8,0},{16,24},{24,16},{1,9},{9,1},{17,25},{25,17},{2,10},{10... | collective-permute-start | bytes 49160 | tf_op jit(solution)/shard_map/ppermute | solution.py:443
  35.5 2.4 %collective-permute-start.10 = (f32[8,512]{1,0:T(8,128)S(1)}, f32[8,512]{1,0:T(8,128)S(1)}, u32[]{:S(2)}, u32[]{:S(2)}) collective-permute-start(f32[8,512]{1,0:T(8,128)S(1)} %get-tuple-element.43), channel_id=1, source_target_pairs={{0,24},{8,16},{16,8},{24,0},{1,25},{9,17},{17,9},{25,1},{2,26},{10... | collective-permute-start | bytes 49160 | tf_op jit(solution)/shard_map/ppermute | solution.py:443
  38.0 0.8 %collective-permute-done.9.got_ref = f32[8,512]{1,0:T(8,128)S(1)} collective-permute-done((f32[8,512]{1,0:T(8,128)S(1)}, f32[8,512]{1,0:T(8,128)S(1)}, u32[]{:S(2)}, u32[]{:S(2)}) %collective-permute-start.9) | collective-permute-done | bytes 16416 | tf_op jit(solution)/shard_map/ppermute | solution.py:443
  38.7 1.4 %collective-permute-done.10.turn_ref = f32[8,512]{1,0:T(8,128)S(1)} collective-permute-done((f32[8,512]{1,0:T(8,128)S(1)}, f32[8,512]{1,0:T(8,128)S(1)}, u32[]{:S(2)}, u32[]{:S(2)}) %collective-permute-start.10) | collective-permute-done | bytes 16416 | tf_op jit(solution)/shard_map/ppermute | solution.py:443
  40.3 1.2 %collective-permute-start.11 = (f32[8,512]{1,0:T(8,128)S(1)}, f32[8,512]{1,0:T(8,128)S(1)}, u32[]{:S(2)}, u32[]{:S(2)}) collective-permute-start(f32[8,512]{1,0:T(8,128)S(1)} %get-tuple-element.44), channel_id=1, source_target_pairs={{0,2},{2,0},{4,6},{6,4},{1,3},{3,1},{5,7},{7,5},{8,10},{10,8},{12,... | collective-permute-start | bytes 49160 | tf_op jit(solution)/shard_map/ppermute | solution.py:443
  41.5 2.3 %collective-permute-start.12 = (f32[8,512]{1,0:T(8,128)S(1)}, f32[8,512]{1,0:T(8,128)S(1)}, u32[]{:S(2)}, u32[]{:S(2)}) collective-permute-start(f32[8,512]{1,0:T(8,128)S(1)} %get-tuple-element.45), channel_id=1, source_target_pairs={{0,6},{2,4},{4,2},{6,0},{1,7},{3,5},{5,3},{7,1},{8,14},{10,12},{12... | collective-permute-start | bytes 49160 | tf_op jit(solution)/shard_map/ppermute | solution.py:443
  43.8 3.7 %shard_map.83 = f32[32,1080]{1,0:T(8,128)} custom-call(s32[1,344]{1,0:T(1,128)S(1)} %get-tuple-element.30.refs_0_, s32[32,8]{1,0:T(8,128)S(1)} %get-tuple-element.31.refs_1_, f32[32,4096]{1,0:T(8,128)S(1)} %copy-done, bf16[8,216,512]{2,1,0:T(8,128)(2,1)S(1)} %get-tuple-element.32.refs_3_, bf16[8,216,512]{2,1,0:T(8,128)(2,1)S(1)} %get-tuple-element.33.refs_4_, ...), custom_call_target="tpu_custom_call" | custom-call | flops 2000000000 | bytes 8000000 | tf_op jit(solution)/shard_map/pallas_call | solution.py:508
  47.7 1.2 %collective-permute-done.18.before_ref.after_ref = f32[32,512]{1,0:T(8,128)S(1)} collective-permute-done((f32[32,512]{1,0:T(8,128)S(1)}, f32[32,512]{1,0:T(8,128)S(1)}, u32[]{:S(2)}, u32[]{:S(2)}) %collective-permute-start.18) | collective-permute-done | bytes 65568 | tf_op jit(solution)/shard_map/ppermute | solution.py:519
  49.0 0.8 %shard_map.85 = f32[32,648]{1,0:T(8,128)} custom-call(f32[32,1024]{1,0:T(8,128)S(1)} %get-tuple-element.56.parts_ref, f32[32,512]{1,0:T(8,128)S(1)} %collective-permute-done.18.before_ref.after_ref, f32[32,512]{1,0:T(8,128)S(1)} %collective-permute-done.18.before_ref.after_ref), custom_call_target="tpu_custom_call" | custom-call | tf_op jit(solution)/shard_map/pallas_call | solution.py:523
  (21 shorter events, 0.4 us)
Async XLA Ops:
  0.6 15.3 %collective-permute-start = (f32[32,1080]{1,0:T(8,128)}, f32[32,1080]{1,0:T(8,128)S(1)}, u32[]{:S(2)}, u32[]{:S(2)}) collective-permute-start(f32[32,1080]{1,0:T(8,128)} %refs_0_.1), channel_id=1, source_target_pairs={{0,2},{2,0},{4,6},{6,4},{1,3},{3,1},{5,7},{7,5},{8,10},{10,8},{12,... | collective-permute-start | bytes 414728 | tf_op jit(solution)/shard_map/ppermute | solution.py:454
  5.1 10.9 %collective-permute-start.2 = (f32[32,512]{1,0:T(8,128)S(1)}, f32[32,512]{1,0:T(8,128)S(1)}, u32[]{:S(2)}, u32[]{:S(2)}) collective-permute-start(f32[32,512]{1,0:T(8,128)S(1)} %get-tuple-element.34.refs_3_.refs_7_), channel_id=1, source_target_pairs={{0,6},{2,4},{4,2},{6,0},{1,7},{3,5},{5,3},{7,1},{8,14},{10,12},{12... | collective-permute-start | bytes 196616 | tf_op jit(solution)/shard_map/ppermute | solution.py:473
  7.6 8.3 %collective-permute-start.1 = (f32[32,512]{1,0:T(8,128)S(1)}, f32[32,512]{1,0:T(8,128)S(1)}, u32[]{:S(2)}, u32[]{:S(2)}) collective-permute-start(f32[32,512]{1,0:T(8,128)S(1)} %get-tuple-element.34.refs_3_.refs_7_), channel_id=1, source_target_pairs={{0,4},{2,6},{4,0},{6,2},{1,5},{3,7},{5,1},{7,3},{8,12},{10,14},{12... | collective-permute-start | bytes 196616 | tf_op jit(solution)/shard_map/ppermute | solution.py:473
  7.8 3.6 %collective-permute-start.3 = (f32[8,128]{1,0:T(8,128)S(1)}, f32[8,128]{1,0:T(8,128)S(1)}, u32[]{:S(2)}, u32[]{:S(2)}) collective-permute-start(f32[8,128]{1,0:T(8,128)S(1)} %get-tuple-element.35), channel_id=1, source_target_pairs={{0,8},{8,0},{16,24},{24,16},{1,9},{9,1},{17,25},{25,17},{2,10},{10... | collective-permute-start | bytes 12296 | tf_op jit(solution)/shard_map/ppermute | solution.py:480
  9.3 4.6 %collective-permute-start.4 = (f32[8,128]{1,0:T(8,128)S(1)}, f32[8,128]{1,0:T(8,128)S(1)}, u32[]{:S(2)}, u32[]{:S(2)}) collective-permute-start(f32[8,128]{1,0:T(8,128)S(1)} %get-tuple-element.36), channel_id=1, source_target_pairs={{0,16},{8,24},{16,0},{24,8},{1,17},{9,25},{17,1},{25,9},{2,18},{10... | collective-permute-start | bytes 12296 | tf_op jit(solution)/shard_map/ppermute | solution.py:480
  11.4 4.5 %collective-permute-start.5 = (f32[8,128]{1,0:T(8,128)S(1)}, f32[8,128]{1,0:T(8,128)S(1)}, u32[]{:S(2)}, u32[]{:S(2)}) collective-permute-start(f32[8,128]{1,0:T(8,128)S(1)} %get-tuple-element.37), channel_id=1, source_target_pairs={{0,24},{8,16},{16,8},{24,0},{1,25},{9,17},{17,9},{25,1},{2,26},{10... | collective-permute-start | bytes 12296 | tf_op jit(solution)/shard_map/ppermute | solution.py:480
  16.4 13.1 %collective-permute-start.6 = (f32[72,512]{1,0:T(8,128)S(1)}, f32[72,512]{1,0:T(8,128)S(1)}, u32[]{:S(2)}, u32[]{:S(2)}) collective-permute-start(f32[72,512]{1,0:T(8,128)S(1)} %get-tuple-element.38), channel_id=1, source_target_pairs={{0,8},{8,0},{16,24},{24,16},{1,9},{9,1},{17,25},{25,17},{2,10},{10... | collective-permute-start | bytes 442376 | tf_op jit(solution)/shard_map/ppermute | solution.py:490
  18.0 6.3 %collective-permute-start.14 = (f32[32,568]{1,0:T(8,128)S(1)}, f32[32,568]{1,0:T(8,128)S(1)}, u32[]{:S(2)}, u32[]{:S(2)}) collective-permute-start(f32[32,568]{1,0:T(8,128)S(1)} %get-tuple-element.48.refs_3_.refs_14_), channel_id=1, source_target_pairs={{0,6},{2,4},{4,2},{6,0},{1,7},{3,5},{5,3},{7,1},{8,14},{10,12},{12... | collective-permute-start | bytes 218120 | tf_op jit(solution)/shard_map/ppermute | solution.py:473
  20.8 6.1 %collective-permute-start.13 = (f32[32,568]{1,0:T(8,128)S(1)}, f32[32,568]{1,0:T(8,128)S(1)}, u32[]{:S(2)}, u32[]{:S(2)}) collective-permute-start(f32[32,568]{1,0:T(8,128)S(1)} %get-tuple-element.48.refs_3_.refs_14_), channel_id=1, source_target_pairs={{0,4},{2,6},{4,0},{6,2},{1,5},{3,7},{5,1},{7,3},{8,12},{10,14},{12... | collective-permute-start | bytes 218120 | tf_op jit(solution)/shard_map/ppermute | solution.py:473
  21.1 10.9 %collective-permute-start.7 = (f32[72,512]{1,0:T(8,128)S(1)}, f32[72,512]{1,0:T(8,128)S(1)}, u32[]{:S(2)}, u32[]{:S(2)}) collective-permute-start(f32[72,512]{1,0:T(8,128)S(1)} %get-tuple-element.39), channel_id=1, source_target_pairs={{0,16},{8,24},{16,0},{24,8},{1,17},{9,25},{17,1},{25,9},{2,18},{10... | collective-permute-start | bytes 442376 | tf_op jit(solution)/shard_map/ppermute | solution.py:490
  22.7 9.4 %collective-permute-start.8 = (f32[72,512]{1,0:T(8,128)S(1)}, f32[72,512]{1,0:T(8,128)S(1)}, u32[]{:S(2)}, u32[]{:S(2)}) collective-permute-start(f32[72,512]{1,0:T(8,128)S(1)} %get-tuple-element.40), channel_id=1, source_target_pairs={{0,24},{8,16},{16,8},{24,0},{1,25},{9,17},{17,9},{25,1},{2,26},{10... | collective-permute-start | bytes 442376 | tf_op jit(solution)/shard_map/ppermute | solution.py:490
  27.4 16.3 %collective-permute-start.15 = (f32[72,568]{1,0:T(8,128)S(1)}, f32[72,568]{1,0:T(8,128)S(1)}, u32[]{:S(2)}, u32[]{:S(2)}) collective-permute-start(f32[72,568]{1,0:T(8,128)S(1)} %get-tuple-element.49), channel_id=1, source_target_pairs={{0,8},{8,0},{16,24},{24,16},{1,9},{9,1},{17,25},{25,17},{2,10},{10... | collective-permute-start | bytes 490760 | tf_op jit(solution)/shard_map/ppermute | solution.py:490
  28.0 15.7 %collective-permute-start.16 = (f32[72,568]{1,0:T(8,128)S(1)}, f32[72,568]{1,0:T(8,128)S(1)}, u32[]{:S(2)}, u32[]{:S(2)}) collective-permute-start(f32[72,568]{1,0:T(8,128)S(1)} %get-tuple-element.50), channel_id=1, source_target_pairs={{0,16},{8,24},{16,0},{24,8},{1,17},{9,25},{17,1},{25,9},{2,18},{10... | collective-permute-start | bytes 490760 | tf_op jit(solution)/shard_map/ppermute | solution.py:490
  29.5 2.5 %copy-start = (f32[32,4096]{1,0:T(8,128)S(1)}, f32[32,4096]{1,0:T(8,128)}, u32[]{:S(2)}) copy-start(f32[32,4096]{1,0:T(8,128)} %refs_2_.3) | copy-start | bytes 1572868
  29.6 2.5 %copy-start.1 = (bf16[216,768]{1,0:T(8,128)(2,1)S(1)}, bf16[216,768]{1,0:T(8,128)(2,1)}, u32[]{:S(2)}) copy-start(bf16[216,768]{1,0:T(8,128)(2,1)} %constant.5.clone.refs_6_) | copy-start | bytes 995332
  29.6 2.5 %copy-start.2 = (bf16[216,768]{1,0:T(8,128)(2,1)S(1)}, bf16[216,768]{1,0:T(8,128)(2,1)}, u32[]{:S(2)}) copy-start(bf16[216,768]{1,0:T(8,128)(2,1)} %constant.4.clone.refs_5_) | copy-start | bytes 995332
  29.6 14.2 %collective-permute-start.17 = (f32[72,568]{1,0:T(8,128)S(1)}, f32[72,568]{1,0:T(8,128)S(1)}, u32[]{:S(2)}, u32[]{:S(2)}) collective-permute-start(f32[72,568]{1,0:T(8,128)S(1)} %get-tuple-element.51), channel_id=1, source_target_pairs={{0,24},{8,16},{16,8},{24,0},{1,25},{9,17},{17,9},{25,1},{2,26},{10... | collective-permute-start | bytes 490760 | tf_op jit(solution)/shard_map/ppermute | solution.py:490
  34.9 3.8 %collective-permute-start.9 = (f32[8,512]{1,0:T(8,128)S(1)}, f32[8,512]{1,0:T(8,128)S(1)}, u32[]{:S(2)}, u32[]{:S(2)}) collective-permute-start(f32[8,512]{1,0:T(8,128)S(1)} %get-tuple-element.42), channel_id=1, source_target_pairs={{0,8},{8,0},{16,24},{24,16},{1,9},{9,1},{17,25},{25,17},{2,10},{10... | collective-permute-start | bytes 49160 | tf_op jit(solution)/shard_map/ppermute | solution.py:443
  35.5 4.6 %collective-permute-start.10 = (f32[8,512]{1,0:T(8,128)S(1)}, f32[8,512]{1,0:T(8,128)S(1)}, u32[]{:S(2)}, u32[]{:S(2)}) collective-permute-start(f32[8,512]{1,0:T(8,128)S(1)} %get-tuple-element.43), channel_id=1, source_target_pairs={{0,24},{8,16},{16,8},{24,0},{1,25},{9,17},{17,9},{25,1},{2,26},{10... | collective-permute-start | bytes 49160 | tf_op jit(solution)/shard_map/ppermute | solution.py:443
  40.3 7.2 %collective-permute-start.11 = (f32[8,512]{1,0:T(8,128)S(1)}, f32[8,512]{1,0:T(8,128)S(1)}, u32[]{:S(2)}, u32[]{:S(2)}) collective-permute-start(f32[8,512]{1,0:T(8,128)S(1)} %get-tuple-element.44), channel_id=1, source_target_pairs={{0,2},{2,0},{4,6},{6,4},{1,3},{3,1},{5,7},{7,5},{8,10},{10,8},{12,... | collective-permute-start | bytes 49160 | tf_op jit(solution)/shard_map/ppermute | solution.py:443
  41.5 6.0 %collective-permute-start.12 = (f32[8,512]{1,0:T(8,128)S(1)}, f32[8,512]{1,0:T(8,128)S(1)}, u32[]{:S(2)}, u32[]{:S(2)}) collective-permute-start(f32[8,512]{1,0:T(8,128)S(1)} %get-tuple-element.45), channel_id=1, source_target_pairs={{0,6},{2,4},{4,2},{6,0},{1,7},{3,5},{5,3},{7,1},{8,14},{10,12},{12... | collective-permute-start | bytes 49160 | tf_op jit(solution)/shard_map/ppermute | solution.py:443
  47.7 1.3 %collective-permute-start.18 = (f32[32,512]{1,0:T(8,128)S(1)}, f32[32,512]{1,0:T(8,128)S(1)}, u32[]{:S(2)}, u32[]{:S(2)}) collective-permute-start(f32[32,512]{1,0:T(8,128)S(1)} %get-tuple-element.57), channel_id=1, source_target_pairs={{0,1},{1,0},{2,3},{3,2},{4,5},{5,4},{6,7},{7,6},{8,9},{9,8},{10,11... | collective-permute-start | bytes 196616 | tf_op jit(solution)/shard_map/ppermute | solution.py:519

commit v2 on v1

--- a/solution.py
+++ b/solution.py
@@ -315,20 +315,40 @@
     send_faces(even, parts[:width], parts[-width:], 36, send_ref, back_ref)
 
 
-def tail_kernel(count, ids_ref, index_ref, jac_ref, high_ref, low_ref, lumped_ref, lead_ref, *refs):
-    near, far = refs[:count], refs[count : 2 * count]
-    out_ref, *picked = refs[2 * count :]
-    elems = jac_ref.shape[0]
+def tail_rows(near, far):
     start = CUT - 128
-    hot = jnp.concatenate(hits(index_ref, ids_ref[...], range(OVL)), 0).astype(BF)
     rows = []
     for a, b in zip(near, far):
         if a.shape[1] == NB * FIELDS:
             rows.append(a[:, start:])
         else:
             rows.append(jnp.concatenate([a[:, start:], b[...]], 1))
-    pick(hot, jnp.concatenate(rows, 0), picked)
-    total = project(2 * NB - start, picked, jac_ref, high_ref, low_ref, False)
+    return jnp.concatenate(rows, 0)
+
+
+def ready_kernel(owners, ids_ref, index_ref, *refs):
+    near, far = refs[:owners], refs[owners : 2 * owners]
+    high_ref, low_ref = refs[2 * owners :]
+    rows = tail_rows(near, far)
+    wanted = ids_ref[:, : rows.shape[0]]
+    hot = jnp.concatenate(hits(index_ref, wanted, range(OVL)), 0).astype(BF)
+    high, low = split(rows)
+    high_ref[...] = dot(hot, high).astype(BF)
+    low_ref[...] = dot(hot, low).astype(BF)
+
+
+def tail_kernel(count, ids_ref, index_ref, jac_ref, high_ref, low_ref, lumped_ref, lead_ref, *refs):
+    base_high, base_low = refs[:2]
+    near, far = refs[2 : 2 + count], refs[2 + count : 2 + 2 * count]
+    out_ref, *picked = refs[2 + 2 * count :]
+    elems = jac_ref.shape[0]
+    rows = tail_rows(near, far)
+    wanted = ids_ref[:, ids_ref.shape[1] - rows.shape[0] :]
+    hot = jnp.concatenate(hits(index_ref, wanted, range(OVL)), 0).astype(BF)
+    high, low = split(rows)
+    picked[0][...] = base_high[...].astype(F32) + dot(hot, high)
+    picked[1][...] = base_low[...].astype(F32) + dot(hot, low)
+    total = project(2 * NB - CUT + 128, picked, jac_ref, high_ref, low_ref, False)
     lumped = lumped_ref[...]
     out_ref[:, : 2 * NB] = lead_ref[...]
     for f in range(3):
@@ -487,8 +507,8 @@
             [VM] * (n_x - 1 + n_y),
         )(*asked, *columns[part])
         arrived = [
-            lax.ppermute(piece, "gx", partner(n_x, step + 1))
-            for step, piece in enumerate(packed)
+            lax.ppermute(piece, "gx", partner(n_x, step))
+            for step, piece in enumerate(packed, 1)
         ]
         gathered.append(columns[part] + arrived)
     near, far = gathered
@@ -501,17 +521,26 @@
         [pltpu.VMEM((OVL * elems, CUT), F32)] * 2,
     )(ids, index, jac, high, low, fhigh, flow, *near)
     got, turn = swap_faces(piece, back, "gx", n_x)
+    rows_here = (*near[:n_y], *far[:n_y])
+    picks = shape((OVL * elems, width - CUT + 128), BF)
+    base = call(
+        lambda *refs: ready_kernel(n_y, *refs),
+        (picks, picks),
+        [VM] * (2 + len(rows_here)),
+        cost=heavy,
+    )(ids, index, *rows_here)
+    got, turn, base = lax.optimization_barrier((got, turn, base))
     face = shape((EX * EZ, 2 * PAD))
     parts, piece, back = call(x_kernel, (whole, face, face), [VM] * 3)(parts, got, turn)
     got, turn = swap_faces(piece, back, "gy", n_y)
     scratch = pltpu.VMEM((OVL * elems, width - CUT + 128), F32)
     fields = call(
-        lambda *refs: tail_kernel(len(near), *refs),
+        lambda *refs: tail_kernel(n_x - 1, *refs),
         shape((elems, width)),
-        [VM] * (7 + 2 * len(near)),
+        [VM] * (9 + 2 * (n_x - 1)),
         [scratch] * 2,
         heavy,
-    )(ids, index, jac, high, low, lumped, lead, *near, *far)
+    )(ids, index, jac, high, low, lumped, lead, *base, *near[n_y:], *far[n_y:])
     got, turn, fields = lax.optimization_barrier((got, turn, fields))
     ends = (shape((elems, 2 * PAD)),) * (1 if n_z == 2 else 2)
     parts, *ends = call(y_kernel, (whole, *ends), [VM] * 3)(parts, got, turn)

time: 50 us -> 48.1 us (0.962)
  waiting for transfers between devices: 9.89 us -> 7.48 us
    ppermute x4, waiting for transfers between devices: 3.77 us -> 0.01 us  [per_device(): lax.ppermute(piece, 'gy', partner(n_y, step))]
    ppermute x6, waiting for transfers between devices: 0.02 us -> 2.16 us  [per_device(): lax.ppermute(piece, 'gx', partner(n_x, step))]
    ppermute x3, waiting for transfers between devices: 2.65 us -> 0.6 us  [per_device(): lax.ppermute(mask, 'gx', partner(n_x, step + 1))]
    ppermute x4, starting transfers between devices: 5.9 us -> 7.52 us  [per_device(): lax.ppermute(piece, 'gy', partner(n_y, step))]
    ppermute x4, starting transfers between devices: 6.51 us -> 4.97 us  [swap_faces(): return (lax.ppermute(piece, axis, near), lax.ppermute(back, axis, across))]
    ppermute x4, waiting for transfers between devices: 2.2 us -> 3.47 us  [swap_faces(): return (lax.ppermute(piece, axis, near), lax.ppermute(back, axis, across))]
    pallas_call x1 -> x2, Pallas kernels: 3.72 us -> 4.03 us  [the longest x1 3.61 us: per_device(): call(lambda *refs: tail_kernel(n_x - 1, *refs), shape((elems, width)), [V...]
  transfers between devices with their start and end apart: 19 -> 19, of which waited for: 7 -> 5; matrix products, arithmetic and copies ran while one was open for 0% -> 0% of each run, Pallas kernels for 19% -> 21%
where the time goes in v2:
time: 48.1 us; the launch traced here: 47.9 us
  starting transfers between devices  28.4 us (59%)
  Pallas kernels  11.2 us (23%)
  waiting for transfers between devices  7.48 us (16%)
  between operations  0.75 us (2%)
    ppermute x4, starting transfers between devices, per_device(): lax.ppermute(piece, 'gy', partner(n_y, step))  7.52 us
    ppermute x6, starting transfers between devices, per_device(): lax.ppermute(piece, 'gx', partner(n_x, step))  7.28 us
    ppermute x3, starting transfers between devices, per_device(): lax.ppermute(mask, 'gx', partner(n_x, step + 1))  5.46 us
    ppermute x4, starting transfers between devices, swap_faces(): return (lax.ppermute(piece, axis, near), lax.ppermute(back, axis, across))  4.97 us
    pallas_call x1, Pallas kernels, per_device(): call(lambda *refs: tail_kernel(n_x - 1, *refs), shape((elems, width)), [V...  3.61 us
    ppermute x4, waiting for transfers between devices, swap_faces(): return (lax.ppermute(piece, axis, near), lax.ppermute(back, axis, across))  3.47 us
    ppermute x1, starting transfers between devices, per_device(): nearest = lax.ppermute(src_fields, 'gy', partner(n_y, 1))  3.12 us
    pallas_call x1, Pallas kernels, per_device(): call(lambda *refs: lead_kernel(n_y, n_x - 1, *refs), (shape((elems, 2 * N...  2.83 us
  transfers between devices with their start and end apart: 19, of which 5 were waited for; matrix products, arithmetic and copies ran while one was open for 0% of the time, Pallas kernels for 21%

profile of v2, /device:TPU:0, one launch (start us, length us, event | category | flops | bytes accessed | tf_op | source)
XLA Modules:
  0.0 47.9 jit_solution(14554952739659110043)
XLA Ops:
  0.6 3.1 %collective-permute-start = (f32[32,1080]{1,0:T(8,128)}, f32[32,1080]{1,0:T(8,128)S(1)}, u32[]{:S(2)}, u32[]{:S(2)}) collective-permute-start(f32[32,1080]{1,0:T(8,128)} %refs_0_.1), channel_id=1, source_target_pairs={{0,2},{2,0},{4,6},{6,4},{1,3},{3,1},{5,7},{7,5},{8,10},{10,8},{12,... | collective-permute-start | bytes 414728 | tf_op jit(solution)/shard_map/ppermute | solution.py:474
  3.7 1.3 %shard_map.77 = (f32[32,512]{1,0:T(8,128)S(1)}, f32[32,568]{1,0:T(8,128)S(1)}, s32[1,344]{1,0:T(1,128)S(1)}, s32[32,8]{1,0:T(8,128)S(1)}, f32[8,128]{1,0:T(8,128...) custom-call(f32[32,1080]{1,0:T(8,128)} %refs_0_.1, s32[8,32]{1,0:T(8,128)} %bitcast.4, s32[8,32]{1,0:T(8,128)} %bitcast.5), custom_call_target="tpu_custom_call" | custom-call | tf_op jit(solution)/shard_map/pallas_call | solution.py:477
  5.1 2.5 %collective-permute-start.2 = (f32[32,512]{1,0:T(8,128)S(1)}, f32[32,512]{1,0:T(8,128)S(1)}, u32[]{:S(2)}, u32[]{:S(2)}) collective-permute-start(f32[32,512]{1,0:T(8,128)S(1)} %get-tuple-element.40.refs_3_.refs_7_.refs_2_), channel_id=1, source_target_pairs={{0,6},{2,4},{4,2},{6,0},{1,7},{3,5},{5,3},{7,1},{8,14},{10,12},{12... | collective-permute-start | bytes 196616 | tf_op jit(solution)/shard_map/ppermute | solution.py:493
  7.6 0.2 collective-permute-start.1
  7.8 1.5 %collective-permute-start.3 = (f32[8,128]{1,0:T(8,128)S(1)}, f32[8,128]{1,0:T(8,128)S(1)}, u32[]{:S(2)}, u32[]{:S(2)}) collective-permute-start(f32[8,128]{1,0:T(8,128)S(1)} %get-tuple-element.41), channel_id=1, source_target_pairs={{0,8},{8,0},{16,24},{24,16},{1,9},{9,1},{17,25},{25,17},{2,10},{10... | collective-permute-start | bytes 12296 | tf_op jit(solution)/shard_map/ppermute | solution.py:500
  9.3 1.5 %collective-permute-start.4 = (f32[8,128]{1,0:T(8,128)S(1)}, f32[8,128]{1,0:T(8,128)S(1)}, u32[]{:S(2)}, u32[]{:S(2)}) collective-permute-start(f32[8,128]{1,0:T(8,128)S(1)} %get-tuple-element.42), channel_id=1, source_target_pairs={{0,16},{8,24},{16,0},{24,8},{1,17},{9,25},{17,1},{25,9},{2,18},{10... | collective-permute-start | bytes 12296 | tf_op jit(solution)/shard_map/ppermute | solution.py:500
  10.8 0.6 %collective-permute-done.3.refs_0_ = f32[8,128]{1,0:T(8,128)S(1)} collective-permute-done((f32[8,128]{1,0:T(8,128)S(1)}, f32[8,128]{1,0:T(8,128)S(1)}, u32[]{:S(2)}, u32[]{:S(2)}) %collective-permute-start.3) | collective-permute-done | bytes 4128 | tf_op jit(solution)/shard_map/ppermute | solution.py:500
  11.4 2.4 %collective-permute-start.5 = (f32[8,128]{1,0:T(8,128)S(1)}, f32[8,128]{1,0:T(8,128)S(1)}, u32[]{:S(2)}, u32[]{:S(2)}) collective-permute-start(f32[8,128]{1,0:T(8,128)S(1)} %get-tuple-element.43), channel_id=1, source_target_pairs={{0,24},{8,16},{16,8},{24,0},{1,25},{9,17},{17,9},{25,1},{2,26},{10... | collective-permute-start | bytes 12296 | tf_op jit(solution)/shard_map/ppermute | solution.py:500
  13.9 2.8 %collective-permute-start.12 = (f32[32,568]{1,0:T(8,128)S(1)}, f32[32,568]{1,0:T(8,128)S(1)}, u32[]{:S(2)}, u32[]{:S(2)}) collective-permute-start(f32[32,568]{1,0:T(8,128)S(1)} %get-tuple-element.50.refs_6_.refs_3_), channel_id=1, source_target_pairs={{0,6},{2,4},{4,2},{6,0},{1,7},{3,5},{5,3},{7,1},{8,14},{10,12},{12... | collective-permute-start | bytes 218120 | tf_op jit(solution)/shard_map/ppermute | solution.py:493
  16.7 1.9 %collective-permute-start.11 = (f32[32,568]{1,0:T(8,128)S(1)}, f32[32,568]{1,0:T(8,128)S(1)}, u32[]{:S(2)}, u32[]{:S(2)}) collective-permute-start(f32[32,568]{1,0:T(8,128)S(1)} %get-tuple-element.50.refs_6_.refs_3_), channel_id=1, source_target_pairs={{0,4},{2,6},{4,0},{6,2},{1,5},{3,7},{5,1},{7,3},{8,12},{10,14},{12... | collective-permute-start | bytes 218120 | tf_op jit(solution)/shard_map/ppermute | solution.py:493
  18.7 0.5 shard_map.79
  19.1 1.6 %collective-permute-start.6 = (f32[72,512]{1,0:T(8,128)S(1)}, f32[72,512]{1,0:T(8,128)S(1)}, u32[]{:S(2)}, u32[]{:S(2)}) collective-permute-start(f32[72,512]{1,0:T(8,128)S(1)} %get-tuple-element.44), channel_id=1, source_target_pairs={{0,8},{8,0},{16,24},{24,16},{1,9},{9,1},{17,25},{25,17},{2,10},{10... | collective-permute-start | bytes 442376 | tf_op jit(solution)/shard_map/ppermute | solution.py:510
  20.7 1.5 %collective-permute-start.7 = (f32[72,512]{1,0:T(8,128)S(1)}, f32[72,512]{1,0:T(8,128)S(1)}, u32[]{:S(2)}, u32[]{:S(2)}) collective-permute-start(f32[72,512]{1,0:T(8,128)S(1)} %get-tuple-element.45), channel_id=1, source_target_pairs={{0,16},{8,24},{16,0},{24,8},{1,17},{9,25},{17,1},{25,9},{2,18},{10... | collective-permute-start | bytes 442376 | tf_op jit(solution)/shard_map/ppermute | solution.py:510
  22.2 0.5 %collective-permute-start.8 = (f32[72,512]{1,0:T(8,128)S(1)}, f32[72,512]{1,0:T(8,128)S(1)}, u32[]{:S(2)}, u32[]{:S(2)}) collective-permute-start(f32[72,512]{1,0:T(8,128)S(1)} %get-tuple-element.46), channel_id=1, source_target_pairs={{0,24},{8,16},{16,8},{24,0},{1,25},{9,17},{17,9},{25,1},{2,26},{10... | collective-permute-start | bytes 442376 | tf_op jit(solution)/shard_map/ppermute | solution.py:510
  22.7 1.0 %shard_map.78 = (bf16[8,216,512]{2,1,0:T(8,128)(2,1)S(1)}, bf16[8,216,512]{2,1,0:T(8,128)(2,1)S(1)}) custom-call(), custom_call_target="tpu_custom_call" | custom-call | flops 2000000000 | bytes 8000000 | tf_op jit(solution)/shard_map/pallas_call | solution.py:499
  23.7 0.5 %shard_map.83 = (f32[72,568]{1,0:T(8,128)S(1)}, f32[72,568]{1,0:T(8,128)S(1)}, f32[72,568]{1,0:T(8,128)S(1)}) custom-call(f32[8,128]{1,0:T(8,128)S(1)} %collective-permute-done.3.refs_0_, f32[8,128]{1,0:T(8,128)S(1)} %collective-permute-done.4.refs_1_, f32[8,128]{1,0:T(8,128)S(1)} %collective-permute-done.5.refs_2_, ...), custom_call_target="tpu_custom_call" | custom-call | tf_op jit(solution)/shard_map/pallas_call | solution.py:504
  24.2 1.6 %collective-permute-start.15 = (f32[72,568]{1,0:T(8,128)S(1)}, f32[72,568]{1,0:T(8,128)S(1)}, u32[]{:S(2)}, u32[]{:S(2)}) collective-permute-start(f32[72,568]{1,0:T(8,128)S(1)} %get-tuple-element.61), channel_id=1, source_target_pairs={{0,8},{8,0},{16,24},{24,16},{1,9},{9,1},{17,25},{25,17},{2,10},{10... | collective-permute-start | bytes 490760 | tf_op jit(solution)/shard_map/ppermute | solution.py:510
  25.8 1.5 %collective-permute-start.16 = (f32[72,568]{1,0:T(8,128)S(1)}, f32[72,568]{1,0:T(8,128)S(1)}, u32[]{:S(2)}, u32[]{:S(2)}) collective-permute-start(f32[72,568]{1,0:T(8,128)S(1)} %get-tuple-element.62), channel_id=1, source_target_pairs={{0,16},{8,24},{16,0},{24,8},{1,17},{9,25},{17,1},{25,9},{2,18},{10... | collective-permute-start | bytes 490760 | tf_op jit(solution)/shard_map/ppermute | solution.py:510
  27.3 0.7 %collective-permute-start.17 = (f32[72,568]{1,0:T(8,128)S(1)}, f32[72,568]{1,0:T(8,128)S(1)}, u32[]{:S(2)}, u32[]{:S(2)}) collective-permute-start(f32[72,568]{1,0:T(8,128)S(1)} %get-tuple-element.63), channel_id=1, source_target_pairs={{0,24},{8,16},{16,8},{24,0},{1,25},{9,17},{17,9},{25,1},{2,26},{10... | collective-permute-start | bytes 490760 | tf_op jit(solution)/shard_map/ppermute | solution.py:510
  27.9 2.1 %collective-permute-done.7.refs_12_.refs_10_ = f32[72,512]{1,0:T(8,128)S(1)} collective-permute-done((f32[72,512]{1,0:T(8,128)S(1)}, f32[72,512]{1,0:T(8,128)S(1)}, u32[]{:S(2)}, u32[]{:S(2)}) %collective-permute-start.7) | collective-permute-done | bytes 147488 | tf_op jit(solution)/shard_map/ppermute | solution.py:510
  30.1 2.8 %shard_map.80 = (f32[32,432]{1,0:T(8,128)S(1)}, f32[32,216]{1,0:T(8,128)S(1)}, f32[32,1024]{1,0:T(8,128)S(1)}, f32[8,512]{1,0:T(8,128)S(1)}, f32[8,512]{1,0:T(8,128)S(1)}) custom-call(s32[1,344]{1,0:T(1,128)S(1)} %get-tuple-element.36.refs_0_, s32[32,8]{1,0:T(8,128)S(1)} %get-tuple-element.37.refs_1_, f32[32,4096]{1,0:T(8,128)S(1)} %copy-done, ...), custom_call_target="tpu_custom_call" | custom-call | tf_op jit(solution)/shard_map/pallas_call | solution.py:517
  32.9 1.2 %collective-permute-start.9 = (f32[8,512]{1,0:T(8,128)S(1)}, f32[8,512]{1,0:T(8,128)S(1)}, u32[]{:S(2)}, u32[]{:S(2)}) collective-permute-start(f32[8,512]{1,0:T(8,128)S(1)} %get-tuple-element.48), channel_id=1, source_target_pairs={{0,8},{8,0},{16,24},{24,16},{1,9},{9,1},{17,25},{25,17},{2,10},{10... | collective-permute-start | bytes 49160 | tf_op jit(solution)/shard_map/ppermute | solution.py:463
  34.1 2.6 %collective-permute-start.10 = (f32[8,512]{1,0:T(8,128)S(1)}, f32[8,512]{1,0:T(8,128)S(1)}, u32[]{:S(2)}, u32[]{:S(2)}) collective-permute-start(f32[8,512]{1,0:T(8,128)S(1)} %get-tuple-element.49), channel_id=1, source_target_pairs={{0,24},{8,16},{16,8},{24,0},{1,25},{9,17},{17,9},{25,1},{2,26},{10... | collective-permute-start | bytes 49160 | tf_op jit(solution)/shard_map/ppermute | solution.py:463
  36.7 0.4 shard_map.81
  37.1 1.6 %collective-permute-done.10.turn_ref = f32[8,512]{1,0:T(8,128)S(1)} collective-permute-done((f32[8,512]{1,0:T(8,128)S(1)}, f32[8,512]{1,0:T(8,128)S(1)}, u32[]{:S(2)}, u32[]{:S(2)}) %collective-permute-start.10) | collective-permute-done | bytes 16416 | tf_op jit(solution)/shard_map/ppermute | solution.py:463
  38.7 0.1 shard_map.82
  38.9 1.2 %collective-permute-start.13 = (f32[8,512]{1,0:T(8,128)S(1)}, f32[8,512]{1,0:T(8,128)S(1)}, u32[]{:S(2)}, u32[]{:S(2)}) collective-permute-start(f32[8,512]{1,0:T(8,128)S(1)} %get-tuple-element.55), channel_id=1, source_target_pairs={{0,2},{2,0},{4,6},{6,4},{1,3},{3,1},{5,7},{7,5},{8,10},{10,8},{12,... | collective-permute-start | bytes 49160 | tf_op jit(solution)/shard_map/ppermute | solution.py:463
  40.1 3.6 %shard_map.84 = f32[32,1080]{1,0:T(8,128)} custom-call(s32[1,344]{1,0:T(1,128)S(1)} %get-tuple-element.36.refs_0_, s32[32,8]{1,0:T(8,128)S(1)} %get-tuple-element.37.refs_1_, f32[32,4096]{1,0:T(8,128)S(1)} %copy-done, bf16[8,216,512]{2,1,0:T(8,128)(2,1)S(1)} %get-tuple-element.38.refs_3_, bf16[8,216,512]{2,1,0:T(8,128)(2,1)S(1)} %get-tuple-element.39.refs_4_, ...), custom_call_target="tpu_custom_call" | custom-call | flops 2000000000 | bytes 8000000 | tf_op jit(solution)/shard_map/pallas_call | solution.py:537
  43.7 1.8 %collective-permute-done.14.turn_ref = f32[8,512]{1,0:T(8,128)S(1)} collective-permute-done((f32[8,512]{1,0:T(8,128)S(1)}, f32[8,512]{1,0:T(8,128)S(1)}, u32[]{:S(2)}, u32[]{:S(2)}) %collective-permute-start.14) | collective-permute-done | bytes 16416 | tf_op jit(solution)/shard_map/ppermute | solution.py:463
  45.6 0.1 shard_map.85
  45.8 1.2 %collective-permute-done.18.before_ref.after_ref = f32[32,512]{1,0:T(8,128)S(1)} collective-permute-done((f32[32,512]{1,0:T(8,128)S(1)}, f32[32,512]{1,0:T(8,128)S(1)}, u32[]{:S(2)}, u32[]{:S(2)}) %collective-permute-start.18) | collective-permute-done | bytes 65568 | tf_op jit(solution)/shard_map/ppermute | solution.py:548
  47.0 0.8 %shard_map.86 = f32[32,648]{1,0:T(8,128)} custom-call(f32[32,1024]{1,0:T(8,128)S(1)} %get-tuple-element.68.parts_ref, f32[32,512]{1,0:T(8,128)S(1)} %collective-permute-done.18.before_ref.after_ref, f32[32,512]{1,0:T(8,128)S(1)} %collective-permute-done.18.before_ref.after_ref), custom_call_target="tpu_custom_call" | custom-call | tf_op jit(solution)/shard_map/pallas_call | solution.py:552
  (22 shorter events, 0.2 us)
Async XLA Ops:
  0.6 18.1 %collective-permute-start = (f32[32,1080]{1,0:T(8,128)}, f32[32,1080]{1,0:T(8,128)S(1)}, u32[]{:S(2)}, u32[]{:S(2)}) collective-permute-start(f32[32,1080]{1,0:T(8,128)} %refs_0_.1), channel_id=1, source_target_pairs={{0,2},{2,0},{4,6},{6,4},{1,3},{3,1},{5,7},{7,5},{8,10},{10,8},{12,... | collective-permute-start | bytes 414728 | tf_op jit(solution)/shard_map/ppermute | solution.py:474
  5.1 13.6 %collective-permute-start.2 = (f32[32,512]{1,0:T(8,128)S(1)}, f32[32,512]{1,0:T(8,128)S(1)}, u32[]{:S(2)}, u32[]{:S(2)}) collective-permute-start(f32[32,512]{1,0:T(8,128)S(1)} %get-tuple-element.40.refs_3_.refs_7_.refs_2_), channel_id=1, source_target_pairs={{0,6},{2,4},{4,2},{6,0},{1,7},{3,5},{5,3},{7,1},{8,14},{10,12},{12... | collective-permute-start | bytes 196616 | tf_op jit(solution)/shard_map/ppermute | solution.py:493
  7.6 11.0 %collective-permute-start.1 = (f32[32,512]{1,0:T(8,128)S(1)}, f32[32,512]{1,0:T(8,128)S(1)}, u32[]{:S(2)}, u32[]{:S(2)}) collective-permute-start(f32[32,512]{1,0:T(8,128)S(1)} %get-tuple-element.40.refs_3_.refs_7_.refs_2_), channel_id=1, source_target_pairs={{0,4},{2,6},{4,0},{6,2},{1,5},{3,7},{5,1},{7,3},{8,12},{10,14},{12... | collective-permute-start | bytes 196616 | tf_op jit(solution)/shard_map/ppermute | solution.py:493
  7.8 3.6 %collective-permute-start.3 = (f32[8,128]{1,0:T(8,128)S(1)}, f32[8,128]{1,0:T(8,128)S(1)}, u32[]{:S(2)}, u32[]{:S(2)}) collective-permute-start(f32[8,128]{1,0:T(8,128)S(1)} %get-tuple-element.41), channel_id=1, source_target_pairs={{0,8},{8,0},{16,24},{24,16},{1,9},{9,1},{17,25},{25,17},{2,10},{10... | collective-permute-start | bytes 12296 | tf_op jit(solution)/shard_map/ppermute | solution.py:500
  9.3 4.6 %collective-permute-start.4 = (f32[8,128]{1,0:T(8,128)S(1)}, f32[8,128]{1,0:T(8,128)S(1)}, u32[]{:S(2)}, u32[]{:S(2)}) collective-permute-start(f32[8,128]{1,0:T(8,128)S(1)} %get-tuple-element.42), channel_id=1, source_target_pairs={{0,16},{8,24},{16,0},{24,8},{1,17},{9,25},{17,1},{25,9},{2,18},{10... | collective-permute-start | bytes 12296 | tf_op jit(solution)/shard_map/ppermute | solution.py:500
  11.4 5.3 %collective-permute-start.5 = (f32[8,128]{1,0:T(8,128)S(1)}, f32[8,128]{1,0:T(8,128)S(1)}, u32[]{:S(2)}, u32[]{:S(2)}) collective-permute-start(f32[8,128]{1,0:T(8,128)S(1)} %get-tuple-element.43), channel_id=1, source_target_pairs={{0,24},{8,16},{16,8},{24,0},{1,25},{9,17},{17,9},{25,1},{2,26},{10... | collective-permute-start | bytes 12296 | tf_op jit(solution)/shard_map/ppermute | solution.py:500
  13.9 9.8 %collective-permute-start.12 = (f32[32,568]{1,0:T(8,128)S(1)}, f32[32,568]{1,0:T(8,128)S(1)}, u32[]{:S(2)}, u32[]{:S(2)}) collective-permute-start(f32[32,568]{1,0:T(8,128)S(1)} %get-tuple-element.50.refs_6_.refs_3_), channel_id=1, source_target_pairs={{0,6},{2,4},{4,2},{6,0},{1,7},{3,5},{5,3},{7,1},{8,14},{10,12},{12... | collective-permute-start | bytes 218120 | tf_op jit(solution)/shard_map/ppermute | solution.py:493
  16.7 7.0 %collective-permute-start.11 = (f32[32,568]{1,0:T(8,128)S(1)}, f32[32,568]{1,0:T(8,128)S(1)}, u32[]{:S(2)}, u32[]{:S(2)}) collective-permute-start(f32[32,568]{1,0:T(8,128)S(1)} %get-tuple-element.50.refs_6_.refs_3_), channel_id=1, source_target_pairs={{0,4},{2,6},{4,0},{6,2},{1,5},{3,7},{5,1},{7,3},{8,12},{10,14},{12... | collective-permute-start | bytes 218120 | tf_op jit(solution)/shard_map/ppermute | solution.py:493
  19.1 8.1 %collective-permute-start.6 = (f32[72,512]{1,0:T(8,128)S(1)}, f32[72,512]{1,0:T(8,128)S(1)}, u32[]{:S(2)}, u32[]{:S(2)}) collective-permute-start(f32[72,512]{1,0:T(8,128)S(1)} %get-tuple-element.44), channel_id=1, source_target_pairs={{0,8},{8,0},{16,24},{24,16},{1,9},{9,1},{17,25},{25,17},{2,10},{10... | collective-permute-start | bytes 442376 | tf_op jit(solution)/shard_map/ppermute | solution.py:510
  20.7 9.4 %collective-permute-start.7 = (f32[72,512]{1,0:T(8,128)S(1)}, f32[72,512]{1,0:T(8,128)S(1)}, u32[]{:S(2)}, u32[]{:S(2)}) collective-permute-start(f32[72,512]{1,0:T(8,128)S(1)} %get-tuple-element.45), channel_id=1, source_target_pairs={{0,16},{8,24},{16,0},{24,8},{1,17},{9,25},{17,1},{25,9},{2,18},{10... | collective-permute-start | bytes 442376 | tf_op jit(solution)/shard_map/ppermute | solution.py:510
  22.2 7.9 %copy-start = (f32[32,4096]{1,0:T(8,128)S(1)}, f32[32,4096]{1,0:T(8,128)}, u32[]{:S(2)}) copy-start(f32[32,4096]{1,0:T(8,128)} %refs_2_.3) | copy-start | bytes 1572868
  22.2 7.9 %copy-start.1 = (bf16[216,768]{1,0:T(8,128)(2,1)S(1)}, bf16[216,768]{1,0:T(8,128)(2,1)}, u32[]{:S(2)}) copy-start(bf16[216,768]{1,0:T(8,128)(2,1)} %constant.5.clone.refs_6_) | copy-start | bytes 995332
  22.2 7.9 %copy-start.2 = (bf16[216,768]{1,0:T(8,128)(2,1)S(1)}, bf16[216,768]{1,0:T(8,128)(2,1)}, u32[]{:S(2)}) copy-start(bf16[216,768]{1,0:T(8,128)(2,1)} %constant.4.clone.refs_5_) | copy-start | bytes 995332
  22.2 7.9 %collective-permute-start.8 = (f32[72,512]{1,0:T(8,128)S(1)}, f32[72,512]{1,0:T(8,128)S(1)}, u32[]{:S(2)}, u32[]{:S(2)}) collective-permute-start(f32[72,512]{1,0:T(8,128)S(1)} %get-tuple-element.46), channel_id=1, source_target_pairs={{0,24},{8,16},{16,8},{24,0},{1,25},{9,17},{17,9},{25,1},{2,26},{10... | collective-permute-start | bytes 442376 | tf_op jit(solution)/shard_map/ppermute | solution.py:510
  24.2 15.9 %collective-permute-start.15 = (f32[72,568]{1,0:T(8,128)S(1)}, f32[72,568]{1,0:T(8,128)S(1)}, u32[]{:S(2)}, u32[]{:S(2)}) collective-permute-start(f32[72,568]{1,0:T(8,128)S(1)} %get-tuple-element.61), channel_id=1, source_target_pairs={{0,8},{8,0},{16,24},{24,16},{1,9},{9,1},{17,25},{25,17},{2,10},{10... | collective-permute-start | bytes 490760 | tf_op jit(solution)/shard_map/ppermute | solution.py:510
  25.8 14.4 %collective-permute-start.16 = (f32[72,568]{1,0:T(8,128)S(1)}, f32[72,568]{1,0:T(8,128)S(1)}, u32[]{:S(2)}, u32[]{:S(2)}) collective-permute-start(f32[72,568]{1,0:T(8,128)S(1)} %get-tuple-element.62), channel_id=1, source_target_pairs={{0,16},{8,24},{16,0},{24,8},{1,17},{9,25},{17,1},{25,9},{2,18},{10... | collective-permute-start | bytes 490760 | tf_op jit(solution)/shard_map/ppermute | solution.py:510
  27.3 12.8 %collective-permute-start.17 = (f32[72,568]{1,0:T(8,128)S(1)}, f32[72,568]{1,0:T(8,128)S(1)}, u32[]{:S(2)}, u32[]{:S(2)}) collective-permute-start(f32[72,568]{1,0:T(8,128)S(1)} %get-tuple-element.63), channel_id=1, source_target_pairs={{0,24},{8,16},{16,8},{24,0},{1,25},{9,17},{17,9},{25,1},{2,26},{10... | collective-permute-start | bytes 490760 | tf_op jit(solution)/shard_map/ppermute | solution.py:510
  32.9 4.2 %collective-permute-start.9 = (f32[8,512]{1,0:T(8,128)S(1)}, f32[8,512]{1,0:T(8,128)S(1)}, u32[]{:S(2)}, u32[]{:S(2)}) collective-permute-start(f32[8,512]{1,0:T(8,128)S(1)} %get-tuple-element.48), channel_id=1, source_target_pairs={{0,8},{8,0},{16,24},{24,16},{1,9},{9,1},{17,25},{25,17},{2,10},{10... | collective-permute-start | bytes 49160 | tf_op jit(solution)/shard_map/ppermute | solution.py:463
  34.1 4.6 %collective-permute-start.10 = (f32[8,512]{1,0:T(8,128)S(1)}, f32[8,512]{1,0:T(8,128)S(1)}, u32[]{:S(2)}, u32[]{:S(2)}) collective-permute-start(f32[8,512]{1,0:T(8,128)S(1)} %get-tuple-element.49), channel_id=1, source_target_pairs={{0,24},{8,16},{16,8},{24,0},{1,25},{9,17},{17,9},{25,1},{2,26},{10... | collective-permute-start | bytes 49160 | tf_op jit(solution)/shard_map/ppermute | solution.py:463
  38.9 4.9 %collective-permute-start.13 = (f32[8,512]{1,0:T(8,128)S(1)}, f32[8,512]{1,0:T(8,128)S(1)}, u32[]{:S(2)}, u32[]{:S(2)}) collective-permute-start(f32[8,512]{1,0:T(8,128)S(1)} %get-tuple-element.55), channel_id=1, source_target_pairs={{0,2},{2,0},{4,6},{6,4},{1,3},{3,1},{5,7},{7,5},{8,10},{10,8},{12,... | collective-permute-start | bytes 49160 | tf_op jit(solution)/shard_map/ppermute | solution.py:463
  40.0 5.5 %collective-permute-start.14 = (f32[8,512]{1,0:T(8,128)S(1)}, f32[8,512]{1,0:T(8,128)S(1)}, u32[]{:S(2)}, u32[]{:S(2)}) collective-permute-start(f32[8,512]{1,0:T(8,128)S(1)} %get-tuple-element.56), channel_id=1, source_target_pairs={{0,6},{2,4},{4,2},{6,0},{1,7},{3,5},{5,3},{7,1},{8,14},{10,12},{12... | collective-permute-start | bytes 49160 | tf_op jit(solution)/shard_map/ppermute | solution.py:463
  45.7 1.3 %collective-permute-start.18 = (f32[32,512]{1,0:T(8,128)S(1)}, f32[32,512]{1,0:T(8,128)S(1)}, u32[]{:S(2)}, u32[]{:S(2)}) collective-permute-start(f32[32,512]{1,0:T(8,128)S(1)} %get-tuple-element.69), channel_id=1, source_target_pairs={{0,1},{1,0},{2,3},{3,2},{4,5},{5,4},{6,7},{7,6},{8,9},{9,8},{10,11... | collective-permute-start | bytes 196616 | tf_op jit(solution)/shard_map/ppermute | solution.py:548

commit v3 on v1

--- a/solution.py
+++ b/solution.py
@@ -204,7 +204,7 @@
     return jnp.where(row + col // 36 * 72 == col + 180, 1.0, 0.0).astype(BF)
 
 
-def project(offset, picked, jac_ref, high_ref, low_ref, extra):
+def project(pairs, offset, picked, jac_ref, high_ref, low_ref, extra):
     elems = jac_ref.shape[0]
     count = (picked[0].shape[1] - offset) // NB
     half = OVL // 2
@@ -221,15 +221,16 @@
             ref[at, offset + f * NB : offset + (f + 1) * NB].astype(BF) for f in range(count)
         ]
 
-    turned = jnp.concatenate([x for ref in picked for x in fields_of(ref, 0, half)], 0)
+    size = len(pairs)
+    turned = jnp.concatenate([x for ref in picked for x in fields_of(ref, 0, size)], 0)
     turned = dot(turned, flip).astype(BF)
     total = None
-    for n in range(half):
+    for spot, n in enumerate(pairs):
         source = []
         for m, ref in enumerate(picked):
-            rows = fields_of(ref, half + n, half + n + 1)
+            rows = fields_of(ref, size + spot, size + spot + 1)
             for f in range(count):
-                base = ((m * count + f) * half + n) * elems
+                base = ((m * count + f) * size + spot) * elems
                 rows.append(turned[base : base + elems])
             source.append(jnp.concatenate(rows, 0))
         values = apply(source, half + n)
@@ -299,7 +300,7 @@
     hot = jnp.concatenate(hits(index_ref, ids_ref[...], range(OVL)), 0).astype(BF)
     rows = lanes_of((*column, *packed), NB * FIELDS, 0)
     pick(hot, jnp.concatenate(rows, 0), picked)
-    total = project(0, picked, jac_ref, high_ref, low_ref, True)
+    total = project(range(OVL // 2), 0, picked, jac_ref, high_ref, low_ref, True)
     lumped = total[2 * elems :]
     lumped_ref[...] = lumped
     fields = [total[f * elems : (f + 1) * elems] / lumped for f in range(2)]
@@ -315,12 +316,17 @@
     send_faces(even, parts[:width], parts[-width:], 36, send_ref, back_ref)
 
 
-def tail_kernel(count, ids_ref, index_ref, jac_ref, high_ref, low_ref, lumped_ref, lead_ref, *refs):
+def tail_kernel(count, pairs, ids_ref, index_ref, jac_ref, high_ref, low_ref, *refs):
     near, far = refs[:count], refs[count : 2 * count]
-    out_ref, *picked = refs[2 * count :]
+    refs = refs[2 * count :]
+    first = pairs[0] == 0
+    if not first:
+        sum_ref, lumped_ref, lead_ref, *refs = refs
+    out_ref, *picked = refs
     elems = jac_ref.shape[0]
     start = CUT - 128
-    hot = jnp.concatenate(hits(index_ref, ids_ref[...], range(OVL)), 0).astype(BF)
+    spans = [*pairs, *[OVL // 2 + n for n in pairs]]
+    hot = jnp.concatenate(hits(index_ref, ids_ref[...], spans), 0).astype(BF)
     rows = []
     for a, b in zip(near, far):
         if a.shape[1] == NB * FIELDS:
@@ -328,7 +334,11 @@
         else:
             rows.append(jnp.concatenate([a[:, start:], b[...]], 1))
     pick(hot, jnp.concatenate(rows, 0), picked)
-    total = project(2 * NB - start, picked, jac_ref, high_ref, low_ref, False)
+    total = project(pairs, 2 * NB - start, picked, jac_ref, high_ref, low_ref, False)
+    if first:
+        out_ref[...] = total
+        return
+    total = total + sum_ref[...]
     lumped = lumped_ref[...]
     out_ref[:, : 2 * NB] = lead_ref[...]
     for f in range(3):
@@ -501,17 +511,25 @@
         [pltpu.VMEM((OVL * elems, CUT), F32)] * 2,
     )(ids, index, jac, high, low, fhigh, flow, *near)
     got, turn = swap_faces(piece, back, "gx", n_x)
+    pairs = range(OVL // 2)
+    split_at = OVL // 4
+
+    def tail(pairs, out, *more):
+        scratch = pltpu.VMEM((2 * len(pairs) * elems, width - CUT + 128), F32)
+        return call(
+            lambda *refs: tail_kernel(len(near), pairs, *refs),
+            out,
+            [VM] * (5 + 2 * len(near) + len(more)),
+            [scratch] * 2,
+            heavy,
+        )(ids, index, jac, high, low, *near, *far, *more)
+
+    partial = tail(pairs[:split_at], shape(((FIELDS - 2) * elems, NB)))
+    got, turn, partial = lax.optimization_barrier((got, turn, partial))
     face = shape((EX * EZ, 2 * PAD))
     parts, piece, back = call(x_kernel, (whole, face, face), [VM] * 3)(parts, got, turn)
     got, turn = swap_faces(piece, back, "gy", n_y)
-    scratch = pltpu.VMEM((OVL * elems, width - CUT + 128), F32)
-    fields = call(
-        lambda *refs: tail_kernel(len(near), *refs),
-        shape((elems, width)),
-        [VM] * (7 + 2 * len(near)),
-        [scratch] * 2,
-        heavy,
-    )(ids, index, jac, high, low, lumped, lead, *near, *far)
+    fields = tail(pairs[split_at:], shape((elems, width)), partial, lumped, lead)
     got, turn, fields = lax.optimization_barrier((got, turn, fields))
     ends = (shape((elems, 2 * PAD)),) * (1 if n_z == 2 else 2)
     parts, *ends = call(y_kernel, (whole, *ends), [VM] * 3)(parts, got, turn)

time: 50 us -> 49.5 us (0.990)
  waiting for transfers between devices: 9.89 us -> 8.44 us
  Pallas kernels: 10.9 us -> 11.8 us
    ppermute x4, waiting for transfers between devices: 2.2 us -> 0.75 us  [swap_faces(): return (lax.ppermute(piece, axis, near), lax.ppermute(back, axis, across))]
    pallas_call x1 -> x2, Pallas kernels: 3.72 us -> 4.67 us  [tail(): call(lambda *refs: tail_kernel(len(near), pairs, *refs), out, [VM] * (5 +...]
  transfers between devices with their start and end apart: 19 -> 19, of which waited for: 7 -> 7; matrix products, arithmetic and copies ran while one was open for 0% -> 0% of each run, Pallas kernels for 19% -> 21%
where the time goes in v3:
time: 49.5 us; the launch traced here: 49.3 us
  starting transfers between devices  28.3 us (57%)
  Pallas kernels  11.8 us (24%)
  waiting for transfers between devices  8.44 us (17%)
  between operations  0.77 us (2%)
    ppermute x6, starting transfers between devices, per_device(): lax.ppermute(piece, 'gx', partner(n_x, step + 1))  7.18 us
    ppermute x4, starting transfers between devices, swap_faces(): return (lax.ppermute(piece, axis, near), lax.ppermute(back, axis, across))  6.52 us
    ppermute x4, starting transfers between devices, per_device(): lax.ppermute(piece, 'gy', partner(n_y, step))  5.9 us
    ppermute x3, starting transfers between devices, per_device(): lax.ppermute(mask, 'gx', partner(n_x, step + 1))  5.46 us
    pallas_call x2, Pallas kernels, tail(): call(lambda *refs: tail_kernel(len(near), pairs, *refs), out, [VM] * (5 +...  4.67 us
    ppermute x4, waiting for transfers between devices, per_device(): lax.ppermute(piece, 'gy', partner(n_y, step))  3.77 us
    ppermute x1, starting transfers between devices, per_device(): nearest = lax.ppermute(src_fields, 'gy', partner(n_y, 1))  3.12 us
    pallas_call x1, Pallas kernels, per_device(): call(lambda *refs: lead_kernel(n_y, n_x - 1, *refs), (shape((elems, 2 * N...  2.8 us
  transfers between devices with their start and end apart: 19, of which 7 were waited for; matrix products, arithmetic and copies ran while one was open for 0% of the time, Pallas kernels for 21%

profile of v3, /device:TPU:0, one launch (start us, length us, event | category | flops | bytes accessed | tf_op | source)
XLA Modules:
  0.0 49.3 jit_solution(7083985279082810127)
XLA Ops:
  0.6 3.1 %collective-permute-start = (f32[32,1080]{1,0:T(8,128)}, f32[32,1080]{1,0:T(8,128)S(1)}, u32[]{:S(2)}, u32[]{:S(2)}) collective-permute-start(f32[32,1080]{1,0:T(8,128)} %refs_0_.1), channel_id=1, source_target_pairs={{0,2},{2,0},{4,6},{6,4},{1,3},{3,1},{5,7},{7,5},{8,10},{10,8},{12,... | collective-permute-start | bytes 414728 | tf_op jit(solution)/shard_map/ppermute | solution.py:464
  3.7 1.3 %shard_map.77 = (f32[32,512]{1,0:T(8,128)S(1)}, f32[32,568]{1,0:T(8,128)S(1)}, s32[1,344]{1,0:T(1,128)S(1)}, s32[32,8]{1,0:T(8,128)S(1)}, f32[8,128]{1,0:T(8,128...) custom-call(f32[32,1080]{1,0:T(8,128)} %refs_0_.1, s32[8,32]{1,0:T(8,128)} %bitcast.4, s32[8,32]{1,0:T(8,128)} %bitcast.5), custom_call_target="tpu_custom_call" | custom-call | tf_op jit(solution)/shard_map/pallas_call | solution.py:467
  5.1 2.5 %collective-permute-start.2 = (f32[32,512]{1,0:T(8,128)S(1)}, f32[32,512]{1,0:T(8,128)S(1)}, u32[]{:S(2)}, u32[]{:S(2)}) collective-permute-start(f32[32,512]{1,0:T(8,128)S(1)} %get-tuple-element.37.refs_3_.refs_7_.refs_5_), channel_id=1, source_target_pairs={{0,6},{2,4},{4,2},{6,0},{1,7},{3,5},{5,3},{7,1},{8,14},{10,12},{12... | collective-permute-start | bytes 196616 | tf_op jit(solution)/shard_map/ppermute | solution.py:483
  7.8 1.5 %collective-permute-start.3 = (f32[8,128]{1,0:T(8,128)S(1)}, f32[8,128]{1,0:T(8,128)S(1)}, u32[]{:S(2)}, u32[]{:S(2)}) collective-permute-start(f32[8,128]{1,0:T(8,128)S(1)} %get-tuple-element.38), channel_id=1, source_target_pairs={{0,8},{8,0},{16,24},{24,16},{1,9},{9,1},{17,25},{25,17},{2,10},{10... | collective-permute-start | bytes 12296 | tf_op jit(solution)/shard_map/ppermute | solution.py:490
  9.3 1.5 %collective-permute-start.4 = (f32[8,128]{1,0:T(8,128)S(1)}, f32[8,128]{1,0:T(8,128)S(1)}, u32[]{:S(2)}, u32[]{:S(2)}) collective-permute-start(f32[8,128]{1,0:T(8,128)S(1)} %get-tuple-element.39), channel_id=1, source_target_pairs={{0,16},{8,24},{16,0},{24,8},{1,17},{9,25},{17,1},{25,9},{2,18},{10... | collective-permute-start | bytes 12296 | tf_op jit(solution)/shard_map/ppermute | solution.py:490
  10.8 0.6 %collective-permute-done.3.refs_0_ = f32[8,128]{1,0:T(8,128)S(1)} collective-permute-done((f32[8,128]{1,0:T(8,128)S(1)}, f32[8,128]{1,0:T(8,128)S(1)}, u32[]{:S(2)}, u32[]{:S(2)}) %collective-permute-start.3) | collective-permute-done | bytes 4128 | tf_op jit(solution)/shard_map/ppermute | solution.py:490
  11.4 2.4 %collective-permute-start.5 = (f32[8,128]{1,0:T(8,128)S(1)}, f32[8,128]{1,0:T(8,128)S(1)}, u32[]{:S(2)}, u32[]{:S(2)}) collective-permute-start(f32[8,128]{1,0:T(8,128)S(1)} %get-tuple-element.40), channel_id=1, source_target_pairs={{0,24},{8,16},{16,8},{24,0},{1,25},{9,17},{17,9},{25,1},{2,26},{10... | collective-permute-start | bytes 12296 | tf_op jit(solution)/shard_map/ppermute | solution.py:490
  13.9 2.1 %collective-permute-done.5.refs_2_ = f32[8,128]{1,0:T(8,128)S(1)} collective-permute-done((f32[8,128]{1,0:T(8,128)S(1)}, f32[8,128]{1,0:T(8,128)S(1)}, u32[]{:S(2)}, u32[]{:S(2)}) %collective-permute-start.5) | collective-permute-done | bytes 4128 | tf_op jit(solution)/shard_map/ppermute | solution.py:490
  16.0 0.4 shard_map.79
  16.4 1.6 %collective-permute-start.6 = (f32[72,512]{1,0:T(8,128)S(1)}, f32[72,512]{1,0:T(8,128)S(1)}, u32[]{:S(2)}, u32[]{:S(2)}) collective-permute-start(f32[72,512]{1,0:T(8,128)S(1)} %get-tuple-element.41), channel_id=1, source_target_pairs={{0,8},{8,0},{16,24},{24,16},{1,9},{9,1},{17,25},{25,17},{2,10},{10... | collective-permute-start | bytes 442376 | tf_op jit(solution)/shard_map/ppermute | solution.py:500
  18.0 2.8 %collective-permute-start.12 = (f32[32,568]{1,0:T(8,128)S(1)}, f32[32,568]{1,0:T(8,128)S(1)}, u32[]{:S(2)}, u32[]{:S(2)}) collective-permute-start(f32[32,568]{1,0:T(8,128)S(1)} %get-tuple-element.47.refs_3_.refs_12_), channel_id=1, source_target_pairs={{0,6},{2,4},{4,2},{6,0},{1,7},{3,5},{5,3},{7,1},{8,14},{10,12},{12... | collective-permute-start | bytes 218120 | tf_op jit(solution)/shard_map/ppermute | solution.py:483
  20.8 0.3 collective-permute-start.11
  21.1 1.5 %collective-permute-start.7 = (f32[72,512]{1,0:T(8,128)S(1)}, f32[72,512]{1,0:T(8,128)S(1)}, u32[]{:S(2)}, u32[]{:S(2)}) collective-permute-start(f32[72,512]{1,0:T(8,128)S(1)} %get-tuple-element.42), channel_id=1, source_target_pairs={{0,16},{8,24},{16,0},{24,8},{1,17},{9,25},{17,1},{25,9},{2,18},{10... | collective-permute-start | bytes 442376 | tf_op jit(solution)/shard_map/ppermute | solution.py:500
  22.7 0.5 collective-permute-start.8
  23.1 1.2 %collective-permute-done.12.refs_6_.refs_15_ = f32[32,568]{1,0:T(8,128)S(1)} collective-permute-done((f32[32,568]{1,0:T(8,128)S(1)}, f32[32,568]{1,0:T(8,128)S(1)}, u32[]{:S(2)}, u32[]{:S(2)}) %collective-permute-start.12) | collective-permute-done | bytes 72736 | tf_op jit(solution)/shard_map/ppermute | solution.py:483
  24.3 2.6 %collective-permute-done.11.refs_5_.refs_14_ = f32[32,568]{1,0:T(8,128)S(1)} collective-permute-done((f32[32,568]{1,0:T(8,128)S(1)}, f32[32,568]{1,0:T(8,128)S(1)}, u32[]{:S(2)}, u32[]{:S(2)}) %collective-permute-start.11) | collective-permute-done | bytes 72736 | tf_op jit(solution)/shard_map/ppermute | solution.py:483
  26.9 0.5 %shard_map.81 = (f32[72,568]{1,0:T(8,128)S(1)}, f32[72,568]{1,0:T(8,128)S(1)}, f32[72,568]{1,0:T(8,128)S(1)}) custom-call(f32[8,128]{1,0:T(8,128)S(1)} %collective-permute-done.3.refs_0_, f32[8,128]{1,0:T(8,128)S(1)} %collective-permute-done.4.refs_1_, f32[8,128]{1,0:T(8,128)S(1)} %collective-permute-done.5.refs_2_, ...), custom_call_target="tpu_custom_call" | custom-call | tf_op jit(solution)/shard_map/pallas_call | solution.py:494
  27.4 0.6 %collective-permute-start.13 = (f32[72,568]{1,0:T(8,128)S(1)}, f32[72,568]{1,0:T(8,128)S(1)}, u32[]{:S(2)}, u32[]{:S(2)}) collective-permute-start(f32[72,568]{1,0:T(8,128)S(1)} %get-tuple-element.48), channel_id=1, source_target_pairs={{0,8},{8,0},{16,24},{24,16},{1,9},{9,1},{17,25},{25,17},{2,10},{10... | collective-permute-start | bytes 490760 | tf_op jit(solution)/shard_map/ppermute | solution.py:500
  28.0 1.5 %collective-permute-start.14 = (f32[72,568]{1,0:T(8,128)S(1)}, f32[72,568]{1,0:T(8,128)S(1)}, u32[]{:S(2)}, u32[]{:S(2)}) collective-permute-start(f32[72,568]{1,0:T(8,128)S(1)} %get-tuple-element.49), channel_id=1, source_target_pairs={{0,16},{8,24},{16,0},{24,8},{1,17},{9,25},{17,1},{25,9},{2,18},{10... | collective-permute-start | bytes 490760 | tf_op jit(solution)/shard_map/ppermute | solution.py:500
  29.6 1.5 %collective-permute-start.15 = (f32[72,568]{1,0:T(8,128)S(1)}, f32[72,568]{1,0:T(8,128)S(1)}, u32[]{:S(2)}, u32[]{:S(2)}) collective-permute-start(f32[72,568]{1,0:T(8,128)S(1)} %get-tuple-element.50), channel_id=1, source_target_pairs={{0,24},{8,16},{16,8},{24,0},{1,25},{9,17},{17,9},{25,1},{2,26},{10... | collective-permute-start | bytes 490760 | tf_op jit(solution)/shard_map/ppermute | solution.py:500
  31.1 1.0 %shard_map.78 = (bf16[8,216,512]{2,1,0:T(8,128)(2,1)S(1)}, bf16[8,216,512]{2,1,0:T(8,128)(2,1)S(1)}) custom-call(), custom_call_target="tpu_custom_call" | custom-call | flops 2000000000 | bytes 8000000 | tf_op jit(solution)/shard_map/pallas_call | solution.py:489
  32.1 2.8 %shard_map.80 = (f32[32,432]{1,0:T(8,128)S(1)}, f32[32,216]{1,0:T(8,128)S(1)}, f32[32,1024]{1,0:T(8,128)S(1)}, f32[8,512]{1,0:T(8,128)S(1)}, f32[8,512]{1,0:T(8,128)S(1)}) custom-call(s32[1,344]{1,0:T(1,128)S(1)} %get-tuple-element.33.refs_0_, s32[32,8]{1,0:T(8,128)S(1)} %get-tuple-element.34.refs_1_, f32[32,4096]{1,0:T(8,128)S(1)} %copy-done, ...), custom_call_target="tpu_custom_call" | custom-call | tf_op jit(solution)/shard_map/pallas_call | solution.py:507
  34.9 0.6 %collective-permute-start.9 = (f32[8,512]{1,0:T(8,128)S(1)}, f32[8,512]{1,0:T(8,128)S(1)}, u32[]{:S(2)}, u32[]{:S(2)}) collective-permute-start(f32[8,512]{1,0:T(8,128)S(1)} %get-tuple-element.45), channel_id=1, source_target_pairs={{0,8},{8,0},{16,24},{24,16},{1,9},{9,1},{17,25},{25,17},{2,10},{10... | collective-permute-start | bytes 49160 | tf_op jit(solution)/shard_map/ppermute | solution.py:453
  35.5 2.4 %collective-permute-start.10 = (f32[8,512]{1,0:T(8,128)S(1)}, f32[8,512]{1,0:T(8,128)S(1)}, u32[]{:S(2)}, u32[]{:S(2)}) collective-permute-start(f32[8,512]{1,0:T(8,128)S(1)} %get-tuple-element.46), channel_id=1, source_target_pairs={{0,24},{8,16},{16,8},{24,0},{1,25},{9,17},{17,9},{25,1},{2,26},{10... | collective-permute-start | bytes 49160 | tf_op jit(solution)/shard_map/ppermute | solution.py:453
  37.9 2.0 %shard_map.82.refs_19_ = f32[96,216]{1,0:T(8,128)S(1)} custom-call(s32[1,344]{1,0:T(1,128)S(1)} %get-tuple-element.33.refs_0_, s32[32,8]{1,0:T(8,128)S(1)} %get-tuple-element.34.refs_1_, f32[32,4096]{1,0:T(8,128)S(1)} %copy-done, bf16[8,216,512]{2,1,0:T(8,128)(2,1)S(1)} %get-tuple-element.35.refs_3_, bf16[8,216,512]{2,1,0:T(8,128)(2,1)S(1)} %get-tuple-element.36.refs_4_, ...), custom_call_target="tpu_custom_call" | custom-call | flops 2000000000 | bytes 8000000 | tf_op jit(solution)/shard_map/pallas_call | solution.py:519
  39.9 0.2 collective-permute-done.10.turn_ref
  40.3 1.2 %collective-permute-start.16 = (f32[8,512]{1,0:T(8,128)S(1)}, f32[8,512]{1,0:T(8,128)S(1)}, u32[]{:S(2)}, u32[]{:S(2)}) collective-permute-start(f32[8,512]{1,0:T(8,128)S(1)} %get-tuple-element.53), channel_id=1, source_target_pairs={{0,2},{2,0},{4,6},{6,4},{1,3},{3,1},{5,7},{7,5},{8,10},{10,8},{12,... | collective-permute-start | bytes 49160 | tf_op jit(solution)/shard_map/ppermute | solution.py:453
  41.5 2.3 %collective-permute-start.17 = (f32[8,512]{1,0:T(8,128)S(1)}, f32[8,512]{1,0:T(8,128)S(1)}, u32[]{:S(2)}, u32[]{:S(2)}) collective-permute-start(f32[8,512]{1,0:T(8,128)S(1)} %get-tuple-element.54), channel_id=1, source_target_pairs={{0,6},{2,4},{4,2},{6,0},{1,7},{3,5},{5,3},{7,1},{8,14},{10,12},{12... | collective-permute-start | bytes 49160 | tf_op jit(solution)/shard_map/ppermute | solution.py:453
  43.7 2.7 %shard_map.84 = f32[32,1080]{1,0:T(8,128)} custom-call(s32[1,344]{1,0:T(1,128)S(1)} %get-tuple-element.33.refs_0_, s32[32,8]{1,0:T(8,128)S(1)} %get-tuple-element.34.refs_1_, f32[32,4096]{1,0:T(8,128)S(1)} %copy-done, bf16[8,216,512]{2,1,0:T(8,128)(2,1)S(1)} %get-tuple-element.35.refs_3_, bf16[8,216,512]{2,1,0:T(8,128)(2,1)S(1)} %get-tuple-element.36.refs_4_, ...), custom_call_target="tpu_custom_call" | custom-call | flops 2000000000 | bytes 8000000 | tf_op jit(solution)/shard_map/pallas_call | solution.py:519
  46.5 0.5 %collective-permute-done.17.turn_ref = f32[8,512]{1,0:T(8,128)S(1)} collective-permute-done((f32[8,512]{1,0:T(8,128)S(1)}, f32[8,512]{1,0:T(8,128)S(1)}, u32[]{:S(2)}, u32[]{:S(2)}) %collective-permute-start.17) | collective-permute-done | bytes 16416 | tf_op jit(solution)/shard_map/ppermute | solution.py:453
  47.2 1.2 %collective-permute-done.18.before_ref.after_ref = f32[32,512]{1,0:T(8,128)S(1)} collective-permute-done((f32[32,512]{1,0:T(8,128)S(1)}, f32[32,512]{1,0:T(8,128)S(1)}, u32[]{:S(2)}, u32[]{:S(2)}) %collective-permute-start.18) | collective-permute-done | bytes 65568 | tf_op jit(solution)/shard_map/ppermute | solution.py:537
  48.5 0.8 %shard_map.86 = f32[32,648]{1,0:T(8,128)} custom-call(f32[32,1024]{1,0:T(8,128)S(1)} %get-tuple-element.62.parts_ref, f32[32,512]{1,0:T(8,128)S(1)} %collective-permute-done.18.before_ref.after_ref, f32[32,512]{1,0:T(8,128)S(1)} %collective-permute-done.18.before_ref.after_ref), custom_call_target="tpu_custom_call" | custom-call | tf_op jit(solution)/shard_map/pallas_call | solution.py:541
  (22 shorter events, 0.6 us)
Async XLA Ops:
  0.6 15.3 %collective-permute-start = (f32[32,1080]{1,0:T(8,128)}, f32[32,1080]{1,0:T(8,128)S(1)}, u32[]{:S(2)}, u32[]{:S(2)}) collective-permute-start(f32[32,1080]{1,0:T(8,128)} %refs_0_.1), channel_id=1, source_target_pairs={{0,2},{2,0},{4,6},{6,4},{1,3},{3,1},{5,7},{7,5},{8,10},{10,8},{12,... | collective-permute-start | bytes 414728 | tf_op jit(solution)/shard_map/ppermute | solution.py:464
  5.1 10.9 %collective-permute-start.2 = (f32[32,512]{1,0:T(8,128)S(1)}, f32[32,512]{1,0:T(8,128)S(1)}, u32[]{:S(2)}, u32[]{:S(2)}) collective-permute-start(f32[32,512]{1,0:T(8,128)S(1)} %get-tuple-element.37.refs_3_.refs_7_.refs_5_), channel_id=1, source_target_pairs={{0,6},{2,4},{4,2},{6,0},{1,7},{3,5},{5,3},{7,1},{8,14},{10,12},{12... | collective-permute-start | bytes 196616 | tf_op jit(solution)/shard_map/ppermute | solution.py:483
  7.6 8.3 %collective-permute-start.1 = (f32[32,512]{1,0:T(8,128)S(1)}, f32[32,512]{1,0:T(8,128)S(1)}, u32[]{:S(2)}, u32[]{:S(2)}) collective-permute-start(f32[32,512]{1,0:T(8,128)S(1)} %get-tuple-element.37.refs_3_.refs_7_.refs_5_), channel_id=1, source_target_pairs={{0,4},{2,6},{4,0},{6,2},{1,5},{3,7},{5,1},{7,3},{8,12},{10,14},{12... | collective-permute-start | bytes 196616 | tf_op jit(solution)/shard_map/ppermute | solution.py:483
  7.8 3.6 %collective-permute-start.3 = (f32[8,128]{1,0:T(8,128)S(1)}, f32[8,128]{1,0:T(8,128)S(1)}, u32[]{:S(2)}, u32[]{:S(2)}) collective-permute-start(f32[8,128]{1,0:T(8,128)S(1)} %get-tuple-element.38), channel_id=1, source_target_pairs={{0,8},{8,0},{16,24},{24,16},{1,9},{9,1},{17,25},{25,17},{2,10},{10... | collective-permute-start | bytes 12296 | tf_op jit(solution)/shard_map/ppermute | solution.py:490
  9.3 4.6 %collective-permute-start.4 = (f32[8,128]{1,0:T(8,128)S(1)}, f32[8,128]{1,0:T(8,128)S(1)}, u32[]{:S(2)}, u32[]{:S(2)}) collective-permute-start(f32[8,128]{1,0:T(8,128)S(1)} %get-tuple-element.39), channel_id=1, source_target_pairs={{0,16},{8,24},{16,0},{24,8},{1,17},{9,25},{17,1},{25,9},{2,18},{10... | collective-permute-start | bytes 12296 | tf_op jit(solution)/shard_map/ppermute | solution.py:490
  11.4 4.5 %collective-permute-start.5 = (f32[8,128]{1,0:T(8,128)S(1)}, f32[8,128]{1,0:T(8,128)S(1)}, u32[]{:S(2)}, u32[]{:S(2)}) collective-permute-start(f32[8,128]{1,0:T(8,128)S(1)} %get-tuple-element.40), channel_id=1, source_target_pairs={{0,24},{8,16},{16,8},{24,0},{1,25},{9,17},{17,9},{25,1},{2,26},{10... | collective-permute-start | bytes 12296 | tf_op jit(solution)/shard_map/ppermute | solution.py:490
  16.4 13.1 %collective-permute-start.6 = (f32[72,512]{1,0:T(8,128)S(1)}, f32[72,512]{1,0:T(8,128)S(1)}, u32[]{:S(2)}, u32[]{:S(2)}) collective-permute-start(f32[72,512]{1,0:T(8,128)S(1)} %get-tuple-element.41), channel_id=1, source_target_pairs={{0,8},{8,0},{16,24},{24,16},{1,9},{9,1},{17,25},{25,17},{2,10},{10... | collective-permute-start | bytes 442376 | tf_op jit(solution)/shard_map/ppermute | solution.py:500
  18.0 6.3 %collective-permute-start.12 = (f32[32,568]{1,0:T(8,128)S(1)}, f32[32,568]{1,0:T(8,128)S(1)}, u32[]{:S(2)}, u32[]{:S(2)}) collective-permute-start(f32[32,568]{1,0:T(8,128)S(1)} %get-tuple-element.47.refs_3_.refs_12_), channel_id=1, source_target_pairs={{0,6},{2,4},{4,2},{6,0},{1,7},{3,5},{5,3},{7,1},{8,14},{10,12},{12... | collective-permute-start | bytes 218120 | tf_op jit(solution)/shard_map/ppermute | solution.py:483
  20.8 6.1 %collective-permute-start.11 = (f32[32,568]{1,0:T(8,128)S(1)}, f32[32,568]{1,0:T(8,128)S(1)}, u32[]{:S(2)}, u32[]{:S(2)}) collective-permute-start(f32[32,568]{1,0:T(8,128)S(1)} %get-tuple-element.47.refs_3_.refs_12_), channel_id=1, source_target_pairs={{0,4},{2,6},{4,0},{6,2},{1,5},{3,7},{5,1},{7,3},{8,12},{10,14},{12... | collective-permute-start | bytes 218120 | tf_op jit(solution)/shard_map/ppermute | solution.py:483
  21.1 10.9 %collective-permute-start.7 = (f32[72,512]{1,0:T(8,128)S(1)}, f32[72,512]{1,0:T(8,128)S(1)}, u32[]{:S(2)}, u32[]{:S(2)}) collective-permute-start(f32[72,512]{1,0:T(8,128)S(1)} %get-tuple-element.42), channel_id=1, source_target_pairs={{0,16},{8,24},{16,0},{24,8},{1,17},{9,25},{17,1},{25,9},{2,18},{10... | collective-permute-start | bytes 442376 | tf_op jit(solution)/shard_map/ppermute | solution.py:500
  22.7 9.4 %collective-permute-start.8 = (f32[72,512]{1,0:T(8,128)S(1)}, f32[72,512]{1,0:T(8,128)S(1)}, u32[]{:S(2)}, u32[]{:S(2)}) collective-permute-start(f32[72,512]{1,0:T(8,128)S(1)} %get-tuple-element.43), channel_id=1, source_target_pairs={{0,24},{8,16},{16,8},{24,0},{1,25},{9,17},{17,9},{25,1},{2,26},{10... | collective-permute-start | bytes 442376 | tf_op jit(solution)/shard_map/ppermute | solution.py:500
  27.4 10.5 %collective-permute-start.13 = (f32[72,568]{1,0:T(8,128)S(1)}, f32[72,568]{1,0:T(8,128)S(1)}, u32[]{:S(2)}, u32[]{:S(2)}) collective-permute-start(f32[72,568]{1,0:T(8,128)S(1)} %get-tuple-element.48), channel_id=1, source_target_pairs={{0,8},{8,0},{16,24},{24,16},{1,9},{9,1},{17,25},{25,17},{2,10},{10... | collective-permute-start | bytes 490760 | tf_op jit(solution)/shard_map/ppermute | solution.py:500
  28.0 9.9 %collective-permute-start.14 = (f32[72,568]{1,0:T(8,128)S(1)}, f32[72,568]{1,0:T(8,128)S(1)}, u32[]{:S(2)}, u32[]{:S(2)}) collective-permute-start(f32[72,568]{1,0:T(8,128)S(1)} %get-tuple-element.49), channel_id=1, source_target_pairs={{0,16},{8,24},{16,0},{24,8},{1,17},{9,25},{17,1},{25,9},{2,18},{10... | collective-permute-start | bytes 490760 | tf_op jit(solution)/shard_map/ppermute | solution.py:500
  29.5 2.5 %copy-start = (f32[32,4096]{1,0:T(8,128)S(1)}, f32[32,4096]{1,0:T(8,128)}, u32[]{:S(2)}) copy-start(f32[32,4096]{1,0:T(8,128)} %refs_2_.5) | copy-start | bytes 1572868
  29.6 2.5 %copy-start.1 = (bf16[216,768]{1,0:T(8,128)(2,1)S(1)}, bf16[216,768]{1,0:T(8,128)(2,1)}, u32[]{:S(2)}) copy-start(bf16[216,768]{1,0:T(8,128)(2,1)} %constant.5.clone.refs_6_) | copy-start | bytes 995332
  29.6 2.5 %copy-start.2 = (bf16[216,768]{1,0:T(8,128)(2,1)S(1)}, bf16[216,768]{1,0:T(8,128)(2,1)}, u32[]{:S(2)}) copy-start(bf16[216,768]{1,0:T(8,128)(2,1)} %constant.4.clone.refs_5_) | copy-start | bytes 995332
  29.6 8.4 %collective-permute-start.15 = (f32[72,568]{1,0:T(8,128)S(1)}, f32[72,568]{1,0:T(8,128)S(1)}, u32[]{:S(2)}, u32[]{:S(2)}) collective-permute-start(f32[72,568]{1,0:T(8,128)S(1)} %get-tuple-element.50), channel_id=1, source_target_pairs={{0,24},{8,16},{16,8},{24,0},{1,25},{9,17},{17,9},{25,1},{2,26},{10... | collective-permute-start | bytes 490760 | tf_op jit(solution)/shard_map/ppermute | solution.py:500
  34.9 5.0 %collective-permute-start.9 = (f32[8,512]{1,0:T(8,128)S(1)}, f32[8,512]{1,0:T(8,128)S(1)}, u32[]{:S(2)}, u32[]{:S(2)}) collective-permute-start(f32[8,512]{1,0:T(8,128)S(1)} %get-tuple-element.45), channel_id=1, source_target_pairs={{0,8},{8,0},{16,24},{24,16},{1,9},{9,1},{17,25},{25,17},{2,10},{10... | collective-permute-start | bytes 49160 | tf_op jit(solution)/shard_map/ppermute | solution.py:453
  35.5 4.6 %collective-permute-start.10 = (f32[8,512]{1,0:T(8,128)S(1)}, f32[8,512]{1,0:T(8,128)S(1)}, u32[]{:S(2)}, u32[]{:S(2)}) collective-permute-start(f32[8,512]{1,0:T(8,128)S(1)} %get-tuple-element.46), channel_id=1, source_target_pairs={{0,24},{8,16},{16,8},{24,0},{1,25},{9,17},{17,9},{25,1},{2,26},{10... | collective-permute-start | bytes 49160 | tf_op jit(solution)/shard_map/ppermute | solution.py:453
  40.3 6.2 %collective-permute-start.16 = (f32[8,512]{1,0:T(8,128)S(1)}, f32[8,512]{1,0:T(8,128)S(1)}, u32[]{:S(2)}, u32[]{:S(2)}) collective-permute-start(f32[8,512]{1,0:T(8,128)S(1)} %get-tuple-element.53), channel_id=1, source_target_pairs={{0,2},{2,0},{4,6},{6,4},{1,3},{3,1},{5,7},{7,5},{8,10},{10,8},{12,... | collective-permute-start | bytes 49160 | tf_op jit(solution)/shard_map/ppermute | solution.py:453
  41.5 5.5 %collective-permute-start.17 = (f32[8,512]{1,0:T(8,128)S(1)}, f32[8,512]{1,0:T(8,128)S(1)}, u32[]{:S(2)}, u32[]{:S(2)}) collective-permute-start(f32[8,512]{1,0:T(8,128)S(1)} %get-tuple-element.54), channel_id=1, source_target_pairs={{0,6},{2,4},{4,2},{6,0},{1,7},{3,5},{5,3},{7,1},{8,14},{10,12},{12... | collective-permute-start | bytes 49160 | tf_op jit(solution)/shard_map/ppermute | solution.py:453
  47.1 1.3 %collective-permute-start.18 = (f32[32,512]{1,0:T(8,128)S(1)}, f32[32,512]{1,0:T(8,128)S(1)}, u32[]{:S(2)}, u32[]{:S(2)}) collective-permute-start(f32[32,512]{1,0:T(8,128)S(1)} %get-tuple-element.63), channel_id=1, source_target_pairs={{0,1},{1,0},{2,3},{3,2},{4,5},{5,4},{6,7},{7,6},{8,9},{9,8},{10,11... | collective-permute-start | bytes 196616 | tf_op jit(solution)/shard_map/ppermute | solution.py:537

commit v4 on v1

--- a/solution.py
+++ b/solution.py
@@ -16,7 +16,9 @@
 QP = 512
 OVL = 8
 PAD = 256
-CUT = 512
+CUT = 440
+BLOCKS = CUT // 128
+EDGE = CUT % 128
 BF = jnp.bfloat16
 F32 = jnp.float32
 
@@ -131,12 +133,11 @@
 
 
 def front_kernel(owners, capacity, rows, owner, local, near_ref, far_ref, ids_ref, index_ref, *refs):
-    *mask_refs, owner_ref, local_ref, sems = refs
+    *mask_refs, owner_ref, local_ref, rows_ref, sems = refs
     pairs = (
         (owner, owner_ref),
         (local, local_ref),
-        (rows.at[:, :CUT], near_ref),
-        (rows.at[:, CUT:], far_ref),
+        (rows, rows_ref),
     )
     copies = [
         pltpu.make_async_copy(source, target, sems.at[n]) for n, (source, target) in enumerate(pairs)
@@ -166,7 +167,8 @@
         ids = jnp.where(ids > 0, ids + ((s + 1) * width - 1), -1)
         ids_ref[:, width + s * slots : width + (s + 1) * slots] = ids
     copies[2].wait()
-    copies[3].wait()
+    near_ref[...] = rows_ref[:, :CUT]
+    far_ref[...] = rows_ref[:, CUT:]
 
 
 def lanes_of(pieces, width, part):
@@ -189,7 +191,33 @@
     packed = (dot(order, high) + dot(order, middle)) + dot(order, low)
     slots = owners * capacity
     for s in range(count):
-        outs[s][...] = packed[s * slots : (s + 1) * slots]
+        piece = packed[s * slots : (s + 1) * slots]
+        if part:
+            outs[s][...] = piece
+            continue
+        for n in range(BLOCKS):
+            outs[s][n * slots : (n + 1) * slots] = piece[:, n * 128 : (n + 1) * 128]
+        first = upper_rows(slots)
+        edge = piece[:, BLOCKS * 128 :]
+        fill = jnp.zeros((2 * first - slots, EDGE), F32)
+        lower = jnp.concatenate([edge[first:], fill], 0) if 2 * first > slots else edge[first:]
+        blank = jnp.zeros((first, 128 - 2 * EDGE), F32)
+        outs[s][BLOCKS * slots :] = jnp.concatenate([edge[:first], lower, blank], 1)
+
+
+def upper_rows(slots):
+    return -(-slots // 16) * 8
+
+
+def edge_lanes(ref, slots):
+    first = upper_rows(slots)
+    edge = ref[BLOCKS * slots :]
+    return jnp.concatenate([edge[:, :EDGE], edge[: slots - first, EDGE : 2 * EDGE]], 0)
+
+
+def dense_rows(ref, slots):
+    blocks = [ref[n * slots : (n + 1) * slots] for n in range(BLOCKS)]
+    return jnp.concatenate([*blocks, edge_lanes(ref, slots)], 1)
 
 
 def pick(hot, rows, outs):
@@ -290,14 +318,14 @@
     return jnp.where(me > 0, before, 0.0), jnp.where(me < count - 1, after, 0.0)
 
 
-def lead_kernel(owners, count, ids_ref, index_ref, jac_ref, high_ref, low_ref, fhigh_ref, flow_ref, *refs):
+def lead_kernel(owners, count, slots, ids_ref, index_ref, jac_ref, high_ref, low_ref, fhigh_ref, flow_ref, *refs):
     column = refs[:owners]
     packed = refs[owners : owners + count]
     refs = refs[owners + count :]
     fields_ref, lumped_ref, parts_ref, send_ref, back_ref, *picked = refs
     elems = jac_ref.shape[0]
     hot = jnp.concatenate(hits(index_ref, ids_ref[...], range(OVL)), 0).astype(BF)
-    rows = lanes_of((*column, *packed), NB * FIELDS, 0)
+    rows = lanes_of(column, NB * FIELDS, 0) + [dense_rows(ref, slots) for ref in packed]
     pick(hot, jnp.concatenate(rows, 0), picked)
     total = project(0, picked, jac_ref, high_ref, low_ref, True)
     lumped = total[2 * elems :]
@@ -315,20 +343,22 @@
     send_faces(even, parts[:width], parts[-width:], 36, send_ref, back_ref)
 
 
-def tail_kernel(count, ids_ref, index_ref, jac_ref, high_ref, low_ref, lumped_ref, lead_ref, *refs):
+def tail_kernel(count, slots, ids_ref, index_ref, jac_ref, high_ref, low_ref, lumped_ref, lead_ref, *refs):
     near, far = refs[:count], refs[count : 2 * count]
     out_ref, *picked = refs[2 * count :]
     elems = jac_ref.shape[0]
-    start = CUT - 128
     hot = jnp.concatenate(hits(index_ref, ids_ref[...], range(OVL)), 0).astype(BF)
     rows = []
     for a, b in zip(near, far):
         if a.shape[1] == NB * FIELDS:
-            rows.append(a[:, start:])
+            rows.append(a[:, 2 * NB :])
+        elif a.shape[1] == CUT:
+            rows.append(jnp.concatenate([a[:, 2 * NB :], b[...]], 1))
         else:
-            rows.append(jnp.concatenate([a[:, start:], b[...]], 1))
+            edge = edge_lanes(a, slots)[:, 2 * NB - BLOCKS * 128 :]
+            rows.append(jnp.concatenate([edge, b[...]], 1))
     pick(hot, jnp.concatenate(rows, 0), picked)
-    total = project(2 * NB - start, picked, jac_ref, high_ref, low_ref, False)
+    total = project(0, picked, jac_ref, high_ref, low_ref, False)
     lumped = lumped_ref[...]
     out_ref[:, : 2 * NB] = lead_ref[...]
     for f in range(3):
@@ -464,7 +494,8 @@
         )
         + (shape((8, n_y * elems)),) * (n_x - 1),
         [HB] * 3,
-        [pltpu.VMEM(turned, jnp.int32)] * 2 + [pltpu.SemaphoreType.DMA((4,))],
+        [pltpu.VMEM(turned, jnp.int32)] * 2
+        + [pltpu.VMEM((elems, width), F32), pltpu.SemaphoreType.DMA((3,))],
     )(*[
         pltpu.with_memory_space_constraint(operand, pltpu.HBM)
         for operand in (src_fields, owner_peer[:, :, 0].T, src_local.T)
@@ -480,10 +511,11 @@
     asked = [lax.ppermute(mask, "gx", partner(n_x, step + 1)) for step, mask in enumerate(masks)]
     gathered = []
     for part in range(2):
-        span = (CUT, width - CUT)[part]
+        dense = (BLOCKS * slots + upper_rows(slots), 128)
+        piece_shape = (dense, (slots, width - CUT))[part]
         packed = call(
             lambda *refs: pack_kernel(n_y, capacity, n_x - 1, width, part, *refs),
-            (shape((slots, span)),) * (n_x - 1),
+            (shape(piece_shape),) * (n_x - 1),
             [VM] * (n_x - 1 + n_y),
         )(*asked, *columns[part])
         arrived = [
@@ -495,7 +527,7 @@
     face = shape((EY * EZ, 2 * PAD))
     whole = shape((elems, 4 * PAD))
     lead, lumped, parts, piece, back = call(
-        lambda *refs: lead_kernel(n_y, n_x - 1, *refs),
+        lambda *refs: lead_kernel(n_y, n_x - 1, slots, *refs),
         (shape((elems, 2 * NB)), shape((elems, NB)), whole, face, face),
         [VM] * (7 + len(near)),
         [pltpu.VMEM((OVL * elems, CUT), F32)] * 2,
@@ -504,9 +536,9 @@
     face = shape((EX * EZ, 2 * PAD))
     parts, piece, back = call(x_kernel, (whole, face, face), [VM] * 3)(parts, got, turn)
     got, turn = swap_faces(piece, back, "gy", n_y)
-    scratch = pltpu.VMEM((OVL * elems, width - CUT + 128), F32)
+    scratch = pltpu.VMEM((OVL * elems, width - 2 * NB), F32)
     fields = call(
-        lambda *refs: tail_kernel(len(near), *refs),
+        lambda *refs: tail_kernel(len(near), slots, *refs),
         shape((elems, width)),
         [VM] * (7 + 2 * len(near)),
         [scratch] * 2,

time: 50 us -> 49.6 us (level)
  starting transfers between devices: 28.2 us -> 27.7 us
    ppermute x4, starting transfers between devices: 6.51 us -> 5.98 us  [swap_faces(): return (lax.ppermute(piece, axis, near), lax.ppermute(back, axis, across))]
where the time goes in v4:
time: 49.6 us; the launch traced here: 49.4 us
  starting transfers between devices  27.7 us (56%)
  Pallas kernels  11 us (22%)
  waiting for transfers between devices  9.89 us (20%)
  between operations  0.75 us (2%)
    ppermute x6, starting transfers between devices, per_device(): lax.ppermute(piece, 'gx', partner(n_x, step + 1))  7.16 us
    ppermute x4, starting transfers between devices, swap_faces(): return (lax.ppermute(piece, axis, near), lax.ppermute(back, axis, across))  5.98 us
    ppermute x4, starting transfers between devices, per_device(): lax.ppermute(piece, 'gy', partner(n_y, step))  5.92 us
    ppermute x3, starting transfers between devices, per_device(): lax.ppermute(mask, 'gx', partner(n_x, step + 1))  5.46 us
    ppermute x4, waiting for transfers between devices, per_device(): lax.ppermute(piece, 'gy', partner(n_y, step))  3.77 us
    pallas_call x1, Pallas kernels, per_device(): call(lambda *refs: tail_kernel(len(near), slots, *refs), shape((elems, wi...  3.62 us
    ppermute x1, starting transfers between devices, per_device(): nearest = lax.ppermute(src_fields, 'gy', partner(n_y, 1))  3.12 us
    pallas_call x1, Pallas kernels, per_device(): call(lambda *refs: lead_kernel(n_y, n_x - 1, slots, *refs), (shape((elems...  2.87 us
  transfers between devices with their start and end apart: 19, of which 7 were waited for; matrix products, arithmetic and copies ran while one was open for 0% of the time, Pallas kernels for 19%

profile of v4, /device:TPU:0, one launch (start us, length us, event | category | flops | bytes accessed | tf_op | source)
XLA Modules:
  0.0 49.4 jit_solution(4308964933054538903)
XLA Ops:
  0.6 3.1 %collective-permute-start = (f32[32,1080]{1,0:T(8,128)}, f32[32,1080]{1,0:T(8,128)S(1)}, u32[]{:S(2)}, u32[]{:S(2)}) collective-permute-start(f32[32,1080]{1,0:T(8,128)} %refs_0_.1), channel_id=1, source_target_pairs={{0,2},{2,0},{4,6},{6,4},{1,3},{3,1},{5,7},{7,5},{8,10},{10,8},{12,... | collective-permute-start | bytes 414728 | tf_op jit(solution)/shard_map/ppermute | solution.py:484
  3.7 1.4 %shard_map.77 = (f32[32,440]{1,0:T(8,128)S(1)}, f32[32,640]{1,0:T(8,128)S(1)}, s32[1,344]{1,0:T(1,128)S(1)}, s32[32,8]{1,0:T(8,128)S(1)}, f32[8,128]{1,0:T(8,128...) custom-call(f32[32,1080]{1,0:T(8,128)} %refs_0_.1, s32[8,32]{1,0:T(8,128)} %bitcast.4, s32[8,32]{1,0:T(8,128)} %bitcast.5), custom_call_target="tpu_custom_call" | custom-call | tf_op jit(solution)/shard_map/pallas_call | solution.py:487
  5.2 2.5 %collective-permute-start.2 = (f32[32,440]{1,0:T(8,128)S(1)}, f32[32,440]{1,0:T(8,128)S(1)}, u32[]{:S(2)}, u32[]{:S(2)}) collective-permute-start(f32[32,440]{1,0:T(8,128)S(1)} %get-tuple-element.34.refs_3_.refs_7_), channel_id=1, source_target_pairs={{0,6},{2,4},{4,2},{6,0},{1,7},{3,5},{5,3},{7,1},{8,14},{10,12},{12... | collective-permute-start | bytes 168968 | tf_op jit(solution)/shard_map/ppermute | solution.py:504
  7.7 0.2 collective-permute-start.1
  7.9 1.5 %collective-permute-start.3 = (f32[8,128]{1,0:T(8,128)S(1)}, f32[8,128]{1,0:T(8,128)S(1)}, u32[]{:S(2)}, u32[]{:S(2)}) collective-permute-start(f32[8,128]{1,0:T(8,128)S(1)} %get-tuple-element.35), channel_id=1, source_target_pairs={{0,8},{8,0},{16,24},{24,16},{1,9},{9,1},{17,25},{25,17},{2,10},{10... | collective-permute-start | bytes 12296 | tf_op jit(solution)/shard_map/ppermute | solution.py:511
  9.4 1.5 %collective-permute-start.4 = (f32[8,128]{1,0:T(8,128)S(1)}, f32[8,128]{1,0:T(8,128)S(1)}, u32[]{:S(2)}, u32[]{:S(2)}) collective-permute-start(f32[8,128]{1,0:T(8,128)S(1)} %get-tuple-element.36), channel_id=1, source_target_pairs={{0,16},{8,24},{16,0},{24,8},{1,17},{9,25},{17,1},{25,9},{2,18},{10... | collective-permute-start | bytes 12296 | tf_op jit(solution)/shard_map/ppermute | solution.py:511
  10.9 0.6 %collective-permute-done.3.refs_0_ = f32[8,128]{1,0:T(8,128)S(1)} collective-permute-done((f32[8,128]{1,0:T(8,128)S(1)}, f32[8,128]{1,0:T(8,128)S(1)}, u32[]{:S(2)}, u32[]{:S(2)}) %collective-permute-start.3) | collective-permute-done | bytes 4128 | tf_op jit(solution)/shard_map/ppermute | solution.py:511
  11.5 2.4 %collective-permute-start.5 = (f32[8,128]{1,0:T(8,128)S(1)}, f32[8,128]{1,0:T(8,128)S(1)}, u32[]{:S(2)}, u32[]{:S(2)}) collective-permute-start(f32[8,128]{1,0:T(8,128)S(1)} %get-tuple-element.37), channel_id=1, source_target_pairs={{0,24},{8,16},{16,8},{24,0},{1,25},{9,17},{17,9},{25,1},{2,26},{10... | collective-permute-start | bytes 12296 | tf_op jit(solution)/shard_map/ppermute | solution.py:511
  14.0 2.1 %collective-permute-done.5.refs_2_ = f32[8,128]{1,0:T(8,128)S(1)} collective-permute-done((f32[8,128]{1,0:T(8,128)S(1)}, f32[8,128]{1,0:T(8,128)S(1)}, u32[]{:S(2)}, u32[]{:S(2)}) %collective-permute-start.5) | collective-permute-done | bytes 4128 | tf_op jit(solution)/shard_map/ppermute | solution.py:511
  16.0 0.5 %shard_map.79 = (f32[256,128]{1,0:T(8,128)S(1)}, f32[256,128]{1,0:T(8,128)S(1)}, f32[256,128]{1,0:T(8,128)S(1)}) custom-call(f32[8,128]{1,0:T(8,128)S(1)} %collective-permute-done.3.refs_0_, f32[8,128]{1,0:T(8,128)S(1)} %collective-permute-done.4.refs_1_, f32[8,128]{1,0:T(8,128)S(1)} %collective-permute-done.5.refs_2_, ...), custom_call_target="tpu_custom_call" | custom-call | tf_op jit(solution)/shard_map/pallas_call | solution.py:516
  16.6 1.6 %collective-permute-start.6 = (f32[256,128]{1,0:T(8,128)S(1)}, f32[256,128]{1,0:T(8,128)S(1)}, u32[]{:S(2)}, u32[]{:S(2)}) collective-permute-start(f32[256,128]{1,0:T(8,128)S(1)} %get-tuple-element.38), channel_id=1, source_target_pairs={{0,8},{8,0},{16,24},{24,16},{1,9},{9,1},{17,25},{25,17},{2,10},{10... | collective-permute-start | bytes 393224 | tf_op jit(solution)/shard_map/ppermute | solution.py:522
  18.1 2.9 %collective-permute-start.14 = (f32[32,640]{1,0:T(8,128)S(1)}, f32[32,640]{1,0:T(8,128)S(1)}, u32[]{:S(2)}, u32[]{:S(2)}) collective-permute-start(f32[32,640]{1,0:T(8,128)S(1)} %get-tuple-element.48.refs_3_.refs_14_), channel_id=1, source_target_pairs={{0,6},{2,4},{4,2},{6,0},{1,7},{3,5},{5,3},{7,1},{8,14},{10,12},{12... | collective-permute-start | bytes 245768 | tf_op jit(solution)/shard_map/ppermute | solution.py:504
  21.0 0.3 collective-permute-start.13
  21.3 1.5 %collective-permute-start.7 = (f32[256,128]{1,0:T(8,128)S(1)}, f32[256,128]{1,0:T(8,128)S(1)}, u32[]{:S(2)}, u32[]{:S(2)}) collective-permute-start(f32[256,128]{1,0:T(8,128)S(1)} %get-tuple-element.39), channel_id=1, source_target_pairs={{0,16},{8,24},{16,0},{24,8},{1,17},{9,25},{17,1},{25,9},{2,18},{10... | collective-permute-start | bytes 393224 | tf_op jit(solution)/shard_map/ppermute | solution.py:522
  22.8 0.5 collective-permute-start.8
  23.3 1.2 %collective-permute-done.14.refs_6_.refs_17_ = f32[32,640]{1,0:T(8,128)S(1)} collective-permute-done((f32[32,640]{1,0:T(8,128)S(1)}, f32[32,640]{1,0:T(8,128)S(1)}, u32[]{:S(2)}, u32[]{:S(2)}) %collective-permute-start.14) | collective-permute-done | bytes 81952 | tf_op jit(solution)/shard_map/ppermute | solution.py:504
  24.4 2.6 %collective-permute-done.13.refs_5_.refs_16_ = f32[32,640]{1,0:T(8,128)S(1)} collective-permute-done((f32[32,640]{1,0:T(8,128)S(1)}, f32[32,640]{1,0:T(8,128)S(1)}, u32[]{:S(2)}, u32[]{:S(2)}) %collective-permute-start.13) | collective-permute-done | bytes 81952 | tf_op jit(solution)/shard_map/ppermute | solution.py:504
  27.0 0.5 %shard_map.82 = (f32[72,640]{1,0:T(8,128)S(1)}, f32[72,640]{1,0:T(8,128)S(1)}, f32[72,640]{1,0:T(8,128)S(1)}) custom-call(f32[8,128]{1,0:T(8,128)S(1)} %collective-permute-done.3.refs_0_, f32[8,128]{1,0:T(8,128)S(1)} %collective-permute-done.4.refs_1_, f32[8,128]{1,0:T(8,128)S(1)} %collective-permute-done.5.refs_2_, ...), custom_call_target="tpu_custom_call" | custom-call | tf_op jit(solution)/shard_map/pallas_call | solution.py:516
  27.6 0.6 %collective-permute-start.15 = (f32[72,640]{1,0:T(8,128)S(1)}, f32[72,640]{1,0:T(8,128)S(1)}, u32[]{:S(2)}, u32[]{:S(2)}) collective-permute-start(f32[72,640]{1,0:T(8,128)S(1)} %get-tuple-element.49), channel_id=1, source_target_pairs={{0,8},{8,0},{16,24},{24,16},{1,9},{9,1},{17,25},{25,17},{2,10},{10... | collective-permute-start | bytes 552968 | tf_op jit(solution)/shard_map/ppermute | solution.py:522
  28.2 1.5 %collective-permute-start.16 = (f32[72,640]{1,0:T(8,128)S(1)}, f32[72,640]{1,0:T(8,128)S(1)}, u32[]{:S(2)}, u32[]{:S(2)}) collective-permute-start(f32[72,640]{1,0:T(8,128)S(1)} %get-tuple-element.50), channel_id=1, source_target_pairs={{0,16},{8,24},{16,0},{24,8},{1,17},{9,25},{17,1},{25,9},{2,18},{10... | collective-permute-start | bytes 552968 | tf_op jit(solution)/shard_map/ppermute | solution.py:522
  29.7 1.5 %collective-permute-start.17 = (f32[72,640]{1,0:T(8,128)S(1)}, f32[72,640]{1,0:T(8,128)S(1)}, u32[]{:S(2)}, u32[]{:S(2)}) collective-permute-start(f32[72,640]{1,0:T(8,128)S(1)} %get-tuple-element.51), channel_id=1, source_target_pairs={{0,24},{8,16},{16,8},{24,0},{1,25},{9,17},{17,9},{25,1},{2,26},{10... | collective-permute-start | bytes 552968 | tf_op jit(solution)/shard_map/ppermute | solution.py:522
  31.2 1.0 %shard_map.78 = (bf16[8,216,512]{2,1,0:T(8,128)(2,1)S(1)}, bf16[8,216,512]{2,1,0:T(8,128)(2,1)S(1)}) custom-call(), custom_call_target="tpu_custom_call" | custom-call | flops 2000000000 | bytes 8000000 | tf_op jit(solution)/shard_map/pallas_call | solution.py:510
  32.2 2.9 %shard_map.80 = (f32[32,432]{1,0:T(8,128)S(1)}, f32[32,216]{1,0:T(8,128)S(1)}, f32[32,1024]{1,0:T(8,128)S(1)}, f32[8,512]{1,0:T(8,128)S(1)}, f32[8,512]{1,0:T(8,128)S(1)}) custom-call(s32[1,344]{1,0:T(1,128)S(1)} %get-tuple-element.30.refs_0_, s32[32,8]{1,0:T(8,128)S(1)} %get-tuple-element.31.refs_1_, f32[32,4096]{1,0:T(8,128)S(1)} %copy-done, ...), custom_call_target="tpu_custom_call" | custom-call | tf_op jit(solution)/shard_map/pallas_call | solution.py:529
  35.1 0.6 %collective-permute-start.9 = (f32[8,512]{1,0:T(8,128)S(1)}, f32[8,512]{1,0:T(8,128)S(1)}, u32[]{:S(2)}, u32[]{:S(2)}) collective-permute-start(f32[8,512]{1,0:T(8,128)S(1)} %get-tuple-element.42), channel_id=1, source_target_pairs={{0,8},{8,0},{16,24},{24,16},{1,9},{9,1},{17,25},{25,17},{2,10},{10... | collective-permute-start | bytes 49160 | tf_op jit(solution)/shard_map/ppermute | solution.py:473
  35.7 2.4 %collective-permute-start.10 = (f32[8,512]{1,0:T(8,128)S(1)}, f32[8,512]{1,0:T(8,128)S(1)}, u32[]{:S(2)}, u32[]{:S(2)}) collective-permute-start(f32[8,512]{1,0:T(8,128)S(1)} %get-tuple-element.43), channel_id=1, source_target_pairs={{0,24},{8,16},{16,8},{24,0},{1,25},{9,17},{17,9},{25,1},{2,26},{10... | collective-permute-start | bytes 49160 | tf_op jit(solution)/shard_map/ppermute | solution.py:473
  38.1 0.8 %collective-permute-done.9.got_ref = f32[8,512]{1,0:T(8,128)S(1)} collective-permute-done((f32[8,512]{1,0:T(8,128)S(1)}, f32[8,512]{1,0:T(8,128)S(1)}, u32[]{:S(2)}, u32[]{:S(2)}) %collective-permute-start.9) | collective-permute-done | bytes 16416 | tf_op jit(solution)/shard_map/ppermute | solution.py:473
  38.9 1.4 %collective-permute-done.10.turn_ref = f32[8,512]{1,0:T(8,128)S(1)} collective-permute-done((f32[8,512]{1,0:T(8,128)S(1)}, f32[8,512]{1,0:T(8,128)S(1)}, u32[]{:S(2)}, u32[]{:S(2)}) %collective-permute-start.10) | collective-permute-done | bytes 16416 | tf_op jit(solution)/shard_map/ppermute | solution.py:473
  40.5 0.3 collective-permute-start.11
  40.8 2.6 %collective-permute-start.12 = (f32[8,512]{1,0:T(8,128)S(1)}, f32[8,512]{1,0:T(8,128)S(1)}, u32[]{:S(2)}, u32[]{:S(2)}) collective-permute-start(f32[8,512]{1,0:T(8,128)S(1)} %get-tuple-element.45), channel_id=1, source_target_pairs={{0,6},{2,4},{4,2},{6,0},{1,7},{3,5},{5,3},{7,1},{8,14},{10,12},{12... | collective-permute-start | bytes 49160 | tf_op jit(solution)/shard_map/ppermute | solution.py:473
  43.4 3.6 %shard_map.83 = f32[32,1080]{1,0:T(8,128)} custom-call(s32[1,344]{1,0:T(1,128)S(1)} %get-tuple-element.30.refs_0_, s32[32,8]{1,0:T(8,128)S(1)} %get-tuple-element.31.refs_1_, f32[32,4096]{1,0:T(8,128)S(1)} %copy-done, bf16[8,216,512]{2,1,0:T(8,128)(2,1)S(1)} %get-tuple-element.32.refs_3_, bf16[8,216,512]{2,1,0:T(8,128)(2,1)S(1)} %get-tuple-element.33.refs_4_, ...), custom_call_target="tpu_custom_call" | custom-call | flops 2000000000 | bytes 8000000 | tf_op jit(solution)/shard_map/pallas_call | solution.py:540
  47.3 1.2 %collective-permute-done.18.before_ref.after_ref = f32[32,512]{1,0:T(8,128)S(1)} collective-permute-done((f32[32,512]{1,0:T(8,128)S(1)}, f32[32,512]{1,0:T(8,128)S(1)}, u32[]{:S(2)}, u32[]{:S(2)}) %collective-permute-start.18) | collective-permute-done | bytes 65568 | tf_op jit(solution)/shard_map/ppermute | solution.py:551
  48.5 0.8 %shard_map.85 = f32[32,648]{1,0:T(8,128)} custom-call(f32[32,1024]{1,0:T(8,128)S(1)} %get-tuple-element.56.parts_ref, f32[32,512]{1,0:T(8,128)S(1)} %collective-permute-done.18.before_ref.after_ref, f32[32,512]{1,0:T(8,128)S(1)} %collective-permute-done.18.before_ref.after_ref), custom_call_target="tpu_custom_call" | custom-call | tf_op jit(solution)/shard_map/pallas_call | solution.py:555
  (21 shorter events, 0.4 us)
Async XLA Ops:
  0.6 15.4 %collective-permute-start = (f32[32,1080]{1,0:T(8,128)}, f32[32,1080]{1,0:T(8,128)S(1)}, u32[]{:S(2)}, u32[]{:S(2)}) collective-permute-start(f32[32,1080]{1,0:T(8,128)} %refs_0_.1), channel_id=1, source_target_pairs={{0,2},{2,0},{4,6},{6,4},{1,3},{3,1},{5,7},{7,5},{8,10},{10,8},{12,... | collective-permute-start | bytes 414728 | tf_op jit(solution)/shard_map/ppermute | solution.py:484
  5.2 10.9 %collective-permute-start.2 = (f32[32,440]{1,0:T(8,128)S(1)}, f32[32,440]{1,0:T(8,128)S(1)}, u32[]{:S(2)}, u32[]{:S(2)}) collective-permute-start(f32[32,440]{1,0:T(8,128)S(1)} %get-tuple-element.34.refs_3_.refs_7_), channel_id=1, source_target_pairs={{0,6},{2,4},{4,2},{6,0},{1,7},{3,5},{5,3},{7,1},{8,14},{10,12},{12... | collective-permute-start | bytes 168968 | tf_op jit(solution)/shard_map/ppermute | solution.py:504
  7.7 8.3 %collective-permute-start.1 = (f32[32,440]{1,0:T(8,128)S(1)}, f32[32,440]{1,0:T(8,128)S(1)}, u32[]{:S(2)}, u32[]{:S(2)}) collective-permute-start(f32[32,440]{1,0:T(8,128)S(1)} %get-tuple-element.34.refs_3_.refs_7_), channel_id=1, source_target_pairs={{0,4},{2,6},{4,0},{6,2},{1,5},{3,7},{5,1},{7,3},{8,12},{10,14},{12... | collective-permute-start | bytes 168968 | tf_op jit(solution)/shard_map/ppermute | solution.py:504
  7.9 3.6 %collective-permute-start.3 = (f32[8,128]{1,0:T(8,128)S(1)}, f32[8,128]{1,0:T(8,128)S(1)}, u32[]{:S(2)}, u32[]{:S(2)}) collective-permute-start(f32[8,128]{1,0:T(8,128)S(1)} %get-tuple-element.35), channel_id=1, source_target_pairs={{0,8},{8,0},{16,24},{24,16},{1,9},{9,1},{17,25},{25,17},{2,10},{10... | collective-permute-start | bytes 12296 | tf_op jit(solution)/shard_map/ppermute | solution.py:511
  9.4 4.6 %collective-permute-start.4 = (f32[8,128]{1,0:T(8,128)S(1)}, f32[8,128]{1,0:T(8,128)S(1)}, u32[]{:S(2)}, u32[]{:S(2)}) collective-permute-start(f32[8,128]{1,0:T(8,128)S(1)} %get-tuple-element.36), channel_id=1, source_target_pairs={{0,16},{8,24},{16,0},{24,8},{1,17},{9,25},{17,1},{25,9},{2,18},{10... | collective-permute-start | bytes 12296 | tf_op jit(solution)/shard_map/ppermute | solution.py:511
  11.5 4.5 %collective-permute-start.5 = (f32[8,128]{1,0:T(8,128)S(1)}, f32[8,128]{1,0:T(8,128)S(1)}, u32[]{:S(2)}, u32[]{:S(2)}) collective-permute-start(f32[8,128]{1,0:T(8,128)S(1)} %get-tuple-element.37), channel_id=1, source_target_pairs={{0,24},{8,16},{16,8},{24,0},{1,25},{9,17},{17,9},{25,1},{2,26},{10... | collective-permute-start | bytes 12296 | tf_op jit(solution)/shard_map/ppermute | solution.py:511
  16.6 13.1 %collective-permute-start.6 = (f32[256,128]{1,0:T(8,128)S(1)}, f32[256,128]{1,0:T(8,128)S(1)}, u32[]{:S(2)}, u32[]{:S(2)}) collective-permute-start(f32[256,128]{1,0:T(8,128)S(1)} %get-tuple-element.38), channel_id=1, source_target_pairs={{0,8},{8,0},{16,24},{24,16},{1,9},{9,1},{17,25},{25,17},{2,10},{10... | collective-permute-start | bytes 393224 | tf_op jit(solution)/shard_map/ppermute | solution.py:522
  18.1 6.3 %collective-permute-start.14 = (f32[32,640]{1,0:T(8,128)S(1)}, f32[32,640]{1,0:T(8,128)S(1)}, u32[]{:S(2)}, u32[]{:S(2)}) collective-permute-start(f32[32,640]{1,0:T(8,128)S(1)} %get-tuple-element.48.refs_3_.refs_14_), channel_id=1, source_target_pairs={{0,6},{2,4},{4,2},{6,0},{1,7},{3,5},{5,3},{7,1},{8,14},{10,12},{12... | collective-permute-start | bytes 245768 | tf_op jit(solution)/shard_map/ppermute | solution.py:504
  21.0 6.1 %collective-permute-start.13 = (f32[32,640]{1,0:T(8,128)S(1)}, f32[32,640]{1,0:T(8,128)S(1)}, u32[]{:S(2)}, u32[]{:S(2)}) collective-permute-start(f32[32,640]{1,0:T(8,128)S(1)} %get-tuple-element.48.refs_3_.refs_14_), channel_id=1, source_target_pairs={{0,4},{2,6},{4,0},{6,2},{1,5},{3,7},{5,1},{7,3},{8,12},{10,14},{12... | collective-permute-start | bytes 245768 | tf_op jit(solution)/shard_map/ppermute | solution.py:504
  21.3 10.9 %collective-permute-start.7 = (f32[256,128]{1,0:T(8,128)S(1)}, f32[256,128]{1,0:T(8,128)S(1)}, u32[]{:S(2)}, u32[]{:S(2)}) collective-permute-start(f32[256,128]{1,0:T(8,128)S(1)} %get-tuple-element.39), channel_id=1, source_target_pairs={{0,16},{8,24},{16,0},{24,8},{1,17},{9,25},{17,1},{25,9},{2,18},{10... | collective-permute-start | bytes 393224 | tf_op jit(solution)/shard_map/ppermute | solution.py:522
  22.8 9.4 %collective-permute-start.8 = (f32[256,128]{1,0:T(8,128)S(1)}, f32[256,128]{1,0:T(8,128)S(1)}, u32[]{:S(2)}, u32[]{:S(2)}) collective-permute-start(f32[256,128]{1,0:T(8,128)S(1)} %get-tuple-element.40), channel_id=1, source_target_pairs={{0,24},{8,16},{16,8},{24,0},{1,25},{9,17},{17,9},{25,1},{2,26},{10... | collective-permute-start | bytes 393224 | tf_op jit(solution)/shard_map/ppermute | solution.py:522
  27.6 15.9 %collective-permute-start.15 = (f32[72,640]{1,0:T(8,128)S(1)}, f32[72,640]{1,0:T(8,128)S(1)}, u32[]{:S(2)}, u32[]{:S(2)}) collective-permute-start(f32[72,640]{1,0:T(8,128)S(1)} %get-tuple-element.49), channel_id=1, source_target_pairs={{0,8},{8,0},{16,24},{24,16},{1,9},{9,1},{17,25},{25,17},{2,10},{10... | collective-permute-start | bytes 552968 | tf_op jit(solution)/shard_map/ppermute | solution.py:522
  28.2 15.3 %collective-permute-start.16 = (f32[72,640]{1,0:T(8,128)S(1)}, f32[72,640]{1,0:T(8,128)S(1)}, u32[]{:S(2)}, u32[]{:S(2)}) collective-permute-start(f32[72,640]{1,0:T(8,128)S(1)} %get-tuple-element.50), channel_id=1, source_target_pairs={{0,16},{8,24},{16,0},{24,8},{1,17},{9,25},{17,1},{25,9},{2,18},{10... | collective-permute-start | bytes 552968 | tf_op jit(solution)/shard_map/ppermute | solution.py:522
  29.7 2.5 %copy-start = (f32[32,4096]{1,0:T(8,128)S(1)}, f32[32,4096]{1,0:T(8,128)}, u32[]{:S(2)}) copy-start(f32[32,4096]{1,0:T(8,128)} %refs_2_.3) | copy-start | bytes 1572868
  29.7 2.5 %copy-start.1 = (bf16[216,768]{1,0:T(8,128)(2,1)S(1)}, bf16[216,768]{1,0:T(8,128)(2,1)}, u32[]{:S(2)}) copy-start(bf16[216,768]{1,0:T(8,128)(2,1)} %constant.5.clone.refs_6_) | copy-start | bytes 995332
  29.7 2.5 %copy-start.2 = (bf16[216,768]{1,0:T(8,128)(2,1)S(1)}, bf16[216,768]{1,0:T(8,128)(2,1)}, u32[]{:S(2)}) copy-start(bf16[216,768]{1,0:T(8,128)(2,1)} %constant.4.clone.refs_5_) | copy-start | bytes 995332
  29.7 13.7 %collective-permute-start.17 = (f32[72,640]{1,0:T(8,128)S(1)}, f32[72,640]{1,0:T(8,128)S(1)}, u32[]{:S(2)}, u32[]{:S(2)}) collective-permute-start(f32[72,640]{1,0:T(8,128)S(1)} %get-tuple-element.51), channel_id=1, source_target_pairs={{0,24},{8,16},{16,8},{24,0},{1,25},{9,17},{17,9},{25,1},{2,26},{10... | collective-permute-start | bytes 552968 | tf_op jit(solution)/shard_map/ppermute | solution.py:522
  35.1 3.8 %collective-permute-start.9 = (f32[8,512]{1,0:T(8,128)S(1)}, f32[8,512]{1,0:T(8,128)S(1)}, u32[]{:S(2)}, u32[]{:S(2)}) collective-permute-start(f32[8,512]{1,0:T(8,128)S(1)} %get-tuple-element.42), channel_id=1, source_target_pairs={{0,8},{8,0},{16,24},{24,16},{1,9},{9,1},{17,25},{25,17},{2,10},{10... | collective-permute-start | bytes 49160 | tf_op jit(solution)/shard_map/ppermute | solution.py:473
  35.7 4.6 %collective-permute-start.10 = (f32[8,512]{1,0:T(8,128)S(1)}, f32[8,512]{1,0:T(8,128)S(1)}, u32[]{:S(2)}, u32[]{:S(2)}) collective-permute-start(f32[8,512]{1,0:T(8,128)S(1)} %get-tuple-element.43), channel_id=1, source_target_pairs={{0,24},{8,16},{16,8},{24,0},{1,25},{9,17},{17,9},{25,1},{2,26},{10... | collective-permute-start | bytes 49160 | tf_op jit(solution)/shard_map/ppermute | solution.py:473
  40.5 6.6 %collective-permute-start.11 = (f32[8,512]{1,0:T(8,128)S(1)}, f32[8,512]{1,0:T(8,128)S(1)}, u32[]{:S(2)}, u32[]{:S(2)}) collective-permute-start(f32[8,512]{1,0:T(8,128)S(1)} %get-tuple-element.44), channel_id=1, source_target_pairs={{0,2},{2,0},{4,6},{6,4},{1,3},{3,1},{5,7},{7,5},{8,10},{10,8},{12,... | collective-permute-start | bytes 49160 | tf_op jit(solution)/shard_map/ppermute | solution.py:473
  40.8 6.3 %collective-permute-start.12 = (f32[8,512]{1,0:T(8,128)S(1)}, f32[8,512]{1,0:T(8,128)S(1)}, u32[]{:S(2)}, u32[]{:S(2)}) collective-permute-start(f32[8,512]{1,0:T(8,128)S(1)} %get-tuple-element.45), channel_id=1, source_target_pairs={{0,6},{2,4},{4,2},{6,0},{1,7},{3,5},{5,3},{7,1},{8,14},{10,12},{12... | collective-permute-start | bytes 49160 | tf_op jit(solution)/shard_map/ppermute | solution.py:473
  47.2 1.3 %collective-permute-start.18 = (f32[32,512]{1,0:T(8,128)S(1)}, f32[32,512]{1,0:T(8,128)S(1)}, u32[]{:S(2)}, u32[]{:S(2)}) collective-permute-start(f32[32,512]{1,0:T(8,128)S(1)} %get-tuple-element.57), channel_id=1, source_target_pairs={{0,1},{1,0},{2,3},{3,2},{4,5},{5,4},{6,7},{7,6},{8,9},{9,8},{10,11... | collective-permute-start | bytes 196616 | tf_op jit(solution)/shard_map/ppermute | solution.py:551

commit v5 on v1

--- a/solution.py
+++ b/solution.py
@@ -315,10 +315,9 @@
     send_faces(even, parts[:width], parts[-width:], 36, send_ref, back_ref)
 
 
-def tail_kernel(count, ids_ref, index_ref, jac_ref, high_ref, low_ref, lumped_ref, lead_ref, *refs):
+def tail_kernel(count, ids_ref, index_ref, jac_ref, high_ref, low_ref, *refs):
     near, far = refs[:count], refs[count : 2 * count]
     out_ref, *picked = refs[2 * count :]
-    elems = jac_ref.shape[0]
     start = CUT - 128
     hot = jnp.concatenate(hits(index_ref, ids_ref[...], range(OVL)), 0).astype(BF)
     rows = []
@@ -328,11 +327,16 @@
         else:
             rows.append(jnp.concatenate([a[:, start:], b[...]], 1))
     pick(hot, jnp.concatenate(rows, 0), picked)
-    total = project(2 * NB - start, picked, jac_ref, high_ref, low_ref, False)
+    out_ref[...] = project(2 * NB - start, picked, jac_ref, high_ref, low_ref, False)
+
+
+def finish_kernel(total_ref, lumped_ref, lead_ref, out_ref):
+    elems = lumped_ref.shape[0]
     lumped = lumped_ref[...]
     out_ref[:, : 2 * NB] = lead_ref[...]
-    for f in range(3):
-        out_ref[:, (f + 2) * NB : (f + 3) * NB] = total[f * elems : (f + 1) * elems] / lumped
+    for f in range(FIELDS - 2):
+        part = total_ref[f * elems : (f + 1) * elems]
+        out_ref[:, (f + 2) * NB : (f + 3) * NB] = part / lumped
 
 
 def face_add(parts, before, after, shift, stride):
@@ -487,8 +491,8 @@
             [VM] * (n_x - 1 + n_y),
         )(*asked, *columns[part])
         arrived = [
-            lax.ppermute(piece, "gx", partner(n_x, step + 1))
-            for step, piece in enumerate(packed)
+            lax.ppermute(piece, "gx", partner(n_x, step))
+            for step, piece in enumerate(packed, 1)
         ]
         gathered.append(columns[part] + arrived)
     near, far = gathered
@@ -505,14 +509,14 @@
     parts, piece, back = call(x_kernel, (whole, face, face), [VM] * 3)(parts, got, turn)
     got, turn = swap_faces(piece, back, "gy", n_y)
     scratch = pltpu.VMEM((OVL * elems, width - CUT + 128), F32)
-    fields = call(
+    rest = call(
         lambda *refs: tail_kernel(len(near), *refs),
-        shape((elems, width)),
-        [VM] * (7 + 2 * len(near)),
+        shape(((FIELDS - 2) * elems, NB)),
+        [VM] * (5 + 2 * len(near)),
         [scratch] * 2,
         heavy,
-    )(ids, index, jac, high, low, lumped, lead, *near, *far)
-    got, turn, fields = lax.optimization_barrier((got, turn, fields))
+    )(ids, index, jac, high, low, *near, *far)
+    got, turn, rest = lax.optimization_barrier((got, turn, rest))
     ends = (shape((elems, 2 * PAD)),) * (1 if n_z == 2 else 2)
     parts, *ends = call(y_kernel, (whole, *ends), [VM] * 3)(parts, got, turn)
     if n_z == 2:
@@ -520,6 +524,8 @@
     else:
         before = lax.ppermute(ends[0], "gz", [(i, i + 1) for i in range(n_z - 1)])
         after = lax.ppermute(ends[1], "gz", [(i + 1, i) for i in range(n_z - 1)])
+    fields = call(finish_kernel, shape((elems, width)), [VM] * 3, cost=heavy)(rest, lumped, lead)
+    before, after, fields = lax.optimization_barrier((before, after, fields))
     accel = call(z_kernel, shape((elems, 3 * NB)), [VM] * 3)(parts, before, after)
     return fields, accel
 

time: 50 us -> 49.5 us (0.990)
  waiting for transfers between devices: 9.89 us -> 9.35 us
    ppermute x1, waiting for transfers between devices: 1.24 us -> 0.48 us  [per_device(): before = after = lax.ppermute(ends[0], 'gz', [(0, 1), (1, 0)])]
    pallas_call x1 -> x2, Pallas kernels: 3.72 us -> 3.75 us  [the longest x1 2.99 us: per_device(): call(lambda *refs: tail_kernel(len(near), *refs), shape(((FIELDS - 2) * e...]
  transfers between devices with their start and end apart: 19 -> 19, of which waited for: 7 -> 8; matrix products, arithmetic and copies ran while one was open for 0% -> 0% of each run, Pallas kernels for 19% -> 19%
where the time goes in v5:
time: 49.5 us; the launch traced here: 49.4 us
  starting transfers between devices  28.3 us (57%)
  Pallas kernels  11 us (22%)
  waiting for transfers between devices  9.35 us (19%)
  between operations  0.77 us (2%)
    ppermute x6, starting transfers between devices, per_device(): lax.ppermute(piece, 'gx', partner(n_x, step))  7.18 us
    ppermute x4, starting transfers between devices, swap_faces(): return (lax.ppermute(piece, axis, near), lax.ppermute(back, axis, across))  6.52 us
    ppermute x4, starting transfers between devices, per_device(): lax.ppermute(piece, 'gy', partner(n_y, step))  5.9 us
    ppermute x3, starting transfers between devices, per_device(): lax.ppermute(mask, 'gx', partner(n_x, step + 1))  5.46 us
    ppermute x4, waiting for transfers between devices, per_device(): lax.ppermute(piece, 'gy', partner(n_y, step))  3.77 us
    ppermute x1, starting transfers between devices, per_device(): nearest = lax.ppermute(src_fields, 'gy', partner(n_y, 1))  3.12 us
    pallas_call x1, Pallas kernels, per_device(): call(lambda *refs: tail_kernel(len(near), *refs), shape(((FIELDS - 2) * e...  2.99 us
    pallas_call x1, Pallas kernels, per_device(): call(lambda *refs: lead_kernel(n_y, n_x - 1, *refs), (shape((elems, 2 * N...  2.83 us
  transfers between devices with their start and end apart: 19, of which 8 were waited for; matrix products, arithmetic and copies ran while one was open for 0% of the time, Pallas kernels for 19%

profile of v5, /device:TPU:0, one launch (start us, length us, event | category | flops | bytes accessed | tf_op | source)
XLA Modules:
  0.0 49.4 jit_solution(11122226740790298730)
XLA Ops:
  0.6 3.1 %collective-permute-start = (f32[32,1080]{1,0:T(8,128)}, f32[32,1080]{1,0:T(8,128)S(1)}, u32[]{:S(2)}, u32[]{:S(2)}) collective-permute-start(f32[32,1080]{1,0:T(8,128)} %refs_0_.1), channel_id=1, source_target_pairs={{0,2},{2,0},{4,6},{6,4},{1,3},{3,1},{5,7},{7,5},{8,10},{10,8},{12,... | collective-permute-start | bytes 414728 | tf_op jit(solution)/shard_map/ppermute | solution.py:458
  3.7 1.3 %shard_map.77 = (f32[32,512]{1,0:T(8,128)S(1)}, f32[32,568]{1,0:T(8,128)S(1)}, s32[1,344]{1,0:T(1,128)S(1)}, s32[32,8]{1,0:T(8,128)S(1)}, f32[8,128]{1,0:T(8,128...) custom-call(f32[32,1080]{1,0:T(8,128)} %refs_0_.1, s32[8,32]{1,0:T(8,128)} %bitcast.4, s32[8,32]{1,0:T(8,128)} %bitcast.5), custom_call_target="tpu_custom_call" | custom-call | tf_op jit(solution)/shard_map/pallas_call | solution.py:461
  5.1 2.5 %collective-permute-start.2 = (f32[32,512]{1,0:T(8,128)S(1)}, f32[32,512]{1,0:T(8,128)S(1)}, u32[]{:S(2)}, u32[]{:S(2)}) collective-permute-start(f32[32,512]{1,0:T(8,128)S(1)} %get-tuple-element.37.refs_3_.refs_7_.refs_5_), channel_id=1, source_target_pairs={{0,6},{2,4},{4,2},{6,0},{1,7},{3,5},{5,3},{7,1},{8,14},{10,12},{12... | collective-permute-start | bytes 196616 | tf_op jit(solution)/shard_map/ppermute | solution.py:477
  7.8 1.5 %collective-permute-start.3 = (f32[8,128]{1,0:T(8,128)S(1)}, f32[8,128]{1,0:T(8,128)S(1)}, u32[]{:S(2)}, u32[]{:S(2)}) collective-permute-start(f32[8,128]{1,0:T(8,128)S(1)} %get-tuple-element.38), channel_id=1, source_target_pairs={{0,8},{8,0},{16,24},{24,16},{1,9},{9,1},{17,25},{25,17},{2,10},{10... | collective-permute-start | bytes 12296 | tf_op jit(solution)/shard_map/ppermute | solution.py:484
  9.3 1.5 %collective-permute-start.4 = (f32[8,128]{1,0:T(8,128)S(1)}, f32[8,128]{1,0:T(8,128)S(1)}, u32[]{:S(2)}, u32[]{:S(2)}) collective-permute-start(f32[8,128]{1,0:T(8,128)S(1)} %get-tuple-element.39), channel_id=1, source_target_pairs={{0,16},{8,24},{16,0},{24,8},{1,17},{9,25},{17,1},{25,9},{2,18},{10... | collective-permute-start | bytes 12296 | tf_op jit(solution)/shard_map/ppermute | solution.py:484
  10.8 0.6 %collective-permute-done.3.refs_0_ = f32[8,128]{1,0:T(8,128)S(1)} collective-permute-done((f32[8,128]{1,0:T(8,128)S(1)}, f32[8,128]{1,0:T(8,128)S(1)}, u32[]{:S(2)}, u32[]{:S(2)}) %collective-permute-start.3) | collective-permute-done | bytes 4128 | tf_op jit(solution)/shard_map/ppermute | solution.py:484
  11.4 2.4 %collective-permute-start.5 = (f32[8,128]{1,0:T(8,128)S(1)}, f32[8,128]{1,0:T(8,128)S(1)}, u32[]{:S(2)}, u32[]{:S(2)}) collective-permute-start(f32[8,128]{1,0:T(8,128)S(1)} %get-tuple-element.40), channel_id=1, source_target_pairs={{0,24},{8,16},{16,8},{24,0},{1,25},{9,17},{17,9},{25,1},{2,26},{10... | collective-permute-start | bytes 12296 | tf_op jit(solution)/shard_map/ppermute | solution.py:484
  13.9 2.1 %collective-permute-done.5.refs_2_ = f32[8,128]{1,0:T(8,128)S(1)} collective-permute-done((f32[8,128]{1,0:T(8,128)S(1)}, f32[8,128]{1,0:T(8,128)S(1)}, u32[]{:S(2)}, u32[]{:S(2)}) %collective-permute-start.5) | collective-permute-done | bytes 4128 | tf_op jit(solution)/shard_map/ppermute | solution.py:484
  16.0 0.4 shard_map.79
  16.4 1.6 %collective-permute-start.6 = (f32[72,512]{1,0:T(8,128)S(1)}, f32[72,512]{1,0:T(8,128)S(1)}, u32[]{:S(2)}, u32[]{:S(2)}) collective-permute-start(f32[72,512]{1,0:T(8,128)S(1)} %get-tuple-element.41), channel_id=1, source_target_pairs={{0,8},{8,0},{16,24},{24,16},{1,9},{9,1},{17,25},{25,17},{2,10},{10... | collective-permute-start | bytes 442376 | tf_op jit(solution)/shard_map/ppermute | solution.py:494
  18.0 2.8 %collective-permute-start.14 = (f32[32,568]{1,0:T(8,128)S(1)}, f32[32,568]{1,0:T(8,128)S(1)}, u32[]{:S(2)}, u32[]{:S(2)}) collective-permute-start(f32[32,568]{1,0:T(8,128)S(1)} %get-tuple-element.50.refs_3_.refs_12_), channel_id=1, source_target_pairs={{0,6},{2,4},{4,2},{6,0},{1,7},{3,5},{5,3},{7,1},{8,14},{10,12},{12... | collective-permute-start | bytes 218120 | tf_op jit(solution)/shard_map/ppermute | solution.py:477
  20.8 0.3 collective-permute-start.13
  21.1 1.5 %collective-permute-start.7 = (f32[72,512]{1,0:T(8,128)S(1)}, f32[72,512]{1,0:T(8,128)S(1)}, u32[]{:S(2)}, u32[]{:S(2)}) collective-permute-start(f32[72,512]{1,0:T(8,128)S(1)} %get-tuple-element.42), channel_id=1, source_target_pairs={{0,16},{8,24},{16,0},{24,8},{1,17},{9,25},{17,1},{25,9},{2,18},{10... | collective-permute-start | bytes 442376 | tf_op jit(solution)/shard_map/ppermute | solution.py:494
  22.7 0.5 collective-permute-start.8
  23.1 1.2 %collective-permute-done.14.refs_6_.refs_15_ = f32[32,568]{1,0:T(8,128)S(1)} collective-permute-done((f32[32,568]{1,0:T(8,128)S(1)}, f32[32,568]{1,0:T(8,128)S(1)}, u32[]{:S(2)}, u32[]{:S(2)}) %collective-permute-start.14) | collective-permute-done | bytes 72736 | tf_op jit(solution)/shard_map/ppermute | solution.py:477
  24.3 2.6 %collective-permute-done.13.refs_5_.refs_14_ = f32[32,568]{1,0:T(8,128)S(1)} collective-permute-done((f32[32,568]{1,0:T(8,128)S(1)}, f32[32,568]{1,0:T(8,128)S(1)}, u32[]{:S(2)}, u32[]{:S(2)}) %collective-permute-start.13) | collective-permute-done | bytes 72736 | tf_op jit(solution)/shard_map/ppermute | solution.py:477
  26.9 0.5 %shard_map.82 = (f32[72,568]{1,0:T(8,128)S(1)}, f32[72,568]{1,0:T(8,128)S(1)}, f32[72,568]{1,0:T(8,128)S(1)}) custom-call(f32[8,128]{1,0:T(8,128)S(1)} %collective-permute-done.3.refs_0_, f32[8,128]{1,0:T(8,128)S(1)} %collective-permute-done.4.refs_1_, f32[8,128]{1,0:T(8,128)S(1)} %collective-permute-done.5.refs_2_, ...), custom_call_target="tpu_custom_call" | custom-call | tf_op jit(solution)/shard_map/pallas_call | solution.py:488
  27.4 0.6 %collective-permute-start.15 = (f32[72,568]{1,0:T(8,128)S(1)}, f32[72,568]{1,0:T(8,128)S(1)}, u32[]{:S(2)}, u32[]{:S(2)}) collective-permute-start(f32[72,568]{1,0:T(8,128)S(1)} %get-tuple-element.51), channel_id=1, source_target_pairs={{0,8},{8,0},{16,24},{24,16},{1,9},{9,1},{17,25},{25,17},{2,10},{10... | collective-permute-start | bytes 490760 | tf_op jit(solution)/shard_map/ppermute | solution.py:494
  28.0 1.5 %collective-permute-start.16 = (f32[72,568]{1,0:T(8,128)S(1)}, f32[72,568]{1,0:T(8,128)S(1)}, u32[]{:S(2)}, u32[]{:S(2)}) collective-permute-start(f32[72,568]{1,0:T(8,128)S(1)} %get-tuple-element.52), channel_id=1, source_target_pairs={{0,16},{8,24},{16,0},{24,8},{1,17},{9,25},{17,1},{25,9},{2,18},{10... | collective-permute-start | bytes 490760 | tf_op jit(solution)/shard_map/ppermute | solution.py:494
  29.6 1.5 %collective-permute-start.17 = (f32[72,568]{1,0:T(8,128)S(1)}, f32[72,568]{1,0:T(8,128)S(1)}, u32[]{:S(2)}, u32[]{:S(2)}) collective-permute-start(f32[72,568]{1,0:T(8,128)S(1)} %get-tuple-element.53), channel_id=1, source_target_pairs={{0,24},{8,16},{16,8},{24,0},{1,25},{9,17},{17,9},{25,1},{2,26},{10... | collective-permute-start | bytes 490760 | tf_op jit(solution)/shard_map/ppermute | solution.py:494
  31.1 1.0 %shard_map.78 = (bf16[8,216,512]{2,1,0:T(8,128)(2,1)S(1)}, bf16[8,216,512]{2,1,0:T(8,128)(2,1)S(1)}) custom-call(), custom_call_target="tpu_custom_call" | custom-call | flops 2000000000 | bytes 8000000 | tf_op jit(solution)/shard_map/pallas_call | solution.py:483
  32.1 2.8 %shard_map.80 = (f32[32,432]{1,0:T(8,128)S(1)}, f32[32,216]{1,0:T(8,128)S(1)}, f32[32,1024]{1,0:T(8,128)S(1)}, f32[8,512]{1,0:T(8,128)S(1)}, f32[8,512]{1,0:T(8,128)S(1)}) custom-call(s32[1,344]{1,0:T(1,128)S(1)} %get-tuple-element.33.refs_0_, s32[32,8]{1,0:T(8,128)S(1)} %get-tuple-element.34.refs_1_, f32[32,4096]{1,0:T(8,128)S(1)} %copy-done, ...), custom_call_target="tpu_custom_call" | custom-call | tf_op jit(solution)/shard_map/pallas_call | solution.py:501
  34.9 0.6 %collective-permute-start.9 = (f32[8,512]{1,0:T(8,128)S(1)}, f32[8,512]{1,0:T(8,128)S(1)}, u32[]{:S(2)}, u32[]{:S(2)}) collective-permute-start(f32[8,512]{1,0:T(8,128)S(1)} %get-tuple-element.45), channel_id=1, source_target_pairs={{0,8},{8,0},{16,24},{24,16},{1,9},{9,1},{17,25},{25,17},{2,10},{10... | collective-permute-start | bytes 49160 | tf_op jit(solution)/shard_map/ppermute | solution.py:447
  35.5 2.4 %collective-permute-start.10 = (f32[8,512]{1,0:T(8,128)S(1)}, f32[8,512]{1,0:T(8,128)S(1)}, u32[]{:S(2)}, u32[]{:S(2)}) collective-permute-start(f32[8,512]{1,0:T(8,128)S(1)} %get-tuple-element.46), channel_id=1, source_target_pairs={{0,24},{8,16},{16,8},{24,0},{1,25},{9,17},{17,9},{25,1},{2,26},{10... | collective-permute-start | bytes 49160 | tf_op jit(solution)/shard_map/ppermute | solution.py:447
  38.0 0.8 %collective-permute-done.9.got_ref = f32[8,512]{1,0:T(8,128)S(1)} collective-permute-done((f32[8,512]{1,0:T(8,128)S(1)}, f32[8,512]{1,0:T(8,128)S(1)}, u32[]{:S(2)}, u32[]{:S(2)}) %collective-permute-start.9) | collective-permute-done | bytes 16416 | tf_op jit(solution)/shard_map/ppermute | solution.py:447
  38.7 1.4 %collective-permute-done.10.turn_ref = f32[8,512]{1,0:T(8,128)S(1)} collective-permute-done((f32[8,512]{1,0:T(8,128)S(1)}, f32[8,512]{1,0:T(8,128)S(1)}, u32[]{:S(2)}, u32[]{:S(2)}) %collective-permute-start.10) | collective-permute-done | bytes 16416 | tf_op jit(solution)/shard_map/ppermute | solution.py:447
  40.3 1.2 %collective-permute-start.11 = (f32[8,512]{1,0:T(8,128)S(1)}, f32[8,512]{1,0:T(8,128)S(1)}, u32[]{:S(2)}, u32[]{:S(2)}) collective-permute-start(f32[8,512]{1,0:T(8,128)S(1)} %get-tuple-element.48), channel_id=1, source_target_pairs={{0,2},{2,0},{4,6},{6,4},{1,3},{3,1},{5,7},{7,5},{8,10},{10,8},{12,... | collective-permute-start | bytes 49160 | tf_op jit(solution)/shard_map/ppermute | solution.py:447
  41.5 2.3 %collective-permute-start.12 = (f32[8,512]{1,0:T(8,128)S(1)}, f32[8,512]{1,0:T(8,128)S(1)}, u32[]{:S(2)}, u32[]{:S(2)}) collective-permute-start(f32[8,512]{1,0:T(8,128)S(1)} %get-tuple-element.49), channel_id=1, source_target_pairs={{0,6},{2,4},{4,2},{6,0},{1,7},{3,5},{5,3},{7,1},{8,14},{10,12},{12... | collective-permute-start | bytes 49160 | tf_op jit(solution)/shard_map/ppermute | solution.py:447
  43.8 3.0 %shard_map.83.total_ref = f32[96,216]{1,0:T(8,128)S(1)} custom-call(s32[1,344]{1,0:T(1,128)S(1)} %get-tuple-element.33.refs_0_, s32[32,8]{1,0:T(8,128)S(1)} %get-tuple-element.34.refs_1_, f32[32,4096]{1,0:T(8,128)S(1)} %copy-done, bf16[8,216,512]{2,1,0:T(8,128)(2,1)S(1)} %get-tuple-element.35.refs_3_, bf16[8,216,512]{2,1,0:T(8,128)(2,1)S(1)} %get-tuple-element.36.refs_4_, ...), custom_call_target="tpu_custom_call" | custom-call | flops 2000000000 | bytes 8000000 | tf_op jit(solution)/shard_map/pallas_call | solution.py:512
  47.3 0.8 %shard_map.85 = f32[32,1080]{1,0:T(8,128)} custom-call(f32[96,216]{1,0:T(8,128)S(1)} %shard_map.83.total_ref, f32[32,216]{1,0:T(8,128)S(1)} %get-tuple-element.58.lumped_ref, f32[32,432]{1,0:T(8,128)S(1)} %get-tuple-element.59.lead_ref), custom_call_target="tpu_custom_call" | custom-call | flops 2000000000 | bytes 8000000 | tf_op jit(solution)/shard_map/pallas_call | solution.py:527
  48.0 0.5 collective-permute-done.18.before_ref.after_ref
  48.5 0.8 %shard_map.86 = f32[32,648]{1,0:T(8,128)} custom-call(f32[32,1024]{1,0:T(8,128)S(1)} %get-tuple-element.61.parts_ref, f32[32,512]{1,0:T(8,128)S(1)} %collective-permute-done.18.before_ref.after_ref, f32[32,512]{1,0:T(8,128)S(1)} %collective-permute-done.18.before_ref.after_ref), custom_call_target="tpu_custom_call" | custom-call | tf_op jit(solution)/shard_map/pallas_call | solution.py:529
  (22 shorter events, 0.8 us)
Async XLA Ops:
  0.6 15.3 %collective-permute-start = (f32[32,1080]{1,0:T(8,128)}, f32[32,1080]{1,0:T(8,128)S(1)}, u32[]{:S(2)}, u32[]{:S(2)}) collective-permute-start(f32[32,1080]{1,0:T(8,128)} %refs_0_.1), channel_id=1, source_target_pairs={{0,2},{2,0},{4,6},{6,4},{1,3},{3,1},{5,7},{7,5},{8,10},{10,8},{12,... | collective-permute-start | bytes 414728 | tf_op jit(solution)/shard_map/ppermute | solution.py:458
  5.1 10.9 %collective-permute-start.2 = (f32[32,512]{1,0:T(8,128)S(1)}, f32[32,512]{1,0:T(8,128)S(1)}, u32[]{:S(2)}, u32[]{:S(2)}) collective-permute-start(f32[32,512]{1,0:T(8,128)S(1)} %get-tuple-element.37.refs_3_.refs_7_.refs_5_), channel_id=1, source_target_pairs={{0,6},{2,4},{4,2},{6,0},{1,7},{3,5},{5,3},{7,1},{8,14},{10,12},{12... | collective-permute-start | bytes 196616 | tf_op jit(solution)/shard_map/ppermute | solution.py:477
  7.6 8.3 %collective-permute-start.1 = (f32[32,512]{1,0:T(8,128)S(1)}, f32[32,512]{1,0:T(8,128)S(1)}, u32[]{:S(2)}, u32[]{:S(2)}) collective-permute-start(f32[32,512]{1,0:T(8,128)S(1)} %get-tuple-element.37.refs_3_.refs_7_.refs_5_), channel_id=1, source_target_pairs={{0,4},{2,6},{4,0},{6,2},{1,5},{3,7},{5,1},{7,3},{8,12},{10,14},{12... | collective-permute-start | bytes 196616 | tf_op jit(solution)/shard_map/ppermute | solution.py:477
  7.8 3.6 %collective-permute-start.3 = (f32[8,128]{1,0:T(8,128)S(1)}, f32[8,128]{1,0:T(8,128)S(1)}, u32[]{:S(2)}, u32[]{:S(2)}) collective-permute-start(f32[8,128]{1,0:T(8,128)S(1)} %get-tuple-element.38), channel_id=1, source_target_pairs={{0,8},{8,0},{16,24},{24,16},{1,9},{9,1},{17,25},{25,17},{2,10},{10... | collective-permute-start | bytes 12296 | tf_op jit(solution)/shard_map/ppermute | solution.py:484
  9.3 4.6 %collective-permute-start.4 = (f32[8,128]{1,0:T(8,128)S(1)}, f32[8,128]{1,0:T(8,128)S(1)}, u32[]{:S(2)}, u32[]{:S(2)}) collective-permute-start(f32[8,128]{1,0:T(8,128)S(1)} %get-tuple-element.39), channel_id=1, source_target_pairs={{0,16},{8,24},{16,0},{24,8},{1,17},{9,25},{17,1},{25,9},{2,18},{10... | collective-permute-start | bytes 12296 | tf_op jit(solution)/shard_map/ppermute | solution.py:484
  11.4 4.5 %collective-permute-start.5 = (f32[8,128]{1,0:T(8,128)S(1)}, f32[8,128]{1,0:T(8,128)S(1)}, u32[]{:S(2)}, u32[]{:S(2)}) collective-permute-start(f32[8,128]{1,0:T(8,128)S(1)} %get-tuple-element.40), channel_id=1, source_target_pairs={{0,24},{8,16},{16,8},{24,0},{1,25},{9,17},{17,9},{25,1},{2,26},{10... | collective-permute-start | bytes 12296 | tf_op jit(solution)/shard_map/ppermute | solution.py:484
  16.4 13.1 %collective-permute-start.6 = (f32[72,512]{1,0:T(8,128)S(1)}, f32[72,512]{1,0:T(8,128)S(1)}, u32[]{:S(2)}, u32[]{:S(2)}) collective-permute-start(f32[72,512]{1,0:T(8,128)S(1)} %get-tuple-element.41), channel_id=1, source_target_pairs={{0,8},{8,0},{16,24},{24,16},{1,9},{9,1},{17,25},{25,17},{2,10},{10... | collective-permute-start | bytes 442376 | tf_op jit(solution)/shard_map/ppermute | solution.py:494
  18.0 6.3 %collective-permute-start.14 = (f32[32,568]{1,0:T(8,128)S(1)}, f32[32,568]{1,0:T(8,128)S(1)}, u32[]{:S(2)}, u32[]{:S(2)}) collective-permute-start(f32[32,568]{1,0:T(8,128)S(1)} %get-tuple-element.50.refs_3_.refs_12_), channel_id=1, source_target_pairs={{0,6},{2,4},{4,2},{6,0},{1,7},{3,5},{5,3},{7,1},{8,14},{10,12},{12... | collective-permute-start | bytes 218120 | tf_op jit(solution)/shard_map/ppermute | solution.py:477
  20.8 6.1 %collective-permute-start.13 = (f32[32,568]{1,0:T(8,128)S(1)}, f32[32,568]{1,0:T(8,128)S(1)}, u32[]{:S(2)}, u32[]{:S(2)}) collective-permute-start(f32[32,568]{1,0:T(8,128)S(1)} %get-tuple-element.50.refs_3_.refs_12_), channel_id=1, source_target_pairs={{0,4},{2,6},{4,0},{6,2},{1,5},{3,7},{5,1},{7,3},{8,12},{10,14},{12... | collective-permute-start | bytes 218120 | tf_op jit(solution)/shard_map/ppermute | solution.py:477
  21.1 10.9 %collective-permute-start.7 = (f32[72,512]{1,0:T(8,128)S(1)}, f32[72,512]{1,0:T(8,128)S(1)}, u32[]{:S(2)}, u32[]{:S(2)}) collective-permute-start(f32[72,512]{1,0:T(8,128)S(1)} %get-tuple-element.42), channel_id=1, source_target_pairs={{0,16},{8,24},{16,0},{24,8},{1,17},{9,25},{17,1},{25,9},{2,18},{10... | collective-permute-start | bytes 442376 | tf_op jit(solution)/shard_map/ppermute | solution.py:494
  22.7 9.4 %collective-permute-start.8 = (f32[72,512]{1,0:T(8,128)S(1)}, f32[72,512]{1,0:T(8,128)S(1)}, u32[]{:S(2)}, u32[]{:S(2)}) collective-permute-start(f32[72,512]{1,0:T(8,128)S(1)} %get-tuple-element.43), channel_id=1, source_target_pairs={{0,24},{8,16},{16,8},{24,0},{1,25},{9,17},{17,9},{25,1},{2,26},{10... | collective-permute-start | bytes 442376 | tf_op jit(solution)/shard_map/ppermute | solution.py:494
  27.4 16.4 %collective-permute-start.15 = (f32[72,568]{1,0:T(8,128)S(1)}, f32[72,568]{1,0:T(8,128)S(1)}, u32[]{:S(2)}, u32[]{:S(2)}) collective-permute-start(f32[72,568]{1,0:T(8,128)S(1)} %get-tuple-element.51), channel_id=1, source_target_pairs={{0,8},{8,0},{16,24},{24,16},{1,9},{9,1},{17,25},{25,17},{2,10},{10... | collective-permute-start | bytes 490760 | tf_op jit(solution)/shard_map/ppermute | solution.py:494
  28.0 15.8 %collective-permute-start.16 = (f32[72,568]{1,0:T(8,128)S(1)}, f32[72,568]{1,0:T(8,128)S(1)}, u32[]{:S(2)}, u32[]{:S(2)}) collective-permute-start(f32[72,568]{1,0:T(8,128)S(1)} %get-tuple-element.52), channel_id=1, source_target_pairs={{0,16},{8,24},{16,0},{24,8},{1,17},{9,25},{17,1},{25,9},{2,18},{10... | collective-permute-start | bytes 490760 | tf_op jit(solution)/shard_map/ppermute | solution.py:494
  29.5 2.5 %copy-start = (f32[32,4096]{1,0:T(8,128)S(1)}, f32[32,4096]{1,0:T(8,128)}, u32[]{:S(2)}) copy-start(f32[32,4096]{1,0:T(8,128)} %refs_2_.3) | copy-start | bytes 1572868
  29.6 2.5 %copy-start.1 = (bf16[216,768]{1,0:T(8,128)(2,1)S(1)}, bf16[216,768]{1,0:T(8,128)(2,1)}, u32[]{:S(2)}) copy-start(bf16[216,768]{1,0:T(8,128)(2,1)} %constant.5.clone.refs_6_) | copy-start | bytes 995332
  29.6 2.5 %copy-start.2 = (bf16[216,768]{1,0:T(8,128)(2,1)S(1)}, bf16[216,768]{1,0:T(8,128)(2,1)}, u32[]{:S(2)}) copy-start(bf16[216,768]{1,0:T(8,128)(2,1)} %constant.4.clone.refs_5_) | copy-start | bytes 995332
  29.6 14.2 %collective-permute-start.17 = (f32[72,568]{1,0:T(8,128)S(1)}, f32[72,568]{1,0:T(8,128)S(1)}, u32[]{:S(2)}, u32[]{:S(2)}) collective-permute-start(f32[72,568]{1,0:T(8,128)S(1)} %get-tuple-element.53), channel_id=1, source_target_pairs={{0,24},{8,16},{16,8},{24,0},{1,25},{9,17},{17,9},{25,1},{2,26},{10... | collective-permute-start | bytes 490760 | tf_op jit(solution)/shard_map/ppermute | solution.py:494
  34.9 3.8 %collective-permute-start.9 = (f32[8,512]{1,0:T(8,128)S(1)}, f32[8,512]{1,0:T(8,128)S(1)}, u32[]{:S(2)}, u32[]{:S(2)}) collective-permute-start(f32[8,512]{1,0:T(8,128)S(1)} %get-tuple-element.45), channel_id=1, source_target_pairs={{0,8},{8,0},{16,24},{24,16},{1,9},{9,1},{17,25},{25,17},{2,10},{10... | collective-permute-start | bytes 49160 | tf_op jit(solution)/shard_map/ppermute | solution.py:447
  35.5 4.6 %collective-permute-start.10 = (f32[8,512]{1,0:T(8,128)S(1)}, f32[8,512]{1,0:T(8,128)S(1)}, u32[]{:S(2)}, u32[]{:S(2)}) collective-permute-start(f32[8,512]{1,0:T(8,128)S(1)} %get-tuple-element.46), channel_id=1, source_target_pairs={{0,24},{8,16},{16,8},{24,0},{1,25},{9,17},{17,9},{25,1},{2,26},{10... | collective-permute-start | bytes 49160 | tf_op jit(solution)/shard_map/ppermute | solution.py:447
  40.3 6.5 %collective-permute-start.11 = (f32[8,512]{1,0:T(8,128)S(1)}, f32[8,512]{1,0:T(8,128)S(1)}, u32[]{:S(2)}, u32[]{:S(2)}) collective-permute-start(f32[8,512]{1,0:T(8,128)S(1)} %get-tuple-element.48), channel_id=1, source_target_pairs={{0,2},{2,0},{4,6},{6,4},{1,3},{3,1},{5,7},{7,5},{8,10},{10,8},{12,... | collective-permute-start | bytes 49160 | tf_op jit(solution)/shard_map/ppermute | solution.py:447
  41.5 5.5 %collective-permute-start.12 = (f32[8,512]{1,0:T(8,128)S(1)}, f32[8,512]{1,0:T(8,128)S(1)}, u32[]{:S(2)}, u32[]{:S(2)}) collective-permute-start(f32[8,512]{1,0:T(8,128)S(1)} %get-tuple-element.49), channel_id=1, source_target_pairs={{0,6},{2,4},{4,2},{6,0},{1,7},{3,5},{5,3},{7,1},{8,14},{10,12},{12... | collective-permute-start | bytes 49160 | tf_op jit(solution)/shard_map/ppermute | solution.py:447
  47.2 1.3 %collective-permute-start.18 = (f32[32,512]{1,0:T(8,128)S(1)}, f32[32,512]{1,0:T(8,128)S(1)}, u32[]{:S(2)}, u32[]{:S(2)}) collective-permute-start(f32[32,512]{1,0:T(8,128)S(1)} %get-tuple-element.56), channel_id=1, source_target_pairs={{0,1},{1,0},{2,3},{3,2},{4,5},{5,4},{6,7},{7,6},{8,9},{9,8},{10,11... | collective-permute-start | bytes 196616 | tf_op jit(solution)/shard_map/ppermute | solution.py:523
